TPU v7x, 32 devices: a whole 2x2x4 slice. The times are simulated.
32 devices in a mesh: group: 2 (over x), stream: 16 (over z, y, core).
Axes of the slice: x: 2, y: 2, z: 4, core: 2. Of those that a mesh axis runs over, the one named last changes fastest.
Arguments:
- snapshot: float32 [256, 4, 512, 64], P('stream', 'group'), parts along dimension 1, may hold values from -6 to 6
- mode_weight: float32 [32, 32, 64, 128], P('stream'), may hold values from -4 to 4
- local_weight: float32 [64, 64], replicated, may hold values from -0.75 to 0.75
- offset_bias: float32 [64], replicated, may hold values from -4 to 4
- upstream: float32 [256, 4, 512, 64], P('stream', 'group'), parts along dimension 1, may hold values from -6 to 6
Outputs:
- activated: float32 [256, 4, 512, 64], P('stream', 'group'), parts along dimension 1
- grad_snapshot: float32 [256, 4, 512, 64], P('stream', 'group'), parts along dimension 1
- grad_modes: float32 [32, 64, 64, 128], P('stream', 'group'), parts along dimension 1
There are 2 independent parts, one for each index of `group`. A program takes and returns all parts, laid end to end along the dimension named above; an argument that names none is the same for every part. Nothing has to cross between parts.
All inputs are finite; a program needn't handle non-finite values.
Results may differ from a plain program's by a relative error of at most 0.00008.
Values sent between devices are 32-bit elements; how exact they have to be, the bound alone decides.
No kernel may reach another device: no remote copies, remote signals or barrier semaphores. Data moves between devices by JAX's collectives and lax.ppermute only.
A program may use at most 64 MiB of HBM per device.

v0:
```python
import math

import jax
import jax.numpy as jnp
from jax import lax
from jax.sharding import PartitionSpec as P


def hi_einsum(form, left, right):
    return jnp.einsum(form, left, right, precision=lax.Precision.HIGHEST)


def swap(values, bit):
    count = lax.axis_size("stream")
    return lax.ppermute(values, "stream", [(i, i ^ bit) for i in range(count)])


def stage_bits():
    count = lax.axis_size("stream")
    bits = [1 << i for i in range(count.bit_length() - 1)]
    assert 1 << len(bits) == count
    return bits


def held_rows(owned):
    bits = stage_bits()
    pattern = [0]
    for bit in reversed(bits):
        pattern = pattern + [p | bit for p in pattern]
    blocks = jnp.asarray(pattern, jnp.int32) ^ lax.axis_index("stream")
    return (blocks[:, None] * owned + jnp.arange(owned, dtype=jnp.int32)[None, :]).reshape(-1)


def scatter_sum(values):
    for bit in stage_bits():
        half = values.shape[0] // 2
        values = values[:half] + swap(values[half:], bit)
    return values


def gather_all(values):
    for bit in reversed(stage_bits()):
        values = jnp.concatenate([values, swap(values, bit)], axis=0)
    return values


def mode_tables(rows, total_modes, length, offset, cells):
    wave = jnp.where(rows < total_modes // 2, rows, rows + length - total_modes)
    points = offset + jnp.arange(cells, dtype=jnp.int32)
    phase = wave[:, None] * points[None, :] % length
    angles = phase.astype(jnp.float32) * (2.0 * math.pi / length)
    return (jnp.cos(angles), jnp.sin(angles))


def span_tables(length, modes, scale):
    points = jnp.arange(length, dtype=jnp.int32)
    waves = jnp.arange(modes, dtype=jnp.int32)
    phase = points[:, None] * waves[None, :] % length
    angles = phase.astype(jnp.float32) * (2.0 * math.pi / length)
    forward = jnp.stack([jnp.cos(angles), -jnp.sin(angles)], axis=2)
    factor = jnp.where(waves == 0, 1.0, 2.0).astype(jnp.float32) / scale
    backward = jnp.stack([jnp.cos(angles).T, -jnp.sin(angles).T], axis=1) * factor[:, None, None]
    return (forward, backward)


def flip_parts(values):
    half = values.shape[-1] // 2
    return jnp.concatenate([values[..., half:], -values[..., :half]], axis=-1)


def flip_back(values):
    half = values.shape[-1] // 2
    return jnp.concatenate([-values[..., half:], values[..., :half]], axis=-1)


def mix_modes(coeffs, weights):
    half = weights.shape[2]
    first = hi_einsum("jbkc,jkcd->jbkd", coeffs[..., :half], weights)
    second = hi_einsum("jbkc,jkcd->jbkd", coeffs[..., half:], weights)
    real_part = first[..., :half] - second[..., half:]
    imag_part = first[..., half:] + second[..., :half]
    return jnp.concatenate([real_part, imag_part], axis=-1)


def mix_adjoint(coeffs, dmixed, weights):
    half = weights.shape[2]
    c_re, c_im = (coeffs[..., :half], coeffs[..., half:])
    d_re, d_im = (dmixed[..., :half], dmixed[..., half:])
    w_re, w_im = (weights[..., :half], weights[..., half:])
    grad_re = hi_einsum("jbkc,jbkd->jkcd", c_re, d_re) + hi_einsum("jbkc,jbkd->jkcd", c_im, d_im)
    grad_im = hi_einsum("jbkc,jbkd->jkcd", c_re, d_im) - hi_einsum("jbkc,jbkd->jkcd", c_im, d_re)
    dmod_re = hi_einsum("jbkd,jkcd->jbkc", d_re, w_re) + hi_einsum("jbkd,jkcd->jbkc", d_im, w_im)
    dmod_im = hi_einsum("jbkd,jkcd->jbkc", d_im, w_re) - hi_einsum("jbkd,jkcd->jbkc", d_re, w_im)
    return (
        jnp.concatenate([grad_re, grad_im], axis=-1),
        jnp.concatenate([dmod_re, dmod_im], axis=-1),
    )


def gelu_slope(values):
    return 0.5 * (1.0 + jax.scipy.special.erf(values / math.sqrt(2.0))) + values * jnp.exp(
        -0.5 * values * values
    ) / math.sqrt(2.0 * math.pi)


def per_device(snapshot, mode_weight, local_weight, offset_bias, upstream):
    cells, planes, span_len, channels = snapshot.shape
    devices = lax.axis_size("stream")
    owned = mode_weight.shape[0]
    span_modes = mode_weight.shape[1]
    total_modes = owned * devices
    stream_len = cells * devices
    offset = lax.axis_index("stream") * cells
    span_fwd, span_inv = span_tables(span_len, span_modes, float(stream_len * span_len))
    spanwise = hi_einsum("xbzc,zkp->xbkpc", snapshot, span_fwd).reshape(
        cells, planes, span_modes, 2 * channels
    )
    spanwise_flip = flip_parts(spanwise)
    rows = held_rows(owned)
    cos_rows, sin_rows = mode_tables(rows, total_modes, stream_len, offset, cells)
    modes = scatter_sum(
        hi_einsum("jx,xbkq->jbkq", cos_rows, spanwise)
        + hi_einsum("jx,xbkq->jbkq", sin_rows, spanwise_flip)
    )
    mixed = mix_modes(modes, mode_weight)
    shards = gather_all(mixed)
    inverse = hi_einsum("jx,jbkq->xbkq", cos_rows, shards) + hi_einsum(
        "jx,jbkq->xbkq", sin_rows, flip_back(shards)
    )
    spectral = hi_einsum(
        "xbkpo,kpz->xbzo", inverse.reshape(cells, planes, span_modes, 2, channels), span_inv
    )
    pre = spectral + hi_einsum("xbzc,cd->xbzd", snapshot, local_weight) + offset_bias
    activated = jax.nn.gelu(pre, approximate=False)
    dpre = upstream * gelu_slope(pre)
    dinverse = hi_einsum("xbzo,kpz->xbkpo", dpre, span_inv).reshape(
        cells, planes, span_modes, 2 * channels
    )
    dmixed = scatter_sum(
        hi_einsum("jx,xbkq->jbkq", cos_rows, dinverse)
        + flip_parts(hi_einsum("jx,xbkq->jbkq", sin_rows, dinverse))
    )
    grad_modes, dmodes = mix_adjoint(modes, dmixed, mode_weight)
    shards = gather_all(dmodes)
    dspanwise = hi_einsum("jx,jbkq->xbkq", cos_rows, shards) + flip_back(
        hi_einsum("jx,jbkq->xbkq", sin_rows, shards)
    )
    grad_snapshot = hi_einsum(
        "xbkpc,zkp->xbzc", dspanwise.reshape(cells, planes, span_modes, 2, channels), span_fwd
    )
    grad_snapshot = grad_snapshot + hi_einsum("xbzo,co->xbzc", dpre, local_weight)
    return (activated, grad_snapshot, grad_modes)


def solution(mesh):
    placed = (
        P("stream", "group", None, None),
        P("stream", None, None, None),
        P(),
        P(),
        P("stream", "group", None, None),
    )
    return jax.shard_map(
        per_device,
        mesh=mesh,
        in_specs=placed,
        out_specs=(
            P("stream", "group", None, None),
            P("stream", "group", None, None),
            P("stream", "group", None, None),
        ),
        check_vma=False,
    )
```

profile of v0, /device:TPU:0, one launch (start us, length us, event | category | flops | bytes accessed | tf_op | source)
XLA Modules:
  0.0 178.6 jit_solution(4561018642268461771)
XLA Ops:
  0.9 8.1 %fusion.27 = f32[16,2,32,2,64]{4,2,1,0,3:T(8,128)S(1)} fusion(f32[16,2,512,64]{2,3,1,0:T(8,128)} %param.6, f32[512,32,1]{0,1,2:T(8,128)S(1)} %get-tuple-element.23, f32[512,32,1]{0,1,2:T(8,128)S(1)} %get-tuple-element.24), kind=kOutput, calls=%fused_computation.42 | convolution fusion | flops 805339136 | bytes 4849664 | tf_op jit(solution)/shard_map/xbzc,zkp->xbkpc/dot_general | solution.py:10
  9.1 0.8 copy.69
  9.9 0.6 reshape.201
  10.9 1.2 fusion.107
  12.1 1.2 convolution_add_fusion.2
  13.3 0.5 collective-permute-start
  13.8 1.5 collective-permute-done
  15.4 3.0 %collective-permute-start.1 = (f32[8,2,32,128]{3,0,2,1:T(8,128)S(1)}, f32[8,2,32,128]{3,0,2,1:T(8,128)S(1)}, u32[]{:S(2)}, u32[]{:S(2)}) collective-permute-start(f32[8,2,32,128]{3,0,2,1:T(8,128)S(1)} %slice.143), channel_id=1, source_target_pairs={{0,2},{1,3},{2,0},{3,1},{4,6},{5,7},{6,4},{7,5},{8,10},{9,11},{10,... | collective-permute-start | bytes 786440 | tf_op jit(solution)/shard_map/ppermute | solution.py:15
  18.4 6.6 %collective-permute-done.1 = f32[8,2,32,128]{3,0,2,1:T(8,128)S(1)} collective-permute-done((f32[8,2,32,128]{3,0,2,1:T(8,128)S(1)}, f32[8,2,32,128]{3,0,2,1:T(8,128)S(1)}, u32[]{:S(2)}, u32[]{:S(2)}) %collective-permute-start.1) | collective-permute-done | bytes 262176 | tf_op jit(solution)/shard_map/ppermute | solution.py:15
  25.1 1.9 %collective-permute-start.2 = (f32[4,2,32,128]{3,0,2,1:T(4,128)S(1)}, f32[4,2,32,128]{3,0,2,1:T(4,128)S(1)}, u32[]{:S(2)}, u32[]{:S(2)}) collective-permute-start(f32[4,2,32,128]{3,0,2,1:T(4,128)S(1)} %slice.145), channel_id=1, source_target_pairs={{0,4},{1,5},{2,6},{3,7},{4,0},{5,1},{6,2},{7,3},{8,12},{9,13},{10,... | collective-permute-start | bytes 393224 | tf_op jit(solution)/shard_map/ppermute | solution.py:15
  26.9 3.2 %collective-permute-done.2 = f32[4,2,32,128]{3,0,2,1:T(4,128)S(1)} collective-permute-done((f32[4,2,32,128]{3,0,2,1:T(4,128)S(1)}, f32[4,2,32,128]{3,0,2,1:T(4,128)S(1)}, u32[]{:S(2)}, u32[]{:S(2)}) %collective-permute-start.2) | collective-permute-done | bytes 131104 | tf_op jit(solution)/shard_map/ppermute | solution.py:15
  30.3 2.8 %collective-permute-start.3 = (f32[2,2,32,128]{3,0,2,1:T(2,128)S(1)}, f32[2,2,32,128]{3,0,2,1:T(2,128)S(1)}, u32[]{:S(2)}, u32[]{:S(2)}) collective-permute-start(f32[2,2,32,128]{3,0,2,1:T(2,128)S(1)} %slice.147), channel_id=1, source_target_pairs={{0,8},{1,9},{2,10},{3,11},{4,12},{5,13},{6,14},{7,15},{8,0},{9,1},... | collective-permute-start | bytes 196616 | tf_op jit(solution)/shard_map/ppermute | solution.py:15
  33.1 2.4 %collective-permute-done.3 = f32[2,2,32,128]{3,0,2,1:T(2,128)S(1)} collective-permute-done((f32[2,2,32,128]{3,0,2,1:T(2,128)S(1)}, f32[2,2,32,128]{3,0,2,1:T(2,128)S(1)}, u32[]{:S(2)}, u32[]{:S(2)}) %collective-permute-start.3) | collective-permute-done | bytes 65568 | tf_op jit(solution)/shard_map/ppermute | solution.py:15
  35.7 1.8 %convolution_bitcast_fusion = f32[2,2,32,128]{3,1,2,0:T(2,128)S(1)} fusion(f32[2,32,64,128]{3,2,1,0:T(8,128)S(1)} %copy-done.1, f32[2,2,32,64]{3,0,2,1:T(2,128)S(1)} %get-tuple-element.22), kind=kOutput, calls=%fused_computation.48 | convolution fusion | flops 12582912 | bytes 2195456 | tf_op jit(solution)/shard_map/jbkc,jkcd->jbkd/dot_general | solution.py:10
  37.5 1.9 %convolution_bitcast_fusion.1 = f32[2,2,32,128]{3,1,2,0:T(2,128)S(1)} fusion(f32[2,32,64,128]{3,2,1,0:T(8,128)S(1)} %copy-done.1, f32[2,2,32,64]{3,0,2,1:T(2,128)S(1)} %get-tuple-element.21), kind=kOutput, calls=%fused_computation.49 | convolution fusion | flops 12582912 | bytes 2195456 | tf_op jit(solution)/shard_map/jbkc,jkcd->jbkd/dot_general | solution.py:10
  39.7 2.9 %collective-permute-start.4 = (f32[2,2,32,128]{3,1,2,0:T(2,128)S(1)}, f32[2,2,32,128]{3,1,2,0:T(2,128)S(1)}, u32[]{:S(2)}, u32[]{:S(2)}) collective-permute-start(f32[2,2,32,128]{3,1,2,0:T(2,128)S(1)} %get-tuple-element.6), channel_id=1, source_target_pairs={{0,8},{1,9},{2,10},{3,11},{4,12},{5,13},{6,14},{7,15},{8,0},{9,1},... | collective-permute-start | bytes 196616 | tf_op jit(solution)/shard_map/ppermute | solution.py:15
  42.6 2.5 %collective-permute-done.4 = f32[2,2,32,128]{3,1,2,0:T(2,128)S(1)} collective-permute-done((f32[2,2,32,128]{3,1,2,0:T(2,128)S(1)}, f32[2,2,32,128]{3,1,2,0:T(2,128)S(1)}, u32[]{:S(2)}, u32[]{:S(2)}) %collective-permute-start.4) | collective-permute-done | bytes 65568 | tf_op jit(solution)/shard_map/ppermute | solution.py:15
  45.2 2.1 %collective-permute-start.5 = (f32[4,2,32,128]{3,1,2,0:T(2,128)S(1)}, f32[4,2,32,128]{3,1,2,0:T(2,128)S(1)}, u32[]{:S(2)}, u32[]{:S(2)}) collective-permute-start(f32[4,2,32,128]{3,1,2,0:T(2,128)S(1)} %pad_maximum_fusion.7), channel_id=1, source_target_pairs={{0,4},{1,5},{2,6},{3,7},{4,0},{5,1},{6,2},{7,3},{8,12},{9,13},{10,... | collective-permute-start | bytes 393224 | tf_op jit(solution)/shard_map/ppermute | solution.py:15
  47.3 2.9 %collective-permute-done.5 = f32[4,2,32,128]{3,1,2,0:T(2,128)S(1)} collective-permute-done((f32[4,2,32,128]{3,1,2,0:T(2,128)S(1)}, f32[4,2,32,128]{3,1,2,0:T(2,128)S(1)}, u32[]{:S(2)}, u32[]{:S(2)}) %collective-permute-start.5) | collective-permute-done | bytes 131104 | tf_op jit(solution)/shard_map/ppermute | solution.py:15
  50.4 1.7 collective-permute-start.6
  52.2 4.7 %collective-permute-done.6 = f32[8,2,32,128]{3,1,2,0:T(2,128)S(1)} collective-permute-done((f32[8,2,32,128]{3,1,2,0:T(2,128)S(1)}, f32[8,2,32,128]{3,1,2,0:T(2,128)S(1)}, u32[]{:S(2)}, u32[]{:S(2)}) %collective-permute-start.6) | collective-permute-done | bytes 262176 | tf_op jit(solution)/shard_map/ppermute | solution.py:15
  56.9 0.3 pad_maximum_fusion.2
  57.3 0.9 sine_negate_fusion.1
  58.3 0.9 collective-permute-done.7
  59.3 1.2 slice_negate_fusion.1
  60.5 1.2 pad_maximum_fusion.1
  61.6 1.5 fusion.49
  63.1 2.1 %convolution_add_fusion.4 = f32[16,2,32,128]{3,0,2,1:T(8,128)} fusion(f32[16,2,32,128]{3,0,2,1:T(8,128)S(1)} %fusion.49, f32[32,2,32,128]{3,1,2,0:T(2,128)S(1)} %constant_dynamic-update-slice_fusion, s32[16]{0:T(128)S(1)} %iota_add_fusion.1, s32[32]{0:T(128)S(1)} %compare_select_fusion), kind=kOutput, calls=%fused_computation.47 | convolution fusion | flops 50469888 | bytes 2097344 | tf_op jit(solution)/shard_map/jx,jbkq->xbkq/dot_general | solution.py:10
  65.2 1.6 reshape.188
  66.8 4.8 %fusion.47 = f32[512,16,2,64,1]{0,3,4,2,1:T(8,128)S(1)} fusion(f32[16,2,32,2,64]{4,3,0,2,1:T(2,128)S(1)} %reshape.188, f32[32,1,512]{2,0,1:T(8,128)S(1)} %get-tuple-element.25, f32[32,1,512]{2,0,1:T(8,128)} %get-tuple-element.26, f32[32]{0:T(128)S(1)} %fusion.119), kind=kOutput, calls=%fused_computation.59 | convolution fusion | flops 805371904 | bytes 4849792 | tf_op jit(solution)/shard_map/xbkpo,kpz->xbzo/dot_general | solution.py:10
  71.7 18.1 %fusion.6 = (f32[16,2,512,64]{2,3,1,0:T(8,128)S(1)}, f32[16,2,512,64]{2,3,1,0:T(8,128)}) fusion(f32[16,2,512,64]{2,3,1,0:T(8,128)} %param.10, f32[64]{0:T(128)S(1)} %copy-done.6, f32[16,2,512,64]{2,3,1,0:T(8,128)S(1)} %copy-done.4, f32[64,64]{1,0:T(8,128)S(1)} %copy-done, f32[512,16,2,64,1]{0,3,4,2,1:T(8,128)S(1)} %fusion.47), kind=kOutput, calls=%fused_computation.8 | convolution fusion | flops 883949568 | bytes 20988160 | tf_op jit(solution)/shard_map/xbzc,cd->xbzd/dot_general | solution.py:10
  89.8 2.0 %copy-done.2 = f32[16,2,512,64]{2,3,1,0:T(8,128)} copy-done((f32[16,2,512,64]{2,3,1,0:T(8,128)}, f32[16,2,512,64]{2,3,1,0:T(8,128)S(1)}, u32[]{:S(2)}) %copy-start.2) | copy-done | bytes 4194328
  91.8 6.2 %fusion.30 = f32[16,2,32,2,64]{4,2,1,0,3:T(8,128)S(1)} fusion(f32[16,2,512,64]{2,3,1,0:T(8,128)S(1)} %get-tuple-element.7, f32[32,1,512]{2,0,1:T(8,128)S(1)} %get-tuple-element.25, f32[32,1,512]{2,0,1:T(8,128)S(1)} %copy-done.5, f32[32]{0:T(128)S(1)} %fusion.119), kind=kOutput, calls=%fused_computation.43 | convolution fusion | flops 805371904 | bytes 4849792 | tf_op jit(solution)/shard_map/xbzo,kpz->xbkpo/dot_general | solution.py:10
  98.0 1.8 copy.71
  99.8 1.8 %reshape.202 = f32[16,2,32,128]{3,0,2,1:T(8,128)S(1)} reshape(f32[16,2,32,2,64]{4,3,0,2,1:T(2,128)} %copy.71) | data formatting | bytes 1048576 | tf_op jit(solution)/shard_map/reshape | solution.py:136
  101.6 1.1 fusion.100
  102.8 0.4 fusion.157
  103.2 1.3 convolution_add_fusion.1
  104.7 1.8 collective-permute-done.8
  106.6 1.7 collective-permute-start.9
  108.3 6.7 %collective-permute-done.9 = f32[8,2,32,128]{3,0,2,1:T(8,128)S(1)} collective-permute-done((f32[8,2,32,128]{3,0,2,1:T(8,128)S(1)}, f32[8,2,32,128]{3,0,2,1:T(8,128)S(1)}, u32[]{:S(2)}, u32[]{:S(2)}) %collective-permute-start.9) | collective-permute-done | bytes 262176 | tf_op jit(solution)/shard_map/ppermute | solution.py:15
  115.1 2.1 %collective-permute-start.10 = (f32[4,2,32,128]{3,0,2,1:T(4,128)S(1)}, f32[4,2,32,128]{3,0,2,1:T(4,128)S(1)}, u32[]{:S(2)}, u32[]{:S(2)}) collective-permute-start(f32[4,2,32,128]{3,0,2,1:T(4,128)S(1)} %slice.163), channel_id=1, source_target_pairs={{0,4},{1,5},{2,6},{3,7},{4,0},{5,1},{6,2},{7,3},{8,12},{9,13},{10,... | collective-permute-start | bytes 393224 | tf_op jit(solution)/shard_map/ppermute | solution.py:15
  117.2 3.0 %collective-permute-done.10 = f32[4,2,32,128]{3,0,2,1:T(4,128)S(1)} collective-permute-done((f32[4,2,32,128]{3,0,2,1:T(4,128)S(1)}, f32[4,2,32,128]{3,0,2,1:T(4,128)S(1)}, u32[]{:S(2)}, u32[]{:S(2)}) %collective-permute-start.10) | collective-permute-done | bytes 131104 | tf_op jit(solution)/shard_map/ppermute | solution.py:15
  120.2 3.4 %collective-permute-start.11 = (f32[2,2,32,128]{3,0,2,1:T(2,128)S(1)}, f32[2,2,32,128]{3,0,2,1:T(2,128)S(1)}, u32[]{:S(2)}, u32[]{:S(2)}) collective-permute-start(f32[2,2,32,128]{3,0,2,1:T(2,128)S(1)} %slice.165), channel_id=1, source_target_pairs={{0,8},{1,9},{2,10},{3,11},{4,12},{5,13},{6,14},{7,15},{8,0},{9,1},... | collective-permute-start | bytes 196616 | tf_op jit(solution)/shard_map/ppermute | solution.py:15
  123.7 2.2 %collective-permute-done.11 = f32[2,2,32,128]{3,0,2,1:T(2,128)S(1)} collective-permute-done((f32[2,2,32,128]{3,0,2,1:T(2,128)S(1)}, f32[2,2,32,128]{3,0,2,1:T(2,128)S(1)}, u32[]{:S(2)}, u32[]{:S(2)}) %collective-permute-start.11) | collective-permute-done | bytes 65568 | tf_op jit(solution)/shard_map/ppermute | solution.py:15
  126.1 3.5 %fusion.19 = f32[2,32,2,64]{3,2,1,0:T(2,128)S(1)} fusion(f32[2,32,64,128]{3,2,1,0:T(8,128)S(1)} %copy-done.1, f32[2,2,32,64]{3,0,2,1:T(2,128)S(1)} %get-tuple-element.20), kind=kOutput, calls=%fused_computation.32 | convolution fusion | flops 6291456 | bytes 2162688 | tf_op jit(solution)/shard_map/jbkd,jkcd->jbkc/dot_general | solution.py:10
  129.5 3.6 %fusion.21 = f32[2,32,2,64]{3,2,1,0:T(2,128)S(1)} fusion(f32[2,32,64,128]{3,2,1,0:T(8,128)S(1)} %copy-done.1, f32[2,2,32,64]{3,0,2,1:T(2,128)S(1)} %get-tuple-element.19), kind=kOutput, calls=%fused_computation.34 | convolution fusion | flops 6291456 | bytes 2162688 | tf_op jit(solution)/shard_map/jbkd,jkcd->jbkc/dot_general | solution.py:10
  133.2 3.4 %fusion.42 = f32[2,2,32,64]{3,1,2,0:T(2,128)S(1)} fusion(f32[2,32,2,64]{3,2,1,0:T(2,128)S(1)} %fusion.19, f32[2,32,64,128]{3,2,1,0:T(8,128)S(1)} %copy-done.1, f32[2,2,32,64]{3,0,2,1:T(2,128)S(1)} %get-tuple-element.19), kind=kOutput, calls=%fused_computation.53 | convolution fusion | flops 6299648 | bytes 2195456 | tf_op jit(solution)/shard_map/jbkd,jkcd->jbkc/dot_general | solution.py:10
  136.5 3.4 %fusion.36 = f32[2,2,32,64]{3,1,2,0:T(2,128)S(1)} fusion(f32[2,32,2,64]{3,2,1,0:T(2,128)S(1)} %fusion.21, f32[2,32,64,128]{3,2,1,0:T(8,128)S(1)} %copy-done.1, f32[2,2,32,64]{3,0,2,1:T(2,128)S(1)} %get-tuple-element.20), kind=kOutput, calls=%fused_computation.51 | convolution fusion | flops 6299648 | bytes 2195456 | tf_op jit(solution)/shard_map/jbkd,jkcd->jbkc/dot_general | solution.py:10
  140.0 3.0 %collective-permute-start.12 = (f32[2,2,32,128]{3,1,2,0:T(2,128)S(1)}, f32[2,2,32,128]{3,1,2,0:T(2,128)S(1)}, u32[]{:S(2)}, u32[]{:S(2)}) collective-permute-start(f32[2,2,32,128]{3,1,2,0:T(2,128)S(1)} %get-tuple-element.4), channel_id=1, source_target_pairs={{0,8},{1,9},{2,10},{3,11},{4,12},{5,13},{6,14},{7,15},{8,0},{9,1},... | collective-permute-start | bytes 196616 | tf_op jit(solution)/shard_map/ppermute | solution.py:15
  143.1 3.4 %fusion.76 = f32[2,32,64,64]{3,2,1,0:T(8,128)S(1)} fusion(f32[2,2,32,64]{3,0,2,1:T(2,128)S(1)} %get-tuple-element.22, f32[2,2,32,64]{3,0,2,1:T(2,128)S(1)} %get-tuple-element.20), kind=kOutput, calls=%fused_computation.118 | convolution fusion | flops 6291456 | bytes 1114112 | tf_op jit(solution)/shard_map/jbkc,jbkd->jkcd/dot_general | solution.py:10
  146.7 2.2 %collective-permute-start.13 = (f32[4,2,32,128]{3,1,2,0:T(2,128)S(1)}, f32[4,2,32,128]{3,1,2,0:T(2,128)S(1)}, u32[]{:S(2)}, u32[]{:S(2)}) collective-permute-start(f32[4,2,32,128]{3,1,2,0:T(2,128)S(1)} %pad_maximum_fusion.8), channel_id=1, source_target_pairs={{0,4},{1,5},{2,6},{3,7},{4,0},{5,1},{6,2},{7,3},{8,12},{9,13},{10,... | collective-permute-start | bytes 393224 | tf_op jit(solution)/shard_map/ppermute | solution.py:15
  148.9 3.7 %convolution_subtract_fusion = f32[2,32,64,64]{3,2,1,0:T(8,128)S(1)} fusion(f32[2,32,64,64]{3,2,1,0:T(8,128)S(1)} %fusion.76, f32[2,2,32,64]{3,0,2,1:T(2,128)S(1)} %get-tuple-element.21, f32[2,2,32,64]{3,0,2,1:T(2,128)S(1)} %get-tuple-element.19), kind=kOutput, calls=%fused_computation.40 | convolution fusion | flops 6553600 | bytes 2162688 | tf_op jit(solution)/shard_map/jbkc,jbkd->jkcd/dot_general | solution.py:10
  152.7 1.6 collective-permute-start.14
  154.3 3.4 %fusion.78 = f32[2,32,64,64]{3,2,1,0:T(8,128)S(1)} fusion(f32[2,2,32,64]{3,0,2,1:T(2,128)S(1)} %get-tuple-element.22, f32[2,2,32,64]{3,0,2,1:T(2,128)S(1)} %get-tuple-element.19), kind=kOutput, calls=%fused_computation.120 | convolution fusion | flops 6291456 | bytes 1114112 | tf_op jit(solution)/shard_map/jbkc,jbkd->jkcd/dot_general | solution.py:10
  157.7 1.4 collective-permute-done.14
  159.2 0.3 pad_maximum_fusion.3
  159.5 3.5 %convolution_add_fusion = f32[2,32,64,64]{3,2,1,0:T(8,128)S(1)} fusion(f32[2,32,64,64]{3,2,1,0:T(8,128)S(1)} %fusion.78, f32[2,2,32,64]{3,0,2,1:T(2,128)S(1)} %get-tuple-element.21, f32[2,2,32,64]{3,0,2,1:T(2,128)S(1)} %get-tuple-element.20), kind=kOutput, calls=%fused_computation.41 | convolution fusion | flops 6553600 | bytes 2162688 | tf_op jit(solution)/shard_map/jbkc,jbkd->jkcd/dot_general | solution.py:10
  163.0 1.9 %pad_maximum_fusion = f32[2,32,64,128]{3,2,1,0:T(8,128)} fusion(f32[2,32,64,64]{3,2,1,0:T(8,128)S(1)} %convolution_subtract_fusion, f32[2,32,64,64]{3,2,1,0:T(8,128)S(1)} %convolution_add_fusion), kind=kLoop, calls=%fused_computation.31 | loop fusion | flops 524288 | bytes 4194304 | tf_op jit(solution)/shard_map/concatenate | solution.py:95
  165.1 1.3 fusion.52
  166.6 1.3 convolution_add_fusion.3
  167.9 0.6 reshape.190
  168.5 4.0 %fusion.45 = f32[512,16,2,64,1]{0,3,4,2,1:T(8,128)S(1)} fusion(f32[16,2,32,2,64]{4,3,0,2,1:T(2,128)S(1)} %reshape.190, f32[512,32,1]{0,1,2:T(8,128)S(1)} %get-tuple-element.23, f32[512,32,1]{0,1,2:T(8,128)S(1)} %get-tuple-element.24), kind=kOutput, calls=%fused_computation.57 | convolution fusion | flops 805339136 | bytes 4849664 | tf_op jit(solution)/shard_map/xbkpc,zkp->xbzc/dot_general | solution.py:10
  172.5 5.8 %bitcast_add_fusion = f32[16,2,512,64]{2,3,1,0:T(8,128)} fusion(f32[512,16,2,64,1]{0,3,4,2,1:T(8,128)S(1)} %fusion.45, f32[16,2,512,64]{2,3,1,0:T(8,128)S(1)} %copy-done.3, f32[64,64]{1,0:T(8,128)S(1)} %copy-done), kind=kOutput, calls=%fused_computation.9 | convolution fusion | flops 806354944 | bytes 12599296 | tf_op jit(solution)/shard_map/xbzo,co->xbzc/dot_general | solution.py:10
  (63 shorter events, 3.6 us)
Async XLA Ops:
  0.6 71.0 %copy-start = (f32[64,64]{1,0:T(8,128)S(1)}, f32[64,64]{1,0:T(8,128)}, u32[]{:S(2)}) copy-start(f32[64,64]{1,0:T(8,128)} %param.8) | copy-start | bytes 49156
  0.9 9.6 %copy-start.7 = (s32[16]{0:T(128)S(1)}, s32[16]{0:T(128)}, u32[]{:S(2)}) copy-start(s32[16]{0:T(128)} %constant.124.clone) | copy-start | bytes 196
  12.1 23.6 %copy-start.1 = (f32[2,32,64,128]{3,2,1,0:T(8,128)S(1)}, f32[2,32,64,128]{3,2,1,0:T(8,128)}, u32[]{:S(2)}) copy-start(f32[2,32,64,128]{3,2,1,0:T(8,128)} %param.7) | copy-start | bytes 6291460
  13.3 2.1 %collective-permute-start = (f32[16,2,32,128]{3,0,2,1:T(8,128)S(1)}, f32[16,2,32,128]{3,0,2,1:T(8,128)S(1)}, u32[]{:S(2)}, u32[]{:S(2)}) collective-permute-start(f32[16,2,32,128]{3,0,2,1:T(8,128)S(1)} %slice.141), channel_id=1, source_target_pairs={{0,1},{1,0},{2,3},{3,2},{4,5},{5,4},{6,7},{7,6},{8,9},{9,8},{10,11... | collective-permute-start | bytes 1572872 | tf_op jit(solution)/shard_map/ppermute | solution.py:15
  15.4 9.6 %collective-permute-start.1 = (f32[8,2,32,128]{3,0,2,1:T(8,128)S(1)}, f32[8,2,32,128]{3,0,2,1:T(8,128)S(1)}, u32[]{:S(2)}, u32[]{:S(2)}) collective-permute-start(f32[8,2,32,128]{3,0,2,1:T(8,128)S(1)} %slice.143), channel_id=1, source_target_pairs={{0,2},{1,3},{2,0},{3,1},{4,6},{5,7},{6,4},{7,5},{8,10},{9,11},{10,... | collective-permute-start | bytes 786440 | tf_op jit(solution)/shard_map/ppermute | solution.py:15
  25.1 5.1 %collective-permute-start.2 = (f32[4,2,32,128]{3,0,2,1:T(4,128)S(1)}, f32[4,2,32,128]{3,0,2,1:T(4,128)S(1)}, u32[]{:S(2)}, u32[]{:S(2)}) collective-permute-start(f32[4,2,32,128]{3,0,2,1:T(4,128)S(1)} %slice.145), channel_id=1, source_target_pairs={{0,4},{1,5},{2,6},{3,7},{4,0},{5,1},{6,2},{7,3},{8,12},{9,13},{10,... | collective-permute-start | bytes 393224 | tf_op jit(solution)/shard_map/ppermute | solution.py:15
  30.3 5.2 %collective-permute-start.3 = (f32[2,2,32,128]{3,0,2,1:T(2,128)S(1)}, f32[2,2,32,128]{3,0,2,1:T(2,128)S(1)}, u32[]{:S(2)}, u32[]{:S(2)}) collective-permute-start(f32[2,2,32,128]{3,0,2,1:T(2,128)S(1)} %slice.147), channel_id=1, source_target_pairs={{0,8},{1,9},{2,10},{3,11},{4,12},{5,13},{6,14},{7,15},{8,0},{9,1},... | collective-permute-start | bytes 196616 | tf_op jit(solution)/shard_map/ppermute | solution.py:15
  39.7 5.4 %collective-permute-start.4 = (f32[2,2,32,128]{3,1,2,0:T(2,128)S(1)}, f32[2,2,32,128]{3,1,2,0:T(2,128)S(1)}, u32[]{:S(2)}, u32[]{:S(2)}) collective-permute-start(f32[2,2,32,128]{3,1,2,0:T(2,128)S(1)} %get-tuple-element.6), channel_id=1, source_target_pairs={{0,8},{1,9},{2,10},{3,11},{4,12},{5,13},{6,14},{7,15},{8,0},{9,1},... | collective-permute-start | bytes 196616 | tf_op jit(solution)/shard_map/ppermute | solution.py:15
  45.2 5.0 %collective-permute-start.5 = (f32[4,2,32,128]{3,1,2,0:T(2,128)S(1)}, f32[4,2,32,128]{3,1,2,0:T(2,128)S(1)}, u32[]{:S(2)}, u32[]{:S(2)}) collective-permute-start(f32[4,2,32,128]{3,1,2,0:T(2,128)S(1)} %pad_maximum_fusion.7), channel_id=1, source_target_pairs={{0,4},{1,5},{2,6},{3,7},{4,0},{5,1},{6,2},{7,3},{8,12},{9,13},{10,... | collective-permute-start | bytes 393224 | tf_op jit(solution)/shard_map/ppermute | solution.py:15
  50.4 6.4 %collective-permute-start.6 = (f32[8,2,32,128]{3,1,2,0:T(2,128)S(1)}, f32[8,2,32,128]{3,1,2,0:T(2,128)S(1)}, u32[]{:S(2)}, u32[]{:S(2)}) collective-permute-start(f32[8,2,32,128]{3,1,2,0:T(2,128)S(1)} %pad_maximum_fusion.4), channel_id=1, source_target_pairs={{0,2},{1,3},{2,0},{3,1},{4,6},{5,7},{6,4},{7,5},{8,10},{9,11},{10,... | collective-permute-start | bytes 786440 | tf_op jit(solution)/shard_map/ppermute | solution.py:15
  57.2 2.0 %collective-permute-start.7 = (f32[16,2,32,128]{3,1,2,0:T(2,128)S(1)}, f32[16,2,32,128]{3,1,2,0:T(2,128)S(1)}, u32[]{:S(2)}, u32[]{:S(2)}) collective-permute-start(f32[16,2,32,128]{3,1,2,0:T(2,128)S(1)} %pad_maximum_fusion.2), channel_id=1, source_target_pairs={{0,1},{1,0},{2,3},{3,2},{4,5},{5,4},{6,7},{7,6},{8,9},{9,8},{10,11... | collective-permute-start | bytes 1572872 | tf_op jit(solution)/shard_map/ppermute | solution.py:15
  63.1 8.6 %copy-start.6 = (f32[64]{0:T(128)S(1)}, f32[64]{0:T(128)}, u32[]{:S(2)}) copy-start(f32[64]{0:T(128)} %param.9) | copy-start | bytes 772
  66.8 4.8 %copy-start.4 = (f32[16,2,512,64]{2,3,1,0:T(8,128)S(1)}, f32[16,2,512,64]{2,3,1,0:T(8,128)}, u32[]{:S(2)}) copy-start(f32[16,2,512,64]{2,3,1,0:T(8,128)} %param.6) | copy-start | bytes 12582916
  71.7 20.1 %copy-start.5 = (f32[32,1,512]{2,0,1:T(8,128)S(1)}, f32[32,1,512]{2,0,1:T(8,128)}, u32[]{:S(2)}) copy-start(f32[32,1,512]{2,0,1:T(8,128)} %get-tuple-element.26) | copy-start | bytes 196612
  89.8 2.0 %copy-start.2 = (f32[16,2,512,64]{2,3,1,0:T(8,128)}, f32[16,2,512,64]{2,3,1,0:T(8,128)S(1)}, u32[]{:S(2)}) copy-start(f32[16,2,512,64]{2,3,1,0:T(8,128)S(1)} %get-tuple-element.7) | copy-start | bytes 12582916
  104.5 2.0 %collective-permute-start.8 = (f32[16,2,32,128]{3,0,2,1:T(8,128)S(1)}, f32[16,2,32,128]{3,0,2,1:T(8,128)S(1)}, u32[]{:S(2)}, u32[]{:S(2)}) collective-permute-start(f32[16,2,32,128]{3,0,2,1:T(8,128)S(1)} %slice.159), channel_id=1, source_target_pairs={{0,1},{1,0},{2,3},{3,2},{4,5},{5,4},{6,7},{7,6},{8,9},{9,8},{10,11... | collective-permute-start | bytes 1572872 | tf_op jit(solution)/shard_map/ppermute | solution.py:15
  106.6 8.4 %collective-permute-start.9 = (f32[8,2,32,128]{3,0,2,1:T(8,128)S(1)}, f32[8,2,32,128]{3,0,2,1:T(8,128)S(1)}, u32[]{:S(2)}, u32[]{:S(2)}) collective-permute-start(f32[8,2,32,128]{3,0,2,1:T(8,128)S(1)} %slice.161), channel_id=1, source_target_pairs={{0,2},{1,3},{2,0},{3,1},{4,6},{5,7},{6,4},{7,5},{8,10},{9,11},{10,... | collective-permute-start | bytes 786440 | tf_op jit(solution)/shard_map/ppermute | solution.py:15
  115.1 5.1 %collective-permute-start.10 = (f32[4,2,32,128]{3,0,2,1:T(4,128)S(1)}, f32[4,2,32,128]{3,0,2,1:T(4,128)S(1)}, u32[]{:S(2)}, u32[]{:S(2)}) collective-permute-start(f32[4,2,32,128]{3,0,2,1:T(4,128)S(1)} %slice.163), channel_id=1, source_target_pairs={{0,4},{1,5},{2,6},{3,7},{4,0},{5,1},{6,2},{7,3},{8,12},{9,13},{10,... | collective-permute-start | bytes 393224 | tf_op jit(solution)/shard_map/ppermute | solution.py:15
  120.2 5.7 %collective-permute-start.11 = (f32[2,2,32,128]{3,0,2,1:T(2,128)S(1)}, f32[2,2,32,128]{3,0,2,1:T(2,128)S(1)}, u32[]{:S(2)}, u32[]{:S(2)}) collective-permute-start(f32[2,2,32,128]{3,0,2,1:T(2,128)S(1)} %slice.165), channel_id=1, source_target_pairs={{0,8},{1,9},{2,10},{3,11},{4,12},{5,13},{6,14},{7,15},{8,0},{9,1},... | collective-permute-start | bytes 196616 | tf_op jit(solution)/shard_map/ppermute | solution.py:15
  140.0 6.5 %collective-permute-start.12 = (f32[2,2,32,128]{3,1,2,0:T(2,128)S(1)}, f32[2,2,32,128]{3,1,2,0:T(2,128)S(1)}, u32[]{:S(2)}, u32[]{:S(2)}) collective-permute-start(f32[2,2,32,128]{3,1,2,0:T(2,128)S(1)} %get-tuple-element.4), channel_id=1, source_target_pairs={{0,8},{1,9},{2,10},{3,11},{4,12},{5,13},{6,14},{7,15},{8,0},{9,1},... | collective-permute-start | bytes 196616 | tf_op jit(solution)/shard_map/ppermute | solution.py:15
  146.7 5.9 %collective-permute-start.13 = (f32[4,2,32,128]{3,1,2,0:T(2,128)S(1)}, f32[4,2,32,128]{3,1,2,0:T(2,128)S(1)}, u32[]{:S(2)}, u32[]{:S(2)}) collective-permute-start(f32[4,2,32,128]{3,1,2,0:T(2,128)S(1)} %pad_maximum_fusion.8), channel_id=1, source_target_pairs={{0,4},{1,5},{2,6},{3,7},{4,0},{5,1},{6,2},{7,3},{8,12},{9,13},{10,... | collective-permute-start | bytes 393224 | tf_op jit(solution)/shard_map/ppermute | solution.py:15
  152.7 6.4 %collective-permute-start.14 = (f32[8,2,32,128]{3,1,2,0:T(2,128)S(1)}, f32[8,2,32,128]{3,1,2,0:T(2,128)S(1)}, u32[]{:S(2)}, u32[]{:S(2)}) collective-permute-start(f32[8,2,32,128]{3,1,2,0:T(2,128)S(1)} %pad_maximum_fusion.5), channel_id=1, source_target_pairs={{0,2},{1,3},{2,0},{3,1},{4,6},{5,7},{6,4},{7,5},{8,10},{9,11},{10,... | collective-permute-start | bytes 786440 | tf_op jit(solution)/shard_map/ppermute | solution.py:15
  159.5 5.6 %collective-permute-start.15 = (f32[16,2,32,128]{3,1,2,0:T(2,128)S(1)}, f32[16,2,32,128]{3,1,2,0:T(2,128)S(1)}, u32[]{:S(2)}, u32[]{:S(2)}) collective-permute-start(f32[16,2,32,128]{3,1,2,0:T(2,128)S(1)} %pad_maximum_fusion.3), channel_id=1, source_target_pairs={{0,1},{1,0},{2,3},{3,2},{4,5},{5,4},{6,7},{7,6},{8,9},{9,8},{10,11... | collective-permute-start | bytes 1572872 | tf_op jit(solution)/shard_map/ppermute | solution.py:15
  168.5 4.0 %copy-start.3 = (f32[16,2,512,64]{2,3,1,0:T(8,128)S(1)}, f32[16,2,512,64]{2,3,1,0:T(8,128)}, u32[]{:S(2)}) copy-start(f32[16,2,512,64]{2,3,1,0:T(8,128)} %copy-done.2) | copy-start | bytes 12582916
where the time goes:
time: 181 us; the launch traced here: 179 us
  matrix products  89.3 us (49%)
  waiting for transfers between devices  39.9 us (22%)
  starting transfers between devices  29.2 us (16%)
  local copies, waits for them, and re-layouts  10.2 us (6%)
  other arithmetic  8.45 us (5%)
    dot_general x24, matrix products, hi_einsum(): return jnp.einsum(form, left, right, precision=lax.Precision.HIGHEST)  89.3 us
    ppermute x16, waiting for transfers between devices, swap(): return lax.ppermute(values, 'stream', [(i, i ^ bit) for i in range(count)])  39.9 us
    ppermute x16, starting transfers between devices, swap(): return lax.ppermute(values, 'stream', [(i, i ^ bit) for i in range(count)])  29.2 us
  transfers between devices with their start and end apart: 16, of which 13 were waited for; matrix products, arithmetic and copies ran while one was open for 10% of the time, Pallas kernels for 0%

commit v1 on v0

v1 whole, which is shorter than its diff:
```python
import functools
import math

import jax
import jax.numpy as jnp
import numpy as np
from jax import lax
from jax.experimental import pallas as pl
from jax.experimental.pallas import tpu as pltpu
from jax.sharding import PartitionSpec as P

F32 = jnp.float32
BF16 = jnp.bfloat16
LANES = 128
SUB = 8
VMEM_LIMIT = 48 << 20


def split_np(values):
    values = values.astype(np.float32)
    high = values.astype(BF16)
    low = (values - high.astype(np.float32)).astype(BF16)
    return high, low


def span_tables(length, modes, scale):
    angle = 2.0 * np.pi * (np.outer(np.arange(length), np.arange(modes)) % length) / length
    forward = np.concatenate([np.cos(angle), -np.sin(angle)], axis=1)
    factor = np.where(np.arange(modes) == 0, 1.0, 2.0) / scale
    backward = forward * np.concatenate([factor, factor])[None, :]

    def analysis(table):
        flipped = np.concatenate([table[:, modes:], -table[:, :modes]], axis=1)
        both = np.concatenate([table, flipped], axis=1)
        return np.concatenate(split_np(both), axis=1)

    def synthesis(table):
        return np.concatenate(split_np(table.T), axis=0)

    return analysis(forward), analysis(backward), synthesis(forward), synthesis(backward)


def stage_bits():
    count = lax.axis_size("stream")
    bits = [1 << i for i in range(count.bit_length() - 1)]
    assert 1 << len(bits) == count
    return bits


def stream_tables(owned, total_modes, cells):
    me = lax.axis_index("stream")
    pattern = [0]
    for bit in reversed(stage_bits()):
        pattern = pattern + [p | bit for p in pattern]
    length = cells * lax.axis_size("stream")
    pattern = np.repeat(np.asarray(pattern, np.int32), owned)
    inner = np.tile(np.arange(owned, dtype=np.int32), total_modes // owned)

    def angles(pattern, inner, cell):
        rows = (pattern ^ me) * owned + inner
        wave = jnp.where(rows < total_modes // 2, rows, rows + length - total_modes)
        phase = wave * (me * cells + cell) % length
        return phase.astype(F32) * (2.0 * math.pi / length)

    lane = np.arange(2 * cells * SUB)
    down = angles(pattern[:, None], inner[:, None], (lane[None, :] // SUB % cells).astype(np.int32))
    down = jnp.where(lane[None, :] < cells * SUB, jnp.cos(down), jnp.sin(down))
    row = np.arange(2 * cells)
    up = angles(
        np.repeat(pattern, SUB)[None, :],
        np.repeat(inner, SUB)[None, :],
        (row[:, None] % cells).astype(np.int32),
    )
    up = jnp.where(row[:, None] < cells, jnp.cos(up), jnp.sin(up))
    return down, up


def split(values):
    high = values.astype(BF16)
    return high, (values - high.astype(F32)).astype(BF16)


def dot(left, right):
    return jnp.dot(left, right, preferred_element_type=F32)


def expand_table(table_ref, scratch_ref):
    rows, lanes = table_ref.shape
    full = jnp.broadcast_to(table_ref[...][:, None, :], (rows, SUB, lanes)).reshape(rows * SUB, lanes)
    row = lax.broadcasted_iota(jnp.int32, full.shape, 0) % SUB
    lane = lax.broadcasted_iota(jnp.int32, full.shape, 1) % SUB
    high, low = split(jnp.where(row == lane, full, 0.0))
    scratch_ref[0] = high
    scratch_ref[1] = low


def analyse(values_high, values_low, table_ref, at, coef_ref):
    full = dot(values_high, table_ref[...])
    full = full[:, :LANES] + full[:, LANES:] + dot(values_low, table_ref[:, :LANES])
    cells = coef_ref.shape[1] // (2 * SUB)
    half = 4 * SUB
    low_lane = lax.broadcasted_iota(jnp.int32, (half, LANES), 1) < LANES // 2
    for i in range(full.shape[0] // (2 * half)):
        low = full[2 * half * i : 2 * half * i + half]
        high = full[2 * half * i + half : 2 * half * (i + 1)]
        plain = jnp.where(low_lane, low, pltpu.roll(high, LANES // 2, 1))
        flipped = jnp.where(low_lane, pltpu.roll(low, LANES // 2, 1), high)
        for block in range(half // SUB):
            rows = slice(SUB * block, SUB * (block + 1))
            coef_ref[block, pl.ds(pl.multiple_of((at + i) * SUB, SUB), SUB)] = plain[rows]
            coef_ref[block, pl.ds(pl.multiple_of((cells + at + i) * SUB, SUB), SUB)] = flipped[rows]


def to_modes(coef_ref, table_ref, keep_ref, send_ref):
    modes = 2 * keep_ref.shape[0]
    for block in range(coef_ref.shape[0]):
        high, low = split(coef_ref[block])
        full = dot(table_ref[0], jnp.concatenate([high, low], axis=1))
        full = full[:, :LANES] + full[:, LANES:] + dot(table_ref[1], high)
        full = full.reshape(modes, SUB, LANES)
        rows = slice(SUB * block, SUB * (block + 1))
        keep_ref[:, 0, rows] = full[: modes // 2]
        send_ref[:, 0, rows] = full[modes // 2 :]


def from_modes(front_ref, back_ref, table_ref, inv_ref):
    modes = 2 * front_ref.shape[0]
    cells = inv_ref.shape[0]
    lane = lax.broadcasted_iota(jnp.int32, (cells * SUB, LANES), 1)
    real = lane % (LANES // 2) < LANES // 4
    for block in range(inv_ref.shape[1] // SUB):
        rows = slice(SUB * block, SUB * (block + 1))
        values = jnp.concatenate([front_ref[:, 0, rows], back_ref[:, 0, rows]], axis=0)
        high, low = split(values.reshape(modes * SUB, LANES))
        full = dot(table_ref[0], jnp.concatenate([high, low], axis=1))
        full = full[:, :LANES] + full[:, LANES:] + dot(table_ref[1], high)
        plain, other = full[: cells * SUB], full[cells * SUB :]
        turned = jnp.where(
            real, -pltpu.roll(other, 3 * LANES // 4, 1), pltpu.roll(other, LANES // 4, 1)
        )
        inv_ref[:, rows] = (plain + turned).reshape(cells, SUB, LANES)


def synthesise(inv, weight, table_ref, high, low):
    half = inv.shape[0]
    low_lane = lax.broadcasted_iota(jnp.int32, (half, LANES), 1) < LANES // 2
    first = jnp.where(low_lane, inv, weight[:half])
    second = jnp.where(low_lane, pltpu.roll(inv, LANES // 2, 1), weight[half:])
    lhs_high, lhs_low = split(jnp.concatenate([first, second], axis=0))
    lhs = jnp.concatenate(
        [
            jnp.concatenate([lhs_high, lhs_high], axis=1),
            jnp.concatenate([lhs_low, jnp.zeros_like(lhs_low)], axis=1),
        ],
        axis=0,
    )
    width = LANES // 2
    rhs = jnp.concatenate([table_ref[:width], high, table_ref[width:], low], axis=0)
    full = dot(lhs, rhs)
    return full[: 2 * half] + full[2 * half :]


def normal_parts(values):
    density = jnp.exp(-0.5 * values * values) * (1.0 / math.sqrt(2.0 * math.pi))
    return 0.5 * (1.0 + lax.erf(values * (1.0 / math.sqrt(2.0)))), density


def transpose_out(rows):
    parts = []
    for half in range(2):
        for part in range(2):
            shift = part * (LANES // 2) + half * (LANES // 4)
            parts.append(pltpu.roll(rows, LANES - shift, 1) if shift else rows)
    return jnp.concatenate(parts, axis=0).T[: LANES // 4]


def transpose_in(values):
    quarter = LANES // 4
    turned = jnp.concatenate([values] * 4, axis=0).T
    lane = lax.broadcasted_iota(jnp.int32, (quarter, LANES), 1) // quarter
    result = turned[:quarter]
    for half in range(2):
        for part in range(2):
            rows = turned[quarter * (2 * half + part) : quarter * (2 * half + part + 1)]
            result = jnp.where(lane == 2 * part + half, rows, result)
    return result


def turn_down(rows):
    lane = lax.broadcasted_iota(jnp.int32, rows.shape, 1) < LANES // 2
    rolled = pltpu.roll(rows, LANES // 2, 1)
    return jnp.where(lane, rolled, -rolled)


def spanwise_kernel(x_ref, table_ref, down_ref, keep_ref, send_ref, coef_ref, down_scr):
    step = pl.program_id(1)
    cells, _, channels, span = x_ref.shape

    @pl.when((step == 0) & (pl.program_id(0) == 0))
    def _():
        expand_table(down_ref, down_scr)

    high, low = split(x_ref[...].reshape(cells * channels, span))
    analyse(high, low, table_ref, step * cells, coef_ref)

    @pl.when(step == pl.num_programs(1) - 1)
    def _():
        to_modes(coef_ref, down_scr, keep_ref, send_ref)


def mix_kernel(*refs):
    *piece_refs, w_ref, modes_ref, mixed_ref, first_scr, second_scr = refs
    planes = modes_ref.shape[1]
    kz_count = w_ref.shape[1]
    quarter = LANES // 4
    for plane in range(planes):
        total = piece_refs[0][0, plane]
        for ref in piece_refs[1:]:
            total = total + ref[0, plane]
        modes_ref[0, plane] = total
        for kz in range(kz_count):
            sums = [None, None]
            for half in range(2):
                weight = w_ref[0, kz, quarter * half : quarter * (half + 1)]
                for part in range(2):
                    at = half * (LANES // 2) + part * quarter + kz
                    term = total[:, at : at + 1] * weight
                    sums[part] = term if sums[part] is None else sums[part] + term
            first_scr[kz : kz + 1] = jnp.sum(sums[0], axis=0, keepdims=True)
            second_scr[kz : kz + 1] = jnp.sum(sums[1], axis=0, keepdims=True)
        rows = first_scr[...] - turn_down(second_scr[...])
        mixed_ref[0, plane] = transpose_out(rows)


def middle_kernel(
    x_ref, up_ref, front_ref, back_ref, local_ref, bias_ref, synth_ref, table_ref,
    down_ref, back_table_ref, *rest
):
    act_ref, dpre_ref, keep_ref, send_ref, inv_ref, coef_ref, down_scr, back_scr = rest[-8:]
    step = pl.program_id(1)
    cells, _, channels, span = x_ref.shape

    @pl.when((step == 0) & (pl.program_id(0) == 0))
    def _():
        expand_table(down_ref, down_scr)
        expand_table(back_table_ref, back_scr)

    @pl.when(step == 0)
    def _():
        from_modes(front_ref, back_ref, back_scr, inv_ref)

    for cell in range(cells):
        high, low = split(x_ref[cell, 0])
        pre = synthesise(inv_ref[step * cells + cell], local_ref[...], synth_ref, high, low)
        pre = pre + bias_ref[...]
        cumulative, density = normal_parts(pre)
        act_ref[cell, 0] = pre * cumulative
        dpre = up_ref[cell, 0] * (cumulative + pre * density)
        dpre_ref[cell, 0] = dpre
        high, low = split(dpre)
        analyse(high, low, table_ref, step * cells + cell, coef_ref)

    @pl.when(step == pl.num_programs(1) - 1)
    def _():
        to_modes(coef_ref, down_scr, keep_ref, send_ref)


def adjoint_kernel(*refs):
    *piece_refs, w_ref, dmixed_ref, dmodes_ref = refs
    planes = dmixed_ref.shape[1]
    kz_count, channels, width = w_ref.shape[1:]
    quarter = LANES // 4
    weight = w_ref[0].reshape(kz_count * channels, width)
    w_high, w_low = split(weight)
    lane = lax.broadcasted_iota(jnp.int32, (channels, LANES // 2), 1) % quarter
    for plane in range(planes):
        total = piece_refs[0][0, plane]
        for ref in piece_refs[1:]:
            total = total + ref[0, plane]
        dmixed_ref[0, plane] = total
        rows = transpose_in(total)
        both = jnp.concatenate([rows, turn_down(rows)], axis=0)
        high, low = split(both)
        right = jnp.concatenate([high, low], axis=0).T
        full = dot(w_high, right)
        full = full[:, : LANES // 2] + full[:, LANES // 2 :] + dot(w_low, right[:, : LANES // 2])
        full = full.reshape(kz_count, channels, LANES // 2)
        result = jnp.zeros((channels, LANES // 2), F32)
        for kz in range(kz_count):
            result = jnp.where(lane == kz, full[kz], result)
        dmodes_ref[0, plane] = jnp.concatenate(
            [result[: channels // 2], result[channels // 2 :]], axis=1
        )


def weight_grad_kernel(modes_ref, dmixed_ref, grad_ref, rows_scr):
    planes = modes_ref.shape[1]
    kz_count = grad_ref.shape[1]
    quarter = LANES // 4
    for plane in range(planes):
        rows = transpose_in(dmixed_ref[0, plane])
        rows_scr[2 * plane] = rows
        rows_scr[2 * plane + 1] = turn_down(rows)
    for kz in range(kz_count):
        for half in range(2):
            total = None
            for plane in range(planes):
                for part in range(2):
                    at = half * (LANES // 2) + part * quarter + kz
                    column = modes_ref[0, plane, :, at : at + 1]
                    term = column * rows_scr[2 * plane + part, kz : kz + 1]
                    total = term if total is None else total + term
            grad_ref[0, kz, quarter * half : quarter * (half + 1)] = total


def input_grad_kernel(dpre_ref, front_ref, back_ref, local_ref, synth_ref, back_table_ref, *rest):
    out_ref, inv_ref, back_scr = rest[-3:]
    step = pl.program_id(1)
    cells = dpre_ref.shape[0]

    @pl.when((step == 0) & (pl.program_id(0) == 0))
    def _():
        expand_table(back_table_ref, back_scr)

    @pl.when(step == 0)
    def _():
        from_modes(front_ref, back_ref, back_scr, inv_ref)

    for cell in range(cells):
        high, low = split(dpre_ref[cell, 0])
        out_ref[cell, 0] = synthesise(
            inv_ref[step * cells + cell], local_ref[...], synth_ref, high, low
        )


def swap(values, bit):
    count = lax.axis_size("stream")
    return lax.ppermute(values, "stream", [(i, i ^ bit) for i in range(count)])


def scatter_sum(keep, send):
    bits = stage_bits()
    pieces = [keep, swap(send, bits[0])]
    half = keep.shape[0]
    for bit in bits[1:]:
        half //= 2
        part = pieces[0][half : 2 * half]
        for piece in pieces[1:]:
            part = part + piece[half : 2 * half]
        pieces.append(swap(part, bit))
    return pieces


def gather_all(values):
    bits = stage_bits()
    for bit in reversed(bits[1:]):
        values = jnp.concatenate([values, swap(values, bit)], axis=0)
    return values, swap(values, bits[0])


def params():
    return pltpu.CompilerParams(vmem_limit_bytes=VMEM_LIMIT)


def whole(array):
    rank = len(array.shape)
    return pl.BlockSpec(array.shape, lambda *_: (0,) * rank)


def per_device(snapshot, mode_weight, local_weight, offset_bias, upstream):
    cells, planes, span, channels = snapshot.shape
    owned, kz_count = mode_weight.shape[:2]
    total_modes = owned * lax.axis_size("stream")
    half_modes = total_modes // 2
    half_channels = channels // 2
    shape = jax.ShapeDtypeStruct
    x = jnp.swapaxes(snapshot, 2, 3)
    up = jnp.swapaxes(upstream, 2, 3)
    scale = float(cells * lax.axis_size("stream") * span)
    ana_fwd, ana_inv, syn_fwd, syn_inv = map(jnp.asarray, span_tables(span, kz_count, scale))
    down, back = stream_tables(owned, total_modes, cells)
    zeros = jnp.zeros((channels, LANES // 2), F32)
    local_out = jnp.concatenate([zeros, local_weight.T], axis=1)
    local_in = jnp.concatenate([zeros, local_weight], axis=1)
    bias = jnp.broadcast_to(offset_bias[:, None], (channels, span))
    step_cells = 4
    steps = cells // step_cells
    groups = [tuple(range(planes))]
    coef_scr = pltpu.VMEM((half_channels // SUB, 2 * cells * SUB, LANES), F32)
    inv_scr = pltpu.VMEM((cells, half_channels, LANES), F32)
    down_scr = pltpu.VMEM((2, total_modes * SUB, 2 * cells * SUB), BF16)
    back_scr = pltpu.VMEM((2, 2 * cells * SUB, total_modes * SUB), BF16)

    def grid_block(first):
        return pl.BlockSpec((step_cells, 1, channels, span), lambda p, s: (s, first + p, 0, 0))

    half_block = pl.BlockSpec((half_modes, 1, half_channels, LANES), lambda p, s: (0, p, 0, 0))
    any_block = pl.BlockSpec(memory_space=pl.ANY)

    def own_block(count):
        return pl.BlockSpec((1, count, half_channels, LANES), lambda j: (j, 0, 0, 0))

    def own_shape(count):
        return shape((owned, count, half_channels, LANES), F32)

    def half_shape(count):
        return shape((half_modes, count, half_channels, LANES), F32)

    weight_block = pl.BlockSpec((1, kz_count, channels, 2 * channels), lambda j: (j, 0, 0, 0))
    act = grad_snapshot = None
    modes_all, dmixed_all, late = [], [], []
    for group in groups:
        count, first = len(group), group[0]
        keep, send = pl.pallas_call(
            spanwise_kernel,
            grid=(count, steps),
            in_specs=[grid_block(first), whole(ana_fwd), whole(down)],
            out_specs=[half_block, half_block],
            out_shape=[half_shape(count)] * 2,
            scratch_shapes=[coef_scr, down_scr],
            compiler_params=params(),
            name="spanwise",
        )(x, ana_fwd, down)
        pieces = scatter_sum(keep, send)
        modes, mixed = pl.pallas_call(
            mix_kernel,
            grid=(owned,),
            in_specs=[own_block(count)] * len(pieces) + [weight_block],
            out_specs=[own_block(count)] * 2,
            out_shape=[own_shape(count)] * 2,
            scratch_shapes=[pltpu.VMEM((kz_count, LANES), F32)] * 2,
            compiler_params=params(),
            name="mix",
        )(*pieces, mode_weight)
        modes_all.append(modes)
        front, behind = gather_all(mixed)
        extra = [] if act is None else [act]
        act, dpre, keep, send = pl.pallas_call(
            middle_kernel,
            grid=(count, steps),
            in_specs=[
                grid_block(first), grid_block(first), half_block, half_block, whole(local_out),
                whole(bias), whole(syn_inv), whole(ana_inv), whole(down), whole(back),
            ] + [any_block] * len(extra),
            out_specs=[grid_block(first), grid_block(0), half_block, half_block],
            out_shape=[shape(x.shape, F32), shape((cells, count, channels, span), F32)]
            + [half_shape(count)] * 2,
            scratch_shapes=[inv_scr, coef_scr, down_scr, back_scr],
            input_output_aliases={10: 0} if extra else {},
            compiler_params=params(),
            name="middle",
        )(x, up, front, behind, local_out, bias, syn_inv, ana_inv, down, back, *extra)
        pieces = scatter_sum(keep, send)
        dmixed, dmodes = pl.pallas_call(
            adjoint_kernel,
            grid=(owned,),
            in_specs=[own_block(count)] * len(pieces) + [weight_block],
            out_specs=[own_block(count)] * 2,
            out_shape=[own_shape(count)] * 2,
            compiler_params=params(),
            name="adjoint",
        )(*pieces, mode_weight)
        dmixed_all.append(dmixed)
        front, behind = gather_all(dmodes)
        extra = [] if grad_snapshot is None else [grad_snapshot]
        grad_snapshot = pl.pallas_call(
            input_grad_kernel,
            grid=(count, steps),
            in_specs=[
                grid_block(0), half_block, half_block, whole(local_in), whole(syn_fwd), whole(back),
            ] + [any_block] * len(extra),
            out_specs=grid_block(first),
            out_shape=shape(x.shape, F32),
            scratch_shapes=[inv_scr, back_scr],
            input_output_aliases={6: 0} if extra else {},
            compiler_params=params(),
            name="input_grad",
        )(dpre, front, behind, local_in, syn_fwd, back, *extra)
    modes = modes_all[0] if len(groups) == 1 else jnp.concatenate(modes_all, axis=1)
    dmixed = dmixed_all[0] if len(groups) == 1 else jnp.concatenate(dmixed_all, axis=1)
    grad_modes = pl.pallas_call(
        weight_grad_kernel,
        grid=(owned,),
        in_specs=[own_block(planes)] * 2,
        out_specs=weight_block,
        out_shape=shape(mode_weight.shape, F32),
        scratch_shapes=[pltpu.VMEM((2 * planes, kz_count, LANES), F32)],
        compiler_params=params(),
        name="weight_grad",
    )(modes, dmixed)
    return jnp.swapaxes(act, 2, 3), jnp.swapaxes(grad_snapshot, 2, 3), grad_modes


def solution(mesh):
    wide = P("stream", "group", None, None)
    return jax.shard_map(
        per_device,
        mesh=mesh,
        in_specs=(wide, P("stream", None, None, None), P(), P(), wide),
        out_specs=(wide, wide, wide),
        check_vma=False,
    )
```

time: 181 us -> 125 us (0.69)
  matrix products: 89.3 us -> 0 us
  Pallas kernels: 0 us -> 36 us
  waiting for transfers between devices: 39.9 us -> 48.2 us
  other arithmetic: 8.45 us -> 3.84 us
  local copies, waits for them, and re-layouts: 10.2 us -> 5.86 us
    dot_general x24 -> x0, matrix products: 89.3 us -> none  [hi_einsum(): return jnp.einsum(form, left, right, precision=lax.Precision.HIGHEST)]
    pallas_call x0 -> x6, Pallas kernels: none -> 36 us  [the longest x1 15.2 us: per_device(): pl.pallas_call(middle_kernel, grid=(count, steps), in_specs=[grid_block(f...]
    ppermute x16, waiting for transfers between devices: 39.9 us -> 48.2 us  [swap(): return lax.ppermute(values, 'stream', [(i, i ^ bit) for i in range(count)])]
    reshape x6 -> x0, local copies, waits for them, and re-layouts: 7.25 us -> none  [the longest x2 3.6 us: per_device(): hi_einsum('xbzo,kpz->xbkpo', dpre, span_inv)]
    concatenate x2 -> x0, other arithmetic: 3.08 us -> none  [the longest x1 1.93 us: mix_adjoint(): jnp.concatenate([grad_re, grad_im], axis=-1)]
    unnamed x22 -> x33, local copies, waits for them, and re-layouts: 2.19 us -> 4.84 us
    neg x4 -> x0, other arithmetic: 2.57 us -> none  [the longest x2 1.4 us: flip_back(): return jnp.concatenate([-values[..., half:], values[..., :half]], axis=-1)]
  transfers between devices with their start and end apart: 16 -> 16, of which waited for: 13 -> 14; matrix products, arithmetic and copies ran while one was open for 10% -> 2% of each run, Pallas kernels for 0% -> 3%
where the time goes in v1:
time: 125 us; the launch traced here: 124 us
  waiting for transfers between devices  48.2 us (39%)
  Pallas kernels  36 us (29%)
  starting transfers between devices  29 us (23%)
  local copies, waits for them, and re-layouts  5.86 us (5%)
  other arithmetic  3.84 us (3%)
    ppermute x16, waiting for transfers between devices, swap(): return lax.ppermute(values, 'stream', [(i, i ^ bit) for i in range(count)])  48.2 us
    ppermute x16, starting transfers between devices, swap(): return lax.ppermute(values, 'stream', [(i, i ^ bit) for i in range(count)])  29 us
    pallas_call x1, Pallas kernels, per_device(): pl.pallas_call(middle_kernel, grid=(count, steps), in_specs=[grid_block(f...  15.2 us
    pallas_call x1, Pallas kernels, per_device(): pl.pallas_call(input_grad_kernel, grid=(count, steps), in_specs=[grid_blo...  6.35 us
    unnamed x33, local copies, waits for them, and re-layouts  4.84 us
    pallas_call x1, Pallas kernels, per_device(): pl.pallas_call(spanwise_kernel, grid=(count, steps), in_specs=[grid_block...  4.39 us
    pallas_call x1, Pallas kernels, per_device(): pl.pallas_call(weight_grad_kernel, grid=(owned,), in_specs=[own_block(pla...  4.22 us
    pallas_call x1, Pallas kernels, per_device(): pl.pallas_call(mix_kernel, grid=(owned,), in_specs=[own_block(count)] * l...  3.88 us
  transfers between devices with their start and end apart: 16, of which 14 were waited for; matrix products, arithmetic and copies ran while one was open for 2% of the time, Pallas kernels for 3%

profile of v1, /device:TPU:0, one launch (start us, length us, event | category | flops | bytes accessed | tf_op | source)
XLA Modules:
  0.0 123.8 jit_solution(9669993872423991621)
XLA Ops:
  0.6 0.7 fusion.6
  1.3 0.7 broadcast_add_fusion
  2.0 0.9 sine_select_fusion.1.down_ref
  2.9 0.0 copy-start
  2.9 2.2 %copy-done = f32[16,2,512,64]{2,3,1,0:T(8,128)S(1)} copy-done((f32[16,2,512,64]{2,3,1,0:T(8,128)S(1)}, f32[16,2,512,64]{2,3,1,0:T(8,128)}, u32[]{:S(2)}) %copy-start) | copy-done | bytes 4194328
  5.1 0.9 copy-done.4
  6.0 4.4 %spanwise.1 = (f32[16,2,32,128]{3,2,1,0:T(8,128)S(1)}, f32[16,2,32,128]{3,2,1,0:T(8,128)S(1)}) custom-call(f32[16,2,64,512]{3,2,1,0:T(8,128)S(1)} %bitcast.12, bf16[512,256]{1,0:T(8,128)(2,1)S(1)} %copy-done.4, f32[32,256]{1,0:T(8,128)S(1)} %sine_select_fusion.1.down_ref), custom_call_target="tpu_custom_call" | custom-call | tf_op jit(solution)/shard_map/spanwise/pallas_call | solution.py:414
  10.4 0.0 copy-start.12
  10.4 0.0 copy-start.7
  10.4 0.0 copy-start.8
  10.5 0.0 copy-start.9
  10.5 0.0 copy-start.11
  10.5 0.0 copy-start.10
  10.5 0.0 copy-start.3
  10.5 0.5 collective-permute-start
  11.0 1.5 %collective-permute-done.refs_1_ = f32[16,2,32,128]{3,2,1,0:T(8,128)S(1)} collective-permute-done((f32[16,2,32,128]{3,2,1,0:T(8,128)S(1)}, f32[16,2,32,128]{3,2,1,0:T(8,128)S(1)}, u32[]{:S(2)}, u32[]{:S(2)}) %collective-permute-start) | collective-permute-done | bytes 524320 | tf_op jit(solution)/shard_map/ppermute | solution.py:338
  12.6 2.9 %collective-permute-start.1 = (f32[8,2,32,128]{3,2,1,0:T(8,128)S(1)}, f32[8,2,32,128]{3,2,1,0:T(8,128)S(1)}, u32[]{:S(2)}, u32[]{:S(2)}) collective-permute-start(f32[8,2,32,128]{3,2,1,0:T(8,128)S(1)} %slice_add_fusion.1), channel_id=1, source_target_pairs={{0,2},{1,3},{2,0},{3,1},{4,6},{5,7},{6,4},{7,5},{8,10},{9,11},{10,... | collective-permute-start | bytes 786440 | tf_op jit(solution)/shard_map/ppermute | solution.py:338
  15.6 6.6 %collective-permute-done.1.refs_2_ = f32[8,2,32,128]{3,2,1,0:T(8,128)S(1)} collective-permute-done((f32[8,2,32,128]{3,2,1,0:T(8,128)S(1)}, f32[8,2,32,128]{3,2,1,0:T(8,128)S(1)}, u32[]{:S(2)}, u32[]{:S(2)}) %collective-permute-start.1) | collective-permute-done | bytes 262176 | tf_op jit(solution)/shard_map/ppermute | solution.py:338
  22.2 1.9 %collective-permute-start.2 = (f32[4,2,32,128]{3,2,1,0:T(8,128)S(1)}, f32[4,2,32,128]{3,2,1,0:T(8,128)S(1)}, u32[]{:S(2)}, u32[]{:S(2)}) collective-permute-start(f32[4,2,32,128]{3,2,1,0:T(8,128)S(1)} %slice_add_fusion.4), channel_id=1, source_target_pairs={{0,4},{1,5},{2,6},{3,7},{4,0},{5,1},{6,2},{7,3},{8,12},{9,13},{10,... | collective-permute-start | bytes 393224 | tf_op jit(solution)/shard_map/ppermute | solution.py:338
  24.1 3.2 %collective-permute-done.2.refs_3_ = f32[4,2,32,128]{3,2,1,0:T(8,128)S(1)} collective-permute-done((f32[4,2,32,128]{3,2,1,0:T(8,128)S(1)}, f32[4,2,32,128]{3,2,1,0:T(8,128)S(1)}, u32[]{:S(2)}, u32[]{:S(2)}) %collective-permute-start.2) | collective-permute-done | bytes 131104 | tf_op jit(solution)/shard_map/ppermute | solution.py:338
  27.3 2.8 %collective-permute-start.3 = (f32[2,2,32,128]{3,2,1,0:T(8,128)S(1)}, f32[2,2,32,128]{3,2,1,0:T(8,128)S(1)}, u32[]{:S(2)}, u32[]{:S(2)}) collective-permute-start(f32[2,2,32,128]{3,2,1,0:T(8,128)S(1)} %slice_add_fusion.9), channel_id=1, source_target_pairs={{0,8},{1,9},{2,10},{3,11},{4,12},{5,13},{6,14},{7,15},{8,0},{9,1},... | collective-permute-start | bytes 196616 | tf_op jit(solution)/shard_map/ppermute | solution.py:338
  30.1 2.4 %collective-permute-done.3.refs_4_ = f32[2,2,32,128]{3,2,1,0:T(8,128)S(1)} collective-permute-done((f32[2,2,32,128]{3,2,1,0:T(8,128)S(1)}, f32[2,2,32,128]{3,2,1,0:T(8,128)S(1)}, u32[]{:S(2)}, u32[]{:S(2)}) %collective-permute-start.3) | collective-permute-done | bytes 65568 | tf_op jit(solution)/shard_map/ppermute | solution.py:338
  32.5 3.9 %mix.1 = (f32[2,2,32,128]{3,2,1,0:T(8,128)S(1)}, f32[2,2,32,128]{3,2,1,0:T(8,128)S(1)}) custom-call(f32[16,2,32,128]{3,2,1,0:T(8,128)S(1)} %get-tuple-element.13.refs_0_, f32[16,2,32,128]{3,2,1,0:T(8,128)S(1)} %collective-permute-done.refs_1_, f32[8,2,32,128]{3,2,1,0:T(8,128)S(1)} %collective-permute-done.1.refs_2_, ...), custom_call_target="tpu_custom_call" | custom-call | tf_op jit(solution)/shard_map/mix/pallas_call | solution.py:425
  36.4 2.9 %collective-permute-start.4 = (f32[2,2,32,128]{3,2,1,0:T(8,128)S(1)}, f32[2,2,32,128]{3,2,1,0:T(8,128)S(1)}, u32[]{:S(2)}, u32[]{:S(2)}) collective-permute-start(f32[2,2,32,128]{3,2,1,0:T(8,128)S(1)} %get-tuple-element.15), channel_id=1, source_target_pairs={{0,8},{1,9},{2,10},{3,11},{4,12},{5,13},{6,14},{7,15},{8,0},{9,1},... | collective-permute-start | bytes 196616 | tf_op jit(solution)/shard_map/ppermute | solution.py:338
  39.3 2.5 %collective-permute-done.4 = f32[2,2,32,128]{3,2,1,0:T(8,128)S(1)} collective-permute-done((f32[2,2,32,128]{3,2,1,0:T(8,128)S(1)}, f32[2,2,32,128]{3,2,1,0:T(8,128)S(1)}, u32[]{:S(2)}, u32[]{:S(2)}) %collective-permute-start.4) | collective-permute-done | bytes 65568 | tf_op jit(solution)/shard_map/ppermute | solution.py:338
  41.8 2.3 %collective-permute-start.5 = (f32[4,2,32,128]{3,2,1,0:T(8,128)S(1)}, f32[4,2,32,128]{3,2,1,0:T(8,128)S(1)}, u32[]{:S(2)}, u32[]{:S(2)}) collective-permute-start(f32[4,2,32,128]{3,2,1,0:T(8,128)S(1)} %pad_maximum_fusion.2), channel_id=1, source_target_pairs={{0,4},{1,5},{2,6},{3,7},{4,0},{5,1},{6,2},{7,3},{8,12},{9,13},{10,... | collective-permute-start | bytes 393224 | tf_op jit(solution)/shard_map/ppermute | solution.py:338
  44.0 2.9 %collective-permute-done.5 = f32[4,2,32,128]{3,2,1,0:T(8,128)S(1)} collective-permute-done((f32[4,2,32,128]{3,2,1,0:T(8,128)S(1)}, f32[4,2,32,128]{3,2,1,0:T(8,128)S(1)}, u32[]{:S(2)}, u32[]{:S(2)}) %collective-permute-start.5) | collective-permute-done | bytes 131104 | tf_op jit(solution)/shard_map/ppermute | solution.py:338
  47.0 1.6 %collective-permute-start.6 = (f32[8,2,32,128]{3,2,1,0:T(8,128)S(1)}, f32[8,2,32,128]{3,2,1,0:T(8,128)S(1)}, u32[]{:S(2)}, u32[]{:S(2)}) collective-permute-start(f32[8,2,32,128]{3,2,1,0:T(8,128)S(1)} %pad_maximum_fusion), channel_id=1, source_target_pairs={{0,2},{1,3},{2,0},{3,1},{4,6},{5,7},{6,4},{7,5},{8,10},{9,11},{10,... | collective-permute-start | bytes 786440 | tf_op jit(solution)/shard_map/ppermute | solution.py:338
  48.6 4.8 %collective-permute-done.6 = f32[8,2,32,128]{3,2,1,0:T(8,128)S(1)} collective-permute-done((f32[8,2,32,128]{3,2,1,0:T(8,128)S(1)}, f32[8,2,32,128]{3,2,1,0:T(8,128)S(1)}, u32[]{:S(2)}, u32[]{:S(2)}) %collective-permute-start.6) | collective-permute-done | bytes 262176 | tf_op jit(solution)/shard_map/ppermute | solution.py:338
  53.5 0.1 collective-permute-start.7
  53.6 0.5 add_bitcast_fusion
  54.1 0.7 copy.20
  54.8 0.8 concatenate.31.local_ref
  55.6 0.0 copy-done.8
  55.6 0.9 sine_select_fusion.back_table_ref
  56.5 0.0 collective-permute-done.7.back_ref
  56.5 0.1 broadcast_in_dim.29.bias_ref
  56.6 0.0 copy-done.3
  56.6 0.0 copy-start.6
  56.6 0.9 copy-done.6
  57.5 15.2 %middle.1 = (f32[16,2,64,512]{3,2,1,0:T(8,128)}, f32[16,2,64,512]{3,2,1,0:T(8,128)}, f32[16,2,32,128]{3,2,1,0:T(8,128)S(1)}, f32[16,2,32,128]{3,2,1,0:T(8,128)S(1)}) custom-call(f32[16,2,64,512]{3,2,1,0:T(8,128)} %bitcast.11, f32[16,2,64,512]{3,2,1,0:T(8,128)} %bitcast.14, f32[16,2,32,128]{3,2,1,0:T(8,128)S(1)} %constant_dynamic-update-slice_fusion.front_ref, ...), custom_call_target="tpu_custom_call" | custom-call | tf_op jit(solution)/shard_map/middle/pallas_call | solution.py:438
  72.7 0.5 collective-permute-start.8
  73.2 1.5 %collective-permute-done.8.refs_1_ = f32[16,2,32,128]{3,2,1,0:T(8,128)S(1)} collective-permute-done((f32[16,2,32,128]{3,2,1,0:T(8,128)S(1)}, f32[16,2,32,128]{3,2,1,0:T(8,128)S(1)}, u32[]{:S(2)}, u32[]{:S(2)}) %collective-permute-start.8) | collective-permute-done | bytes 524320 | tf_op jit(solution)/shard_map/ppermute | solution.py:338
  74.8 0.0 copy-start.2
  74.8 0.0 copy-start.5
  74.8 1.6 %collective-permute-start.9 = (f32[8,2,32,128]{3,2,1,0:T(8,128)S(1)}, f32[8,2,32,128]{3,2,1,0:T(8,128)S(1)}, u32[]{:S(2)}, u32[]{:S(2)}) collective-permute-start(f32[8,2,32,128]{3,2,1,0:T(8,128)S(1)} %slice_add_fusion), channel_id=1, source_target_pairs={{0,2},{1,3},{2,0},{3,1},{4,6},{5,7},{6,4},{7,5},{8,10},{9,11},{10,... | collective-permute-start | bytes 786440 | tf_op jit(solution)/shard_map/ppermute | solution.py:338
  76.4 7.1 %collective-permute-done.9.refs_2_ = f32[8,2,32,128]{3,2,1,0:T(8,128)S(1)} collective-permute-done((f32[8,2,32,128]{3,2,1,0:T(8,128)S(1)}, f32[8,2,32,128]{3,2,1,0:T(8,128)S(1)}, u32[]{:S(2)}, u32[]{:S(2)}) %collective-permute-start.9) | collective-permute-done | bytes 262176 | tf_op jit(solution)/shard_map/ppermute | solution.py:338
  83.5 2.1 %collective-permute-start.10 = (f32[4,2,32,128]{3,2,1,0:T(8,128)S(1)}, f32[4,2,32,128]{3,2,1,0:T(8,128)S(1)}, u32[]{:S(2)}, u32[]{:S(2)}) collective-permute-start(f32[4,2,32,128]{3,2,1,0:T(8,128)S(1)} %slice_add_fusion.2), channel_id=1, source_target_pairs={{0,4},{1,5},{2,6},{3,7},{4,0},{5,1},{6,2},{7,3},{8,12},{9,13},{10,... | collective-permute-start | bytes 393224 | tf_op jit(solution)/shard_map/ppermute | solution.py:338
  85.5 3.2 %collective-permute-done.10.refs_3_ = f32[4,2,32,128]{3,2,1,0:T(8,128)S(1)} collective-permute-done((f32[4,2,32,128]{3,2,1,0:T(8,128)S(1)}, f32[4,2,32,128]{3,2,1,0:T(8,128)S(1)}, u32[]{:S(2)}, u32[]{:S(2)}) %collective-permute-start.10) | collective-permute-done | bytes 131104 | tf_op jit(solution)/shard_map/ppermute | solution.py:338
  88.8 3.1 %collective-permute-start.11 = (f32[2,2,32,128]{3,2,1,0:T(8,128)S(1)}, f32[2,2,32,128]{3,2,1,0:T(8,128)S(1)}, u32[]{:S(2)}, u32[]{:S(2)}) collective-permute-start(f32[2,2,32,128]{3,2,1,0:T(8,128)S(1)} %slice_add_fusion.6), channel_id=1, source_target_pairs={{0,8},{1,9},{2,10},{3,11},{4,12},{5,13},{6,14},{7,15},{8,0},{9,1},... | collective-permute-start | bytes 196616 | tf_op jit(solution)/shard_map/ppermute | solution.py:338
  91.9 2.2 %collective-permute-done.11.refs_4_ = f32[2,2,32,128]{3,2,1,0:T(8,128)S(1)} collective-permute-done((f32[2,2,32,128]{3,2,1,0:T(8,128)S(1)}, f32[2,2,32,128]{3,2,1,0:T(8,128)S(1)}, u32[]{:S(2)}, u32[]{:S(2)}) %collective-permute-start.11) | collective-permute-done | bytes 65568 | tf_op jit(solution)/shard_map/ppermute | solution.py:338
  94.1 2.0 %adjoint.1 = (f32[2,2,32,128]{3,2,1,0:T(8,128)S(1)}, f32[2,2,32,128]{3,2,1,0:T(8,128)S(1)}) custom-call(f32[16,2,32,128]{3,2,1,0:T(8,128)S(1)} %get-tuple-element.18.refs_0_, f32[16,2,32,128]{3,2,1,0:T(8,128)S(1)} %collective-permute-done.8.refs_1_, f32[8,2,32,128]{3,2,1,0:T(8,128)S(1)} %collective-permute-done.9.refs_2_, ...), custom_call_target="tpu_custom_call" | custom-call | tf_op jit(solution)/shard_map/adjoint/pallas_call | solution.py:454
  96.2 3.0 %collective-permute-start.12 = (f32[2,2,32,128]{3,2,1,0:T(8,128)S(1)}, f32[2,2,32,128]{3,2,1,0:T(8,128)S(1)}, u32[]{:S(2)}, u32[]{:S(2)}) collective-permute-start(f32[2,2,32,128]{3,2,1,0:T(8,128)S(1)} %get-tuple-element.20), channel_id=1, source_target_pairs={{0,8},{1,9},{2,10},{3,11},{4,12},{5,13},{6,14},{7,15},{8,0},{9,1},... | collective-permute-start | bytes 196616 | tf_op jit(solution)/shard_map/ppermute | solution.py:338
  99.2 2.3 %collective-permute-done.12 = f32[2,2,32,128]{3,2,1,0:T(8,128)S(1)} collective-permute-done((f32[2,2,32,128]{3,2,1,0:T(8,128)S(1)}, f32[2,2,32,128]{3,2,1,0:T(8,128)S(1)}, u32[]{:S(2)}, u32[]{:S(2)}) %collective-permute-start.12) | collective-permute-done | bytes 65568 | tf_op jit(solution)/shard_map/ppermute | solution.py:338
  101.5 2.1 %collective-permute-start.13 = (f32[4,2,32,128]{3,2,1,0:T(8,128)S(1)}, f32[4,2,32,128]{3,2,1,0:T(8,128)S(1)}, u32[]{:S(2)}, u32[]{:S(2)}) collective-permute-start(f32[4,2,32,128]{3,2,1,0:T(8,128)S(1)} %pad_maximum_fusion.3), channel_id=1, source_target_pairs={{0,4},{1,5},{2,6},{3,7},{4,0},{5,1},{6,2},{7,3},{8,12},{9,13},{10,... | collective-permute-start | bytes 393224 | tf_op jit(solution)/shard_map/ppermute | solution.py:338
  103.6 2.9 %collective-permute-done.13 = f32[4,2,32,128]{3,2,1,0:T(8,128)S(1)} collective-permute-done((f32[4,2,32,128]{3,2,1,0:T(8,128)S(1)}, f32[4,2,32,128]{3,2,1,0:T(8,128)S(1)}, u32[]{:S(2)}, u32[]{:S(2)}) %collective-permute-start.13) | collective-permute-done | bytes 131104 | tf_op jit(solution)/shard_map/ppermute | solution.py:338
  106.6 1.6 %collective-permute-start.14 = (f32[8,2,32,128]{3,2,1,0:T(8,128)S(1)}, f32[8,2,32,128]{3,2,1,0:T(8,128)S(1)}, u32[]{:S(2)}, u32[]{:S(2)}) collective-permute-start(f32[8,2,32,128]{3,2,1,0:T(8,128)S(1)} %pad_maximum_fusion.1), channel_id=1, source_target_pairs={{0,2},{1,3},{2,0},{3,1},{4,6},{5,7},{6,4},{7,5},{8,10},{9,11},{10,... | collective-permute-start | bytes 786440 | tf_op jit(solution)/shard_map/ppermute | solution.py:338
  108.2 4.8 %collective-permute-done.14 = f32[8,2,32,128]{3,2,1,0:T(8,128)S(1)} collective-permute-done((f32[8,2,32,128]{3,2,1,0:T(8,128)S(1)}, f32[8,2,32,128]{3,2,1,0:T(8,128)S(1)}, u32[]{:S(2)}, u32[]{:S(2)}) %collective-permute-start.14) | collective-permute-done | bytes 262176 | tf_op jit(solution)/shard_map/ppermute | solution.py:338
  113.1 0.1 collective-permute-start.15
  113.1 0.1 concatenate.35.local_ref
  113.2 4.2 %weight_grad.1 = f32[2,32,64,128]{3,2,1,0:T(8,128)} custom-call(f32[2,2,32,128]{3,2,1,0:T(8,128)S(1)} %get-tuple-element.21.modes_ref, f32[2,2,32,128]{3,2,1,0:T(8,128)S(1)} %get-tuple-element.22.dmixed_ref), custom_call_target="tpu_custom_call" | custom-call | tf_op jit(solution)/shard_map/weight_grad/pallas_call | solution.py:481
  117.4 0.0 collective-permute-done.15.back_ref
  117.4 0.0 copy-done.2
  117.5 6.4 %input_grad.1 = f32[16,2,64,512]{3,2,1,0:T(8,128)} custom-call(f32[16,2,64,512]{3,2,1,0:T(8,128)S(1)} %copy-done.2, f32[16,2,32,128]{3,2,1,0:T(8,128)S(1)} %constant_dynamic-update-slice_fusion.4.front_ref, f32[16,2,32,128]{3,2,1,0:T(8,128)S(1)} %collective-permute-done.15.back_ref, f32[64,128]{1,0:T(8,128)S(1)} %concatenate.35.local_ref, ...), custom_call_target="tpu_custom_call" | custom-call | tf_op jit(solution)/shard_map/input_grad/pallas_call | solution.py:466
  (28 shorter events, 0.3 us)
Async XLA Ops:
  2.9 2.2 %copy-start = (f32[16,2,512,64]{2,3,1,0:T(8,128)S(1)}, f32[16,2,512,64]{2,3,1,0:T(8,128)}, u32[]{:S(2)}) copy-start(f32[16,2,512,64]{2,3,1,0:T(8,128)} %param.17) | copy-start | bytes 12582916
  5.1 0.9 copy-start.4
  6.0 26.5 %copy-start.1 = (f32[2,32,64,128]{3,2,1,0:T(8,128)S(1)}, f32[2,32,64,128]{3,2,1,0:T(8,128)}, u32[]{:S(2)}) copy-start(f32[2,32,64,128]{3,2,1,0:T(8,128)} %refs_5_.3) | copy-start | bytes 6291460
  10.4 43.1 %copy-start.12 = (s32[32,1]{0,1:T(1,128)S(1)}, s32[32,1]{0,1:T(1,128)}, u32[]{:S(2)}) copy-start(s32[32,1]{0,1:T(1,128)} %constant.78.clone) | copy-start | bytes 388
  10.4 43.6 %copy-start.7 = (f32[64,64]{1,0:T(8,128)S(1)}, f32[64,64]{1,0:T(8,128)}, u32[]{:S(2)}) copy-start(f32[64,64]{1,0:T(8,128)} %param.19) | copy-start | bytes 49156
  10.4 45.2 %copy-start.8 = (s32[1,256]{1,0:T(1,128)S(1)}, s32[1,256]{1,0:T(1,128)}, u32[]{:S(2)}) copy-start(s32[1,256]{1,0:T(1,128)} %constant.77.clone) | copy-start | bytes 3076
  10.5 45.2 %copy-start.9 = (s32[1,256]{1,0:T(1,128)S(1)}, s32[1,256]{1,0:T(1,128)}, u32[]{:S(2)}) copy-start(s32[1,256]{1,0:T(1,128)} %constant.76.clone) | copy-start | bytes 3076
  10.5 45.2 %copy-start.11 = (pred[32]{0:T(512)(128)(4,1)S(1)}, pred[32]{0:T(512)(128)(4,1)}, u32[]{:S(2)}) copy-start(pred[32]{0:T(512)(128)(4,1)} %constant.86) | copy-start | bytes 100
  10.5 46.0 %copy-start.10 = (f32[64]{0:T(128)S(1)}, f32[64]{0:T(128)}, u32[]{:S(2)}) copy-start(f32[64]{0:T(128)} %param.20) | copy-start | bytes 772
  10.5 46.1 %copy-start.3 = (bf16[512,256]{1,0:T(8,128)(2,1)S(1)}, bf16[512,256]{1,0:T(8,128)(2,1)}, u32[]{:S(2)}) copy-start(bf16[512,256]{1,0:T(8,128)(2,1)} %constant.69.clone.table_ref) | copy-start | bytes 786436
  10.5 2.1 %collective-permute-start = (f32[16,2,32,128]{3,2,1,0:T(8,128)S(1)}, f32[16,2,32,128]{3,2,1,0:T(8,128)S(1)}, u32[]{:S(2)}, u32[]{:S(2)}) collective-permute-start(f32[16,2,32,128]{3,2,1,0:T(8,128)S(1)} %get-tuple-element.14), channel_id=1, source_target_pairs={{0,1},{1,0},{2,3},{3,2},{4,5},{5,4},{6,7},{7,6},{8,9},{9,8},{10,11... | collective-permute-start | bytes 1572872 | tf_op jit(solution)/shard_map/ppermute | solution.py:338
  12.6 9.6 %collective-permute-start.1 = (f32[8,2,32,128]{3,2,1,0:T(8,128)S(1)}, f32[8,2,32,128]{3,2,1,0:T(8,128)S(1)}, u32[]{:S(2)}, u32[]{:S(2)}) collective-permute-start(f32[8,2,32,128]{3,2,1,0:T(8,128)S(1)} %slice_add_fusion.1), channel_id=1, source_target_pairs={{0,2},{1,3},{2,0},{3,1},{4,6},{5,7},{6,4},{7,5},{8,10},{9,11},{10,... | collective-permute-start | bytes 786440 | tf_op jit(solution)/shard_map/ppermute | solution.py:338
  22.2 5.1 %collective-permute-start.2 = (f32[4,2,32,128]{3,2,1,0:T(8,128)S(1)}, f32[4,2,32,128]{3,2,1,0:T(8,128)S(1)}, u32[]{:S(2)}, u32[]{:S(2)}) collective-permute-start(f32[4,2,32,128]{3,2,1,0:T(8,128)S(1)} %slice_add_fusion.4), channel_id=1, source_target_pairs={{0,4},{1,5},{2,6},{3,7},{4,0},{5,1},{6,2},{7,3},{8,12},{9,13},{10,... | collective-permute-start | bytes 393224 | tf_op jit(solution)/shard_map/ppermute | solution.py:338
  27.3 5.2 %collective-permute-start.3 = (f32[2,2,32,128]{3,2,1,0:T(8,128)S(1)}, f32[2,2,32,128]{3,2,1,0:T(8,128)S(1)}, u32[]{:S(2)}, u32[]{:S(2)}) collective-permute-start(f32[2,2,32,128]{3,2,1,0:T(8,128)S(1)} %slice_add_fusion.9), channel_id=1, source_target_pairs={{0,8},{1,9},{2,10},{3,11},{4,12},{5,13},{6,14},{7,15},{8,0},{9,1},... | collective-permute-start | bytes 196616 | tf_op jit(solution)/shard_map/ppermute | solution.py:338
  36.4 5.3 %collective-permute-start.4 = (f32[2,2,32,128]{3,2,1,0:T(8,128)S(1)}, f32[2,2,32,128]{3,2,1,0:T(8,128)S(1)}, u32[]{:S(2)}, u32[]{:S(2)}) collective-permute-start(f32[2,2,32,128]{3,2,1,0:T(8,128)S(1)} %get-tuple-element.15), channel_id=1, source_target_pairs={{0,8},{1,9},{2,10},{3,11},{4,12},{5,13},{6,14},{7,15},{8,0},{9,1},... | collective-permute-start | bytes 196616 | tf_op jit(solution)/shard_map/ppermute | solution.py:338
  41.8 5.2 %collective-permute-start.5 = (f32[4,2,32,128]{3,2,1,0:T(8,128)S(1)}, f32[4,2,32,128]{3,2,1,0:T(8,128)S(1)}, u32[]{:S(2)}, u32[]{:S(2)}) collective-permute-start(f32[4,2,32,128]{3,2,1,0:T(8,128)S(1)} %pad_maximum_fusion.2), channel_id=1, source_target_pairs={{0,4},{1,5},{2,6},{3,7},{4,0},{5,1},{6,2},{7,3},{8,12},{9,13},{10,... | collective-permute-start | bytes 393224 | tf_op jit(solution)/shard_map/ppermute | solution.py:338
  47.0 6.4 %collective-permute-start.6 = (f32[8,2,32,128]{3,2,1,0:T(8,128)S(1)}, f32[8,2,32,128]{3,2,1,0:T(8,128)S(1)}, u32[]{:S(2)}, u32[]{:S(2)}) collective-permute-start(f32[8,2,32,128]{3,2,1,0:T(8,128)S(1)} %pad_maximum_fusion), channel_id=1, source_target_pairs={{0,2},{1,3},{2,0},{3,1},{4,6},{5,7},{6,4},{7,5},{8,10},{9,11},{10,... | collective-permute-start | bytes 786440 | tf_op jit(solution)/shard_map/ppermute | solution.py:338
  53.5 3.0 %collective-permute-start.7 = (f32[16,2,32,128]{3,2,1,0:T(8,128)S(1)}, f32[16,2,32,128]{3,2,1,0:T(8,128)S(1)}, u32[]{:S(2)}, u32[]{:S(2)}) collective-permute-start(f32[16,2,32,128]{3,2,1,0:T(8,128)S(1)} %constant_dynamic-update-slice_fusion.front_ref), channel_id=1, source_target_pairs={{0,1},{1,0},{2,3},{3,2},{4,5},{5,4},{6,7},{7,6},{8,9},{9,8},{10,11... | collective-permute-start | bytes 1572872 | tf_op jit(solution)/shard_map/ppermute | solution.py:338
  56.6 0.9 copy-start.6
  72.7 2.0 %collective-permute-start.8 = (f32[16,2,32,128]{3,2,1,0:T(8,128)S(1)}, f32[16,2,32,128]{3,2,1,0:T(8,128)S(1)}, u32[]{:S(2)}, u32[]{:S(2)}) collective-permute-start(f32[16,2,32,128]{3,2,1,0:T(8,128)S(1)} %get-tuple-element.19), channel_id=1, source_target_pairs={{0,1},{1,0},{2,3},{3,2},{4,5},{5,4},{6,7},{7,6},{8,9},{9,8},{10,11... | collective-permute-start | bytes 1572872 | tf_op jit(solution)/shard_map/ppermute | solution.py:338
  74.8 42.7 %copy-start.2 = (f32[16,2,64,512]{3,2,1,0:T(8,128)S(1)}, f32[16,2,64,512]{3,2,1,0:T(8,128)}, u32[]{:S(2)}) copy-start(f32[16,2,64,512]{3,2,1,0:T(8,128)} %get-tuple-element.17.dpre_ref) | copy-start | bytes 12582916
  74.8 42.7 %copy-start.5 = (bf16[128,512]{1,0:T(8,128)(2,1)S(1)}, bf16[128,512]{1,0:T(8,128)(2,1)}, u32[]{:S(2)}) copy-start(bf16[128,512]{1,0:T(8,128)(2,1)} %constant.70.clone.synth_ref) | copy-start | bytes 393220
  74.8 8.7 %collective-permute-start.9 = (f32[8,2,32,128]{3,2,1,0:T(8,128)S(1)}, f32[8,2,32,128]{3,2,1,0:T(8,128)S(1)}, u32[]{:S(2)}, u32[]{:S(2)}) collective-permute-start(f32[8,2,32,128]{3,2,1,0:T(8,128)S(1)} %slice_add_fusion), channel_id=1, source_target_pairs={{0,2},{1,3},{2,0},{3,1},{4,6},{5,7},{6,4},{7,5},{8,10},{9,11},{10,... | collective-permute-start | bytes 786440 | tf_op jit(solution)/shard_map/ppermute | solution.py:338
  83.5 5.3 %collective-permute-start.10 = (f32[4,2,32,128]{3,2,1,0:T(8,128)S(1)}, f32[4,2,32,128]{3,2,1,0:T(8,128)S(1)}, u32[]{:S(2)}, u32[]{:S(2)}) collective-permute-start(f32[4,2,32,128]{3,2,1,0:T(8,128)S(1)} %slice_add_fusion.2), channel_id=1, source_target_pairs={{0,4},{1,5},{2,6},{3,7},{4,0},{5,1},{6,2},{7,3},{8,12},{9,13},{10,... | collective-permute-start | bytes 393224 | tf_op jit(solution)/shard_map/ppermute | solution.py:338
  88.8 5.4 %collective-permute-start.11 = (f32[2,2,32,128]{3,2,1,0:T(8,128)S(1)}, f32[2,2,32,128]{3,2,1,0:T(8,128)S(1)}, u32[]{:S(2)}, u32[]{:S(2)}) collective-permute-start(f32[2,2,32,128]{3,2,1,0:T(8,128)S(1)} %slice_add_fusion.6), channel_id=1, source_target_pairs={{0,8},{1,9},{2,10},{3,11},{4,12},{5,13},{6,14},{7,15},{8,0},{9,1},... | collective-permute-start | bytes 196616 | tf_op jit(solution)/shard_map/ppermute | solution.py:338
  96.2 5.4 %collective-permute-start.12 = (f32[2,2,32,128]{3,2,1,0:T(8,128)S(1)}, f32[2,2,32,128]{3,2,1,0:T(8,128)S(1)}, u32[]{:S(2)}, u32[]{:S(2)}) collective-permute-start(f32[2,2,32,128]{3,2,1,0:T(8,128)S(1)} %get-tuple-element.20), channel_id=1, source_target_pairs={{0,8},{1,9},{2,10},{3,11},{4,12},{5,13},{6,14},{7,15},{8,0},{9,1},... | collective-permute-start | bytes 196616 | tf_op jit(solution)/shard_map/ppermute | solution.py:338
  101.5 5.1 %collective-permute-start.13 = (f32[4,2,32,128]{3,2,1,0:T(8,128)S(1)}, f32[4,2,32,128]{3,2,1,0:T(8,128)S(1)}, u32[]{:S(2)}, u32[]{:S(2)}) collective-permute-start(f32[4,2,32,128]{3,2,1,0:T(8,128)S(1)} %pad_maximum_fusion.3), channel_id=1, source_target_pairs={{0,4},{1,5},{2,6},{3,7},{4,0},{5,1},{6,2},{7,3},{8,12},{9,13},{10,... | collective-permute-start | bytes 393224 | tf_op jit(solution)/shard_map/ppermute | solution.py:338
  106.6 6.4 %collective-permute-start.14 = (f32[8,2,32,128]{3,2,1,0:T(8,128)S(1)}, f32[8,2,32,128]{3,2,1,0:T(8,128)S(1)}, u32[]{:S(2)}, u32[]{:S(2)}) collective-permute-start(f32[8,2,32,128]{3,2,1,0:T(8,128)S(1)} %pad_maximum_fusion.1), channel_id=1, source_target_pairs={{0,2},{1,3},{2,0},{3,1},{4,6},{5,7},{6,4},{7,5},{8,10},{9,11},{10,... | collective-permute-start | bytes 786440 | tf_op jit(solution)/shard_map/ppermute | solution.py:338
  113.1 4.4 %collective-permute-start.15 = (f32[16,2,32,128]{3,2,1,0:T(8,128)S(1)}, f32[16,2,32,128]{3,2,1,0:T(8,128)S(1)}, u32[]{:S(2)}, u32[]{:S(2)}) collective-permute-start(f32[16,2,32,128]{3,2,1,0:T(8,128)S(1)} %constant_dynamic-update-slice_fusion.4.front_ref), channel_id=1, source_target_pairs={{0,1},{1,0},{2,3},{3,2},{4,5},{5,4},{6,7},{7,6},{8,9},{9,8},{10,11... | collective-permute-start | bytes 1572872 | tf_op jit(solution)/shard_map/ppermute | solution.py:338

commit v2 on v1

v2 whole, which is shorter than its diff:
```python
import functools
import math

import jax
import jax.numpy as jnp
import numpy as np
from jax import lax
from jax.experimental import pallas as pl
from jax.experimental.pallas import tpu as pltpu
from jax.sharding import PartitionSpec as P

F32 = jnp.float32
BF16 = jnp.bfloat16
LANES = 128
SUB = 8
VMEM_LIMIT = 16 << 20


def split_np(values):
    values = values.astype(np.float32)
    high = values.astype(BF16)
    low = (values - high.astype(np.float32)).astype(BF16)
    return high, low


def span_tables(length, modes, scale):
    angle = 2.0 * np.pi * (np.outer(np.arange(length), np.arange(modes)) % length) / length
    forward = np.concatenate([np.cos(angle), -np.sin(angle)], axis=1)
    factor = np.where(np.arange(modes) == 0, 1.0, 2.0) / scale
    backward = forward * np.concatenate([factor, factor])[None, :]

    def analysis(table):
        flipped = np.concatenate([table[:, modes:], -table[:, :modes]], axis=1)
        both = np.concatenate([table, flipped], axis=1)
        return np.concatenate(split_np(both), axis=1)

    def synthesis(table):
        high, low = split_np(table.T)
        return np.concatenate([high, low, high, np.zeros_like(high)], axis=0)

    return analysis(forward), analysis(backward), synthesis(forward), synthesis(backward)


def stage_masks():
    count = lax.axis_size("stream")
    bits = count.bit_length() - 1
    assert 1 << bits == count
    return [1] + [1 << i | 1 for i in range(1, bits)]


def stage_class(index):
    return (index ^ index >> 1 ^ index >> 2) & 1


def stage_mask(index, step):
    masks = stage_masks()
    if len(masks) > 2 and step in (1, 2) and stage_class(index):
        step = 3 - step
    return masks[step]


def mode_angles(position, inner, cell, owned, total_modes, cells):
    me = lax.axis_index("stream")
    masks = stage_masks()
    steps = len(masks)
    length = cells * (1 << steps)
    assert length & (length - 1) == 0
    bits = [position >> (steps - 1 - step) & 1 for step in range(steps)]
    if steps > 2:
        other = (bits[0] ^ stage_class(me)) & 1
        bits[1], bits[2] = (
            jnp.where(other == 1, bits[2], bits[1]),
            jnp.where(other == 1, bits[1], bits[2]),
        )
    block = jnp.zeros_like(position) + me
    for bit, mask in zip(bits, masks):
        block = block ^ bit * mask
    rows = block * owned + inner
    wave = jnp.where(rows < total_modes // 2, rows, rows - total_modes)
    phase = wave * (me * cells + cell) & (length - 1)
    phase = jnp.where(phase > length // 2, phase - length, phase)
    return phase.astype(F32) * (2.0 * math.pi / length)


def split(values):
    high = values.astype(BF16)
    return high, (values - high.astype(F32)).astype(BF16)


def dot(left, right):
    return jnp.dot(left, right, preferred_element_type=F32)


def make_tables(down_ref, back_ref, owned, total_modes, cells):
    def iota(shape, axis):
        return lax.broadcasted_iota(jnp.int32, shape, axis)

    def expand(table, ref):
        rows, lanes = table.shape
        full = jnp.broadcast_to(table[:, None, :], (rows, SUB, lanes)).reshape(rows * SUB, lanes)
        same = (iota(full.shape, 0) & (SUB - 1)) == (iota(full.shape, 1) & (SUB - 1))
        high, low = split(jnp.where(same, full, 0.0))
        ref[0] = high
        ref[1] = low

    def table(shape, mode_axis):
        mode = iota(shape, mode_axis)
        cell = iota(shape, 1 - mode_axis)
        if mode_axis == 1:
            mode = mode >> 3
        else:
            cell = cell >> 3
        shift = owned.bit_length() - 1
        angles = mode_angles(
            mode >> shift, mode & (owned - 1), cell & (cells - 1), owned, total_modes, cells
        )
        return jnp.where(cell < cells, jnp.cos(angles), jnp.sin(angles))

    expand(table((total_modes, 2 * cells * SUB), 0), down_ref)
    expand(table((2 * cells, total_modes * SUB), 1), back_ref)


def analyse(values_high, values_low, table_ref, at, coef_ref):
    full = dot(values_high, table_ref[...])
    full = full[:, :LANES] + full[:, LANES:] + dot(values_low, table_ref[:, :LANES])
    cells = coef_ref.shape[1] // (2 * SUB)
    half = 4 * SUB
    low_lane = lax.broadcasted_iota(jnp.int32, (half, LANES), 1) < LANES // 2
    for i in range(full.shape[0] // (2 * half)):
        low = full[2 * half * i : 2 * half * i + half]
        high = full[2 * half * i + half : 2 * half * (i + 1)]
        plain = jnp.where(low_lane, low, pltpu.roll(high, LANES // 2, 1))
        flipped = jnp.where(low_lane, pltpu.roll(low, LANES // 2, 1), high)
        for block in range(half // SUB):
            rows = slice(SUB * block, SUB * (block + 1))
            coef_ref[block, pl.ds(pl.multiple_of((at + i) * SUB, SUB), SUB)] = plain[rows]
            coef_ref[block, pl.ds(pl.multiple_of((cells + at + i) * SUB, SUB), SUB)] = flipped[rows]


def to_modes(coef_ref, table_ref, keep_ref, send_ref):
    modes = 2 * keep_ref.shape[0]
    for block in range(coef_ref.shape[0]):
        high, low = split(coef_ref[block])
        full = dot(table_ref[0], jnp.concatenate([high, low], axis=1))
        full = full[:, :LANES] + full[:, LANES:] + dot(table_ref[1], high)
        full = full.reshape(modes, SUB, LANES)
        rows = slice(SUB * block, SUB * (block + 1))
        keep_ref[:, 0, rows] = full[: modes // 2]
        send_ref[:, 0, rows] = full[modes // 2 :]


def from_modes(front_ref, back_ref, table_ref, lhs_ref):
    modes = 2 * front_ref.shape[0]
    cells, channels = lhs_ref.shape[:2]
    half = channels // 2
    lane = lax.broadcasted_iota(jnp.int32, (cells * SUB, LANES), 1)
    real = lane % (LANES // 2) < LANES // 4
    low_lane = lane < LANES // 2
    for block in range(half // SUB):
        rows = slice(SUB * block, SUB * (block + 1))
        values = jnp.concatenate([front_ref[:, 0, rows], back_ref[:, 0, rows]], axis=0)
        high, low = split(values.reshape(modes * SUB, LANES))
        full = dot(table_ref[0], jnp.concatenate([high, low], axis=1))
        full = full[:, :LANES] + full[:, LANES:] + dot(table_ref[1], high)
        plain, other = full[: cells * SUB], full[cells * SUB :]
        turned = jnp.where(
            real, -pltpu.roll(other, 3 * LANES // 4, 1), pltpu.roll(other, LANES // 4, 1)
        )
        inv = plain + turned
        swapped = pltpu.roll(inv, LANES // 2, 1)
        for at, doubled in (
            (0, jnp.where(low_lane, inv, swapped)),
            (half, jnp.where(low_lane, swapped, inv)),
        ):
            lhs_ref[:, at + SUB * block : at + SUB * (block + 1)] = doubled.reshape(
                cells, SUB, LANES
            )


def synthesise(lhs_ref, first, count, table_ref):
    values = lhs_ref[pl.ds(first, count)]
    high, low = split(values.reshape(-1, LANES))
    return dot(jnp.concatenate([high, low], axis=1), table_ref[...])


TAIL = (
    0.11650589762013625,
    0.06758867364360233,
    0.2686846227283619,
    -0.23671861048677273,
    0.38970758618179535,
    -0.10576817864886755,
)


def normal_parts(values):
    bell = jnp.exp(-0.5 * values * values)
    inner = 1.0 / (1.0 + 0.28 * jnp.abs(values))
    tail = TAIL[-1] * inner
    for factor in TAIL[-2::-1]:
        tail = (tail + factor) * inner
    tail = tail * bell
    return jnp.where(values >= 0.0, 1.0 - tail, tail), bell * (1.0 / math.sqrt(2.0 * math.pi))


def transpose_out(rows):
    parts = []
    for half in range(2):
        for part in range(2):
            shift = part * (LANES // 2) + half * (LANES // 4)
            parts.append(pltpu.roll(rows, LANES - shift, 1) if shift else rows)
    return jnp.concatenate(parts, axis=0).T[: LANES // 4]


def transpose_in(values):
    quarter = LANES // 4
    turned = jnp.concatenate([values] * 4, axis=0).T
    lane = lax.broadcasted_iota(jnp.int32, (quarter, LANES), 1) // quarter
    result = turned[:quarter]
    for half in range(2):
        for part in range(2):
            rows = turned[quarter * (2 * half + part) : quarter * (2 * half + part + 1)]
            result = jnp.where(lane == 2 * part + half, rows, result)
    return result


def turn_down(rows):
    lane = lax.broadcasted_iota(jnp.int32, rows.shape, 1) < LANES // 2
    rolled = pltpu.roll(rows, LANES // 2, 1)
    return jnp.where(lane, rolled, -rolled)


def spanwise_kernel(sizes, x_ref, table_ref, keep_ref, send_ref, down_ref, back_ref, coef_ref):
    step = pl.program_id(1)
    cells, _, channels, span = x_ref.shape

    @pl.when((step == 0) & (pl.program_id(0) == 0))
    def _():
        make_tables(down_ref, back_ref, *sizes)

    high, low = split(x_ref[...].reshape(cells * channels, span))
    analyse(high, low, table_ref, step * cells, coef_ref)

    @pl.when(step == pl.num_programs(1) - 1)
    def _():
        to_modes(coef_ref, down_ref, keep_ref, send_ref)


def pointwise_kernel(transposed, values_ref, local_ref, bias_ref, out_ref):
    weight = local_ref[...]
    channels = weight.shape[0]
    if transposed:
        weight = weight.T
    high, low = split(weight)
    lhs = jnp.concatenate([high, high, low], axis=1)
    if bias_ref is not None:
        row = jnp.broadcast_to(bias_ref[...], (channels, channels))
        column = row.T[:, :1]
    for cell in range(values_ref.shape[0]):
        high, low = split(values_ref[cell, 0])
        full = dot(lhs, jnp.concatenate([high, low, high], axis=0))
        out_ref[cell, 0] = full if bias_ref is None else full + column


def mix_kernel(*refs):
    *piece_refs, w_ref, modes_ref, mixed_ref, first_scr, second_scr = refs
    planes = modes_ref.shape[1]
    kz_count = w_ref.shape[1]
    quarter = LANES // 4
    for plane in range(planes):
        total = piece_refs[0][0, plane]
        for ref in piece_refs[1:]:
            total = total + ref[0, plane]
        modes_ref[0, plane] = total
        for kz in range(kz_count):
            sums = [None, None]
            for half in range(2):
                weight = w_ref[0, kz, quarter * half : quarter * (half + 1)]
                for part in range(2):
                    at = half * (LANES // 2) + part * quarter + kz
                    term = total[:, at : at + 1] * weight
                    sums[part] = term if sums[part] is None else sums[part] + term
            first_scr[kz : kz + 1] = jnp.sum(sums[0], axis=0, keepdims=True)
            second_scr[kz : kz + 1] = jnp.sum(sums[1], axis=0, keepdims=True)
        rows = first_scr[...] - turn_down(second_scr[...])
        mixed_ref[0, plane] = transpose_out(rows)


def middle_kernel(
    local_ref, up_ref, front_ref, back_ref, synth_ref, table_ref, down_ref, back_table_ref, *rest
):
    act_ref, dpre_ref, keep_ref, send_ref, lhs_ref, coef_ref = rest[-6:]
    step = pl.program_id(1)
    cells, _, channels, span = up_ref.shape

    @pl.when(step == 0)
    def _():
        from_modes(front_ref, back_ref, back_table_ref, lhs_ref)

    spectral = synthesise(lhs_ref, step * cells, cells, synth_ref)
    pre = spectral.reshape(cells, channels, span) + local_ref[:, 0]
    cumulative, density = normal_parts(pre)
    act_ref[:, 0] = pre * cumulative
    dpre = up_ref[:, 0] * (cumulative + pre * density)
    dpre_ref[:, 0] = dpre
    high, low = split(dpre.reshape(cells * channels, span))
    analyse(high, low, table_ref, step * cells, coef_ref)

    @pl.when(step == pl.num_programs(1) - 1)
    def _():
        to_modes(coef_ref, down_ref, keep_ref, send_ref)


def adjoint_kernel(*refs):
    *piece_refs, w_ref, dmixed_ref, dmodes_ref = refs
    planes = dmixed_ref.shape[1]
    kz_count, channels, width = w_ref.shape[1:]
    quarter = LANES // 4
    weight = w_ref[0].reshape(kz_count * channels, width)
    w_high, w_low = split(weight)
    lane = lax.broadcasted_iota(jnp.int32, (channels, LANES // 2), 1) % quarter
    for plane in range(planes):
        total = piece_refs[0][0, plane]
        for ref in piece_refs[1:]:
            total = total + ref[0, plane]
        dmixed_ref[0, plane] = total
        rows = transpose_in(total)
        both = jnp.concatenate([rows, turn_down(rows)], axis=0)
        high, low = split(both)
        right = jnp.concatenate([high, low], axis=0).T
        full = dot(w_high, right)
        full = full[:, : LANES // 2] + full[:, LANES // 2 :] + dot(w_low, right[:, : LANES // 2])
        full = full.reshape(kz_count, channels, LANES // 2)
        result = jnp.zeros((channels, LANES // 2), F32)
        for kz in range(kz_count):
            result = jnp.where(lane == kz, full[kz], result)
        dmodes_ref[0, plane] = jnp.concatenate(
            [result[: channels // 2], result[channels // 2 :]], axis=1
        )


def weight_grad_kernel(modes_ref, dmixed_ref, grad_ref, rows_scr):
    planes = modes_ref.shape[1]
    kz_count = grad_ref.shape[1]
    quarter = LANES // 4
    for plane in range(planes):
        rows = transpose_in(dmixed_ref[0, plane])
        rows_scr[2 * plane] = rows
        rows_scr[2 * plane + 1] = turn_down(rows)
    for kz in range(kz_count):
        for half in range(2):
            total = None
            for plane in range(planes):
                for part in range(2):
                    at = half * (LANES // 2) + part * quarter + kz
                    column = modes_ref[0, plane, :, at : at + 1]
                    term = column * rows_scr[2 * plane + part, kz : kz + 1]
                    total = term if total is None else total + term
            grad_ref[0, kz, quarter * half : quarter * (half + 1)] = total


def input_grad_kernel(local_ref, front_ref, back_ref, synth_ref, back_table_ref, *rest):
    out_ref, lhs_ref = rest[-2:]
    step = pl.program_id(1)
    cells, _, channels, span = local_ref.shape

    @pl.when(step == 0)
    def _():
        from_modes(front_ref, back_ref, back_table_ref, lhs_ref)

    spectral = synthesise(lhs_ref, step * cells, cells, synth_ref)
    out_ref[:, 0] = spectral.reshape(cells, channels, span) + local_ref[:, 0]


def swap(values, step):
    count = lax.axis_size("stream")
    return lax.ppermute(values, "stream", [(i, i ^ stage_mask(i, step)) for i in range(count)])


def beside(first, second):
    return lax.optimization_barrier((first, second))


def scatter_sum(keep, send, work):
    pieces = [keep, swap(send, 0)]
    half = keep.shape[0]
    done = None
    for step in range(1, len(stage_masks())):
        half //= 2
        part = pieces[0][half : 2 * half]
        for piece in pieces[1:]:
            part = part + piece[half : 2 * half]
        moved = swap(part, step)
        if step == 1:
            moved, done = beside(moved, work())
        pieces.append(moved)
    return pieces, done


def gather_all(values, work=None):
    done = None
    for step in reversed(range(1, len(stage_masks()))):
        moved = swap(values, step)
        if step == 1 and work is not None:
            moved, done = beside(moved, work())
        values = jnp.concatenate([values, moved], axis=0)
    return values, swap(values, 0), done


def params():
    return pltpu.CompilerParams(vmem_limit_bytes=VMEM_LIMIT)


def whole(array):
    rank = len(array.shape)
    return pl.BlockSpec(array.shape, lambda *_: (0,) * rank)


def per_device(snapshot, mode_weight, local_weight, offset_bias, upstream):
    cells, planes, span, channels = snapshot.shape
    owned, kz_count = mode_weight.shape[:2]
    total_modes = owned * lax.axis_size("stream")
    half_modes = total_modes // 2
    half_channels = channels // 2
    shape = jax.ShapeDtypeStruct
    x = jnp.swapaxes(snapshot, 2, 3)
    up = jnp.swapaxes(upstream, 2, 3)
    scale = float(cells * lax.axis_size("stream") * span)
    ana_fwd, ana_inv, syn_fwd, syn_inv = map(jnp.asarray, span_tables(span, kz_count, scale))
    step_cells = 4
    grid = (planes, cells // step_cells)
    coef_scr = pltpu.VMEM((half_channels // SUB, 2 * cells * SUB, LANES), F32)
    lhs_scr = pltpu.VMEM((cells, channels, LANES), F32)
    down = shape((2, total_modes * SUB, 2 * cells * SUB), BF16)
    back = shape((2, 2 * cells * SUB, total_modes * SUB), BF16)
    grid_block = pl.BlockSpec((step_cells, 1, channels, span), lambda p, s: (s, p, 0, 0))
    half_block = pl.BlockSpec((half_modes, 1, half_channels, LANES), lambda p, s: (0, p, 0, 0))
    own_block = pl.BlockSpec((1, planes, half_channels, LANES), lambda j: (j, 0, 0, 0))
    weight_block = pl.BlockSpec((1, kz_count, channels, 2 * channels), lambda j: (j, 0, 0, 0))
    own_shape = shape((owned, planes, half_channels, LANES), F32)
    half_shape = shape((half_modes, planes, half_channels, LANES), F32)
    grid_shape = shape(x.shape, F32)

    keep, send, down, back = pl.pallas_call(
        functools.partial(spanwise_kernel, (owned, total_modes, cells)),
        grid=grid,
        in_specs=[grid_block, whole(ana_fwd)],
        out_specs=[half_block, half_block, whole(down), whole(back)],
        out_shape=[half_shape, half_shape, down, back],
        scratch_shapes=[coef_scr],
        compiler_params=params(),
        name="spanwise",
    )(x, ana_fwd)

    def local_forward():
        return pl.pallas_call(
            functools.partial(pointwise_kernel, True),
            grid=grid,
            in_specs=[grid_block, whole(local_weight), whole(offset_bias[None])],
            out_specs=grid_block,
            out_shape=grid_shape,
            compiler_params=params(),
            name="local_forward",
        )(x, local_weight, offset_bias[None])

    pieces, local = scatter_sum(keep, send, local_forward)
    modes, mixed = pl.pallas_call(
        mix_kernel,
        grid=(owned,),
        in_specs=[own_block] * len(pieces) + [weight_block],
        out_specs=[own_block] * 2,
        out_shape=[own_shape] * 2,
        scratch_shapes=[pltpu.VMEM((kz_count, LANES), F32)] * 2,
        compiler_params=params(),
        name="mix",
    )(*pieces, mode_weight)
    front, behind, _ = gather_all(mixed)
    act, dpre, keep, send = pl.pallas_call(
        middle_kernel,
        grid=grid,
        in_specs=[
            grid_block, grid_block, half_block, half_block,
            whole(syn_inv), whole(ana_inv), whole(down), whole(back),
        ],
        out_specs=[grid_block, grid_block, half_block, half_block],
        out_shape=[grid_shape, grid_shape, half_shape, half_shape],
        scratch_shapes=[lhs_scr, coef_scr],
        compiler_params=params(),
        name="middle",
    )(local, up, front, behind, syn_inv, ana_inv, down, back)

    def local_backward():
        return pl.pallas_call(
            lambda values, weight, out: pointwise_kernel(False, values, weight, None, out),
            grid=grid,
            in_specs=[grid_block, whole(local_weight)],
            out_specs=grid_block,
            out_shape=grid_shape,
            compiler_params=params(),
            name="local_backward",
        )(dpre, local_weight)

    pieces, local = scatter_sum(keep, send, local_backward)
    dmixed, dmodes = pl.pallas_call(
        adjoint_kernel,
        grid=(owned,),
        in_specs=[own_block] * len(pieces) + [weight_block],
        out_specs=[own_block] * 2,
        out_shape=[own_shape] * 2,
        compiler_params=params(),
        name="adjoint",
    )(*pieces, mode_weight)

    def weight_grad():
        return pl.pallas_call(
            weight_grad_kernel,
            grid=(owned,),
            in_specs=[own_block] * 2,
            out_specs=weight_block,
            out_shape=shape(mode_weight.shape, F32),
            scratch_shapes=[pltpu.VMEM((2 * planes, kz_count, LANES), F32)],
            compiler_params=params(),
            name="weight_grad",
        )(modes, dmixed)

    front, behind, grad_modes = gather_all(dmodes, weight_grad)
    grad_snapshot = pl.pallas_call(
        input_grad_kernel,
        grid=grid,
        in_specs=[grid_block, half_block, half_block, whole(syn_fwd), whole(back)],
        out_specs=grid_block,
        out_shape=grid_shape,
        scratch_shapes=[lhs_scr],
        compiler_params=params(),
        name="input_grad",
    )(local, front, behind, syn_fwd, back)
    return jnp.swapaxes(act, 2, 3), jnp.swapaxes(grad_snapshot, 2, 3), grad_modes


def solution(mesh):
    wide = P("stream", "group", None, None)
    return jax.shard_map(
        per_device,
        mesh=mesh,
        in_specs=(wide, P("stream", None, None, None), P(), P(), wide),
        out_specs=(wide, wide, wide),
        check_vma=False,
    )
```

time: 125 us -> 108 us (0.86)
  waiting for transfers between devices: 48.2 us -> 41.1 us
  starting transfers between devices: 29 us -> 23.6 us
  other arithmetic: 3.84 us -> 0.23 us
  Pallas kernels: 36 us -> 38.7 us
  local copies, waits for them, and re-layouts: 5.86 us -> 3.26 us
    ppermute x16, waiting for transfers between devices: 48.2 us -> 41.1 us  [swap(): lax.ppermute(values, 'stream', [(i, i ^ stage_mask(i, step)) for i in ran...]
    ppermute x16, starting transfers between devices: 29 us -> 23.6 us  [swap(): lax.ppermute(values, 'stream', [(i, i ^ stage_mask(i, step)) for i in ran...]
    pallas_call x6 -> x8, Pallas kernels: 36 us -> 38.7 us  [the longest x1 11.4 us: per_device(): pl.pallas_call(middle_kernel, grid=grid, in_specs=[grid_block, grid_block...]
    select_n x3 -> x0, other arithmetic: 1.74 us -> none  [the longest x1 0.87 us: stream_tables(): down = jnp.where(lane[None, :] < cells * SUB, jnp.cos(down), jnp.sin(down))]
    unnamed x33 -> x24, local copies, waits for them, and re-layouts: 4.84 us -> 3.22 us
  transfers between devices with their start and end apart: 16 -> 16, of which waited for: 14 -> 15; matrix products, arithmetic and copies ran while one was open for 2% -> 0% of each run, Pallas kernels for 3% -> 10%
where the time goes in v2:
time: 108 us
  waiting for transfers between devices  41.1 us (38%)
  Pallas kernels  38.7 us (36%)
  starting transfers between devices  23.6 us (22%)
  local copies, waits for them, and re-layouts  3.26 us (3%)
    ppermute x16, waiting for transfers between devices, swap(): lax.ppermute(values, 'stream', [(i, i ^ stage_mask(i, step)) for i in ran...  41.1 us
    ppermute x16, starting transfers between devices, swap(): lax.ppermute(values, 'stream', [(i, i ^ stage_mask(i, step)) for i in ran...  23.6 us
    pallas_call x1, Pallas kernels, per_device(): pl.pallas_call(middle_kernel, grid=grid, in_specs=[grid_block, grid_block...  11.4 us
    pallas_call x1, Pallas kernels, per_device(): pl.pallas_call(input_grad_kernel, grid=grid, in_specs=[grid_block, half_b...  5.78 us
    pallas_call x1, Pallas kernels, per_device(): pl.pallas_call(functools.partial(spanwise_kernel, (owned, total_modes, ce...  4.73 us
    pallas_call x1, Pallas kernels, weight_grad(): pl.pallas_call(weight_grad_kernel, grid=(owned,), in_specs=[own_block] *...  4.22 us
    pallas_call x1, Pallas kernels, per_device(): pl.pallas_call(mix_kernel, grid=(owned,), in_specs=[own_block] * len(piec...  3.89 us
    pallas_call x1, Pallas kernels, local_forward(): pl.pallas_call(functools.partial(pointwise_kernel, True), grid=grid, in_s...  3.63 us
  transfers between devices with their start and end apart: 16, of which 15 were waited for; matrix products, arithmetic and copies ran while one was open for 0% of the time, Pallas kernels for 10%

profile of v2, /device:TPU:0, one launch (start us, length us, event | category | flops | bytes accessed | tf_op | source)
XLA Modules:
  0.0 107.6 jit_solution(9316395762060514953)
XLA Ops:
  0.6 0.0 copy-start.8
  0.6 0.0 copy-start
  0.7 2.2 %copy-done = f32[16,2,512,64]{2,3,1,0:T(8,128)S(1)} copy-done((f32[16,2,512,64]{2,3,1,0:T(8,128)S(1)}, f32[16,2,512,64]{2,3,1,0:T(8,128)}, u32[]{:S(2)}) %copy-start) | copy-done | bytes 4194328
  2.8 0.0 copy-start.6
  2.8 0.9 copy-done.6
  3.8 0.0 copy-start.7
  3.8 4.7 %spanwise.1 = (f32[16,2,32,128]{3,2,1,0:T(8,128)S(1)}, f32[16,2,32,128]{3,2,1,0:T(8,128)S(1)}, bf16[2,256,256]{2,1,0:T(8,128)(2,1)S(1)}, bf16[2,256,256]{2,1,0:T(8,128)(2,1)S(1)}) custom-call(f32[16,2,64,512]{3,2,1,0:T(8,128)S(1)} %bitcast.5, bf16[512,256]{1,0:T(8,128)(2,1)S(1)} %copy-done.6), custom_call_target="tpu_custom_call" | custom-call | tf_op jit(solution)/shard_map/spanwise/pallas_call | solution.py:444
  8.5 0.5 collective-permute-start
  9.0 1.5 %collective-permute-done.refs_1_ = f32[16,2,32,128]{3,2,1,0:T(8,128)S(1)} collective-permute-done((f32[16,2,32,128]{3,2,1,0:T(8,128)S(1)}, f32[16,2,32,128]{3,2,1,0:T(8,128)S(1)}, u32[]{:S(2)}, u32[]{:S(2)}) %collective-permute-start) | collective-permute-done | bytes 524320 | tf_op jit(solution)/shard_map/ppermute | solution.py:377
  10.6 2.7 %collective-permute-start.1 = (f32[8,2,32,128]{3,2,1,0:T(8,128)S(1)}, f32[8,2,32,128]{3,2,1,0:T(8,128)S(1)}, u32[]{:S(2)}, u32[]{:S(2)}) collective-permute-start(f32[8,2,32,128]{3,2,1,0:T(8,128)S(1)} %slice_add_fusion.1), channel_id=1, source_target_pairs={{0,3},{1,4},{2,7},{3,0},{4,1},{5,6},{6,5},{7,2},{8,11},{9,12},{10,... | collective-permute-start | bytes 786440 | tf_op jit(solution)/shard_map/ppermute | solution.py:377
  13.3 0.0 copy-done.8
  13.3 0.0 copy-done.7
  13.3 0.0 copy-start.1
  13.3 3.6 %local_forward.1.local_ref = f32[16,2,64,512]{3,2,1,0:T(8,128)S(1)} custom-call(f32[16,2,64,512]{3,2,1,0:T(8,128)S(1)} %bitcast.6, f32[64,64]{1,0:T(8,128)S(1)} %copy-done.7, f32[1,64]{1,0:T(1,128)S(1)} %bitcast.8), custom_call_target="tpu_custom_call" | custom-call | tf_op jit(solution)/shard_map/local_forward/pallas_call | solution.py:456
  17.0 0.0 copy-start.2
  17.0 0.0 copy-start.4
  17.0 0.0 copy-start.5
  17.0 0.4 collective-permute-done.1.refs_2_
  17.4 1.9 %collective-permute-start.2 = (f32[4,2,32,128]{3,2,1,0:T(8,128)S(1)}, f32[4,2,32,128]{3,2,1,0:T(8,128)S(1)}, u32[]{:S(2)}, u32[]{:S(2)}) collective-permute-start(f32[4,2,32,128]{3,2,1,0:T(8,128)S(1)} %fusion.1), channel_id=1, source_target_pairs={{0,5},{1,2},{2,1},{3,6},{4,7},{5,0},{6,3},{7,4},{8,13},{9,10},{10,... | collective-permute-start | bytes 393224 | tf_op jit(solution)/shard_map/ppermute | solution.py:377
  19.3 2.7 %collective-permute-done.2.refs_3_ = f32[4,2,32,128]{3,2,1,0:T(8,128)S(1)} collective-permute-done((f32[4,2,32,128]{3,2,1,0:T(8,128)S(1)}, f32[4,2,32,128]{3,2,1,0:T(8,128)S(1)}, u32[]{:S(2)}, u32[]{:S(2)}) %collective-permute-start.2) | collective-permute-done | bytes 131104 | tf_op jit(solution)/shard_map/ppermute | solution.py:377
  22.0 2.8 %collective-permute-start.3 = (f32[2,2,32,128]{3,2,1,0:T(8,128)S(1)}, f32[2,2,32,128]{3,2,1,0:T(8,128)S(1)}, u32[]{:S(2)}, u32[]{:S(2)}) collective-permute-start(f32[2,2,32,128]{3,2,1,0:T(8,128)S(1)} %slice_add_fusion.6), channel_id=1, source_target_pairs={{0,9},{1,8},{2,11},{3,10},{4,13},{5,12},{6,15},{7,14},{8,1},{9,0},... | collective-permute-start | bytes 196616 | tf_op jit(solution)/shard_map/ppermute | solution.py:377
  24.8 2.2 %collective-permute-done.3.refs_4_ = f32[2,2,32,128]{3,2,1,0:T(8,128)S(1)} collective-permute-done((f32[2,2,32,128]{3,2,1,0:T(8,128)S(1)}, f32[2,2,32,128]{3,2,1,0:T(8,128)S(1)}, u32[]{:S(2)}, u32[]{:S(2)}) %collective-permute-start.3) | collective-permute-done | bytes 65568 | tf_op jit(solution)/shard_map/ppermute | solution.py:377
  26.9 0.0 copy-done.1
  26.9 3.9 %mix.1 = (f32[2,2,32,128]{3,2,1,0:T(8,128)S(1)}, f32[2,2,32,128]{3,2,1,0:T(8,128)S(1)}) custom-call(f32[16,2,32,128]{3,2,1,0:T(8,128)S(1)} %get-tuple-element.21.refs_0_, f32[16,2,32,128]{3,2,1,0:T(8,128)S(1)} %collective-permute-done.refs_1_, f32[8,2,32,128]{3,2,1,0:T(8,128)S(1)} %collective-permute-done.1.refs_2_, ...), custom_call_target="tpu_custom_call" | custom-call | tf_op jit(solution)/shard_map/mix/pallas_call | solution.py:467
  30.8 3.0 %collective-permute-start.4 = (f32[2,2,32,128]{3,2,1,0:T(8,128)S(1)}, f32[2,2,32,128]{3,2,1,0:T(8,128)S(1)}, u32[]{:S(2)}, u32[]{:S(2)}) collective-permute-start(f32[2,2,32,128]{3,2,1,0:T(8,128)S(1)} %get-tuple-element.25), channel_id=1, source_target_pairs={{0,9},{1,8},{2,11},{3,10},{4,13},{5,12},{6,15},{7,14},{8,1},{9,0},... | collective-permute-start | bytes 196616 | tf_op jit(solution)/shard_map/ppermute | solution.py:377
  33.8 2.2 %collective-permute-done.4 = f32[2,2,32,128]{3,2,1,0:T(8,128)S(1)} collective-permute-done((f32[2,2,32,128]{3,2,1,0:T(8,128)S(1)}, f32[2,2,32,128]{3,2,1,0:T(8,128)S(1)}, u32[]{:S(2)}, u32[]{:S(2)}) %collective-permute-start.4) | collective-permute-done | bytes 65568 | tf_op jit(solution)/shard_map/ppermute | solution.py:377
  36.0 3.0 %collective-permute-start.5 = (f32[4,2,32,128]{3,2,1,0:T(8,128)S(1)}, f32[4,2,32,128]{3,2,1,0:T(8,128)S(1)}, u32[]{:S(2)}, u32[]{:S(2)}) collective-permute-start(f32[4,2,32,128]{3,2,1,0:T(8,128)S(1)} %pad_maximum_fusion.2), channel_id=1, source_target_pairs={{0,5},{1,2},{2,1},{3,6},{4,7},{5,0},{6,3},{7,4},{8,13},{9,10},{10,... | collective-permute-start | bytes 393224 | tf_op jit(solution)/shard_map/ppermute | solution.py:377
  39.0 2.7 %collective-permute-done.5 = f32[4,2,32,128]{3,2,1,0:T(8,128)S(1)} collective-permute-done((f32[4,2,32,128]{3,2,1,0:T(8,128)S(1)}, f32[4,2,32,128]{3,2,1,0:T(8,128)S(1)}, u32[]{:S(2)}, u32[]{:S(2)}) %collective-permute-start.5) | collective-permute-done | bytes 131104 | tf_op jit(solution)/shard_map/ppermute | solution.py:377
  41.7 2.9 %collective-permute-start.6 = (f32[8,2,32,128]{3,2,1,0:T(8,128)S(1)}, f32[8,2,32,128]{3,2,1,0:T(8,128)S(1)}, u32[]{:S(2)}, u32[]{:S(2)}) collective-permute-start(f32[8,2,32,128]{3,2,1,0:T(8,128)S(1)} %pad_maximum_fusion), channel_id=1, source_target_pairs={{0,3},{1,4},{2,7},{3,0},{4,1},{5,6},{6,5},{7,2},{8,11},{9,12},{10,... | collective-permute-start | bytes 786440 | tf_op jit(solution)/shard_map/ppermute | solution.py:377
  44.6 4.0 %collective-permute-done.6 = f32[8,2,32,128]{3,2,1,0:T(8,128)S(1)} collective-permute-done((f32[8,2,32,128]{3,2,1,0:T(8,128)S(1)}, f32[8,2,32,128]{3,2,1,0:T(8,128)S(1)}, u32[]{:S(2)}, u32[]{:S(2)}) %collective-permute-start.6) | collective-permute-done | bytes 262176 | tf_op jit(solution)/shard_map/ppermute | solution.py:377
  48.7 0.1 collective-permute-start.7
  48.8 1.9 %collective-permute-done.7.back_ref = f32[16,2,32,128]{3,2,1,0:T(8,128)S(1)} collective-permute-done((f32[16,2,32,128]{3,2,1,0:T(8,128)S(1)}, f32[16,2,32,128]{3,2,1,0:T(8,128)S(1)}, u32[]{:S(2)}, u32[]{:S(2)}) %collective-permute-start.7) | collective-permute-done | bytes 524320 | tf_op jit(solution)/shard_map/ppermute | solution.py:377
  50.7 0.0 copy-done.2
  50.7 0.0 copy-done.4
  50.7 0.0 copy-done.5
  50.7 11.4 %middle.1 = (f32[16,2,64,512]{3,2,1,0:T(8,128)}, f32[16,2,64,512]{3,2,1,0:T(8,128)S(1)}, f32[16,2,32,128]{3,2,1,0:T(8,128)S(1)}, f32[16,2,32,128]{3,2,1,0:T(8,128)S(1)}) custom-call(f32[16,2,64,512]{3,2,1,0:T(8,128)S(1)} %local_forward.1.local_ref, f32[16,2,64,512]{3,2,1,0:T(8,128)S(1)} %bitcast.7, ...), custom_call_target="tpu_custom_call" | custom-call | tf_op jit(solution)/shard_map/middle/pallas_call | solution.py:478
  62.1 0.1 collective-permute-start.8
  62.2 1.8 %collective-permute-done.8.refs_1_ = f32[16,2,32,128]{3,2,1,0:T(8,128)S(1)} collective-permute-done((f32[16,2,32,128]{3,2,1,0:T(8,128)S(1)}, f32[16,2,32,128]{3,2,1,0:T(8,128)S(1)}, u32[]{:S(2)}, u32[]{:S(2)}) %collective-permute-start.8) | collective-permute-done | bytes 524320 | tf_op jit(solution)/shard_map/ppermute | solution.py:377
  64.1 1.8 %collective-permute-start.9 = (f32[8,2,32,128]{3,2,1,0:T(8,128)S(1)}, f32[8,2,32,128]{3,2,1,0:T(8,128)S(1)}, u32[]{:S(2)}, u32[]{:S(2)}) collective-permute-start(f32[8,2,32,128]{3,2,1,0:T(8,128)S(1)} %slice_add_fusion), channel_id=1, source_target_pairs={{0,3},{1,4},{2,7},{3,0},{4,1},{5,6},{6,5},{7,2},{8,11},{9,12},{10,... | collective-permute-start | bytes 786440 | tf_op jit(solution)/shard_map/ppermute | solution.py:377
  65.9 3.0 %local_backward.1.local_ref = f32[16,2,64,512]{3,2,1,0:T(8,128)S(1)} custom-call(f32[16,2,64,512]{3,2,1,0:T(8,128)S(1)} %get-tuple-element.31.values, f32[64,64]{1,0:T(8,128)S(1)} %copy-done.7), custom_call_target="tpu_custom_call" | custom-call | tf_op jit(solution)/shard_map/local_backward/pallas_call | solution.py:493
  68.8 0.0 copy-start.3
  68.9 1.1 collective-permute-done.9.refs_2_
  70.0 0.7 collective-permute-start.10
  70.7 3.8 %collective-permute-done.10.refs_3_ = f32[4,2,32,128]{3,2,1,0:T(8,128)S(1)} collective-permute-done((f32[4,2,32,128]{3,2,1,0:T(8,128)S(1)}, f32[4,2,32,128]{3,2,1,0:T(8,128)S(1)}, u32[]{:S(2)}, u32[]{:S(2)}) %collective-permute-start.10) | collective-permute-done | bytes 131104 | tf_op jit(solution)/shard_map/ppermute | solution.py:377
  74.4 1.9 %collective-permute-start.11 = (f32[2,2,32,128]{3,2,1,0:T(8,128)S(1)}, f32[2,2,32,128]{3,2,1,0:T(8,128)S(1)}, u32[]{:S(2)}, u32[]{:S(2)}) collective-permute-start(f32[2,2,32,128]{3,2,1,0:T(8,128)S(1)} %slice_add_fusion.4), channel_id=1, source_target_pairs={{0,9},{1,8},{2,11},{3,10},{4,13},{5,12},{6,15},{7,14},{8,1},{9,0},... | collective-permute-start | bytes 196616 | tf_op jit(solution)/shard_map/ppermute | solution.py:377
  76.3 4.6 %collective-permute-done.11.refs_4_ = f32[2,2,32,128]{3,2,1,0:T(8,128)S(1)} collective-permute-done((f32[2,2,32,128]{3,2,1,0:T(8,128)S(1)}, f32[2,2,32,128]{3,2,1,0:T(8,128)S(1)}, u32[]{:S(2)}, u32[]{:S(2)}) %collective-permute-start.11) | collective-permute-done | bytes 65568 | tf_op jit(solution)/shard_map/ppermute | solution.py:377
  80.9 2.0 %adjoint.1 = (f32[2,2,32,128]{3,2,1,0:T(8,128)S(1)}, f32[2,2,32,128]{3,2,1,0:T(8,128)S(1)}) custom-call(f32[16,2,32,128]{3,2,1,0:T(8,128)S(1)} %get-tuple-element.29.refs_0_, f32[16,2,32,128]{3,2,1,0:T(8,128)S(1)} %collective-permute-done.8.refs_1_, f32[8,2,32,128]{3,2,1,0:T(8,128)S(1)} %collective-permute-done.9.refs_2_, ...), custom_call_target="tpu_custom_call" | custom-call | tf_op jit(solution)/shard_map/adjoint/pallas_call | solution.py:504
  82.9 0.3 collective-permute-start.12
  83.2 6.2 %collective-permute-done.12 = f32[2,2,32,128]{3,2,1,0:T(8,128)S(1)} collective-permute-done((f32[2,2,32,128]{3,2,1,0:T(8,128)S(1)}, f32[2,2,32,128]{3,2,1,0:T(8,128)S(1)}, u32[]{:S(2)}, u32[]{:S(2)}) %collective-permute-start.12) | collective-permute-done | bytes 65568 | tf_op jit(solution)/shard_map/ppermute | solution.py:377
  89.5 0.1 collective-permute-start.13
  89.5 4.4 %collective-permute-done.13 = f32[4,2,32,128]{3,2,1,0:T(8,128)S(1)} collective-permute-done((f32[4,2,32,128]{3,2,1,0:T(8,128)S(1)}, f32[4,2,32,128]{3,2,1,0:T(8,128)S(1)}, u32[]{:S(2)}, u32[]{:S(2)}) %collective-permute-start.13) | collective-permute-done | bytes 131104 | tf_op jit(solution)/shard_map/ppermute | solution.py:377
  93.9 1.6 %collective-permute-start.14 = (f32[8,2,32,128]{3,2,1,0:T(8,128)S(1)}, f32[8,2,32,128]{3,2,1,0:T(8,128)S(1)}, u32[]{:S(2)}, u32[]{:S(2)}) collective-permute-start(f32[8,2,32,128]{3,2,1,0:T(8,128)S(1)} %pad_maximum_fusion.1), channel_id=1, source_target_pairs={{0,3},{1,4},{2,7},{3,0},{4,1},{5,6},{6,5},{7,2},{8,11},{9,12},{10,... | collective-permute-start | bytes 786440 | tf_op jit(solution)/shard_map/ppermute | solution.py:377
  95.5 4.2 %weight_grad.1 = f32[2,32,64,128]{3,2,1,0:T(8,128)} custom-call(f32[2,2,32,128]{3,2,1,0:T(8,128)S(1)} %get-tuple-element.35.modes_ref, f32[2,2,32,128]{3,2,1,0:T(8,128)S(1)} %get-tuple-element.36.dmixed_ref), custom_call_target="tpu_custom_call" | custom-call | tf_op jit(solution)/shard_map/weight_grad/pallas_call | solution.py:515
  99.8 0.0 collective-permute-done.14
  99.8 0.2 collective-permute-start.15
  100.1 1.7 %collective-permute-done.15.back_ref = f32[16,2,32,128]{3,2,1,0:T(8,128)S(1)} collective-permute-done((f32[16,2,32,128]{3,2,1,0:T(8,128)S(1)}, f32[16,2,32,128]{3,2,1,0:T(8,128)S(1)}, u32[]{:S(2)}, u32[]{:S(2)}) %collective-permute-start.15) | collective-permute-done | bytes 524320 | tf_op jit(solution)/shard_map/ppermute | solution.py:377
  101.8 0.0 copy-done.3
  101.8 5.8 %input_grad.1 = f32[16,2,64,512]{3,2,1,0:T(8,128)} custom-call(f32[16,2,64,512]{3,2,1,0:T(8,128)S(1)} %local_backward.1.local_ref, f32[16,2,32,128]{3,2,1,0:T(8,128)S(1)} %constant_dynamic-update-slice_fusion.4.front_ref, f32[16,2,32,128]{3,2,1,0:T(8,128)S(1)} %collective-permute-done.15.back_ref, bf16[256,512]{1,0:T(8,128)(2,1)S(1)} %copy-done.3, ...), custom_call_target="tpu_custom_call" | custom-call | tf_op jit(solution)/shard_map/input_grad/pallas_call | solution.py:527
  (18 shorter events, 0.3 us)
Async XLA Ops:
  0.6 12.7 %copy-start.8 = (f32[64]{0:T(128)S(1)}, f32[64]{0:T(128)}, u32[]{:S(2)}) copy-start(f32[64]{0:T(128)} %param.12) | copy-start | bytes 772
  0.6 2.2 %copy-start = (f32[16,2,512,64]{2,3,1,0:T(8,128)S(1)}, f32[16,2,512,64]{2,3,1,0:T(8,128)}, u32[]{:S(2)}) copy-start(f32[16,2,512,64]{2,3,1,0:T(8,128)} %param.9) | copy-start | bytes 12582916
  2.8 0.9 copy-start.6
  3.8 9.5 %copy-start.7 = (f32[64,64]{1,0:T(8,128)S(1)}, f32[64,64]{1,0:T(8,128)}, u32[]{:S(2)}) copy-start(f32[64,64]{1,0:T(8,128)} %weight.1) | copy-start | bytes 49156
  8.5 2.1 %collective-permute-start = (f32[16,2,32,128]{3,2,1,0:T(8,128)S(1)}, f32[16,2,32,128]{3,2,1,0:T(8,128)S(1)}, u32[]{:S(2)}, u32[]{:S(2)}) collective-permute-start(f32[16,2,32,128]{3,2,1,0:T(8,128)S(1)} %get-tuple-element.22), channel_id=1, source_target_pairs={{0,1},{1,0},{2,3},{3,2},{4,5},{5,4},{6,7},{7,6},{8,9},{9,8},{10,11... | collective-permute-start | bytes 1572872 | tf_op jit(solution)/shard_map/ppermute | solution.py:377
  10.6 6.8 %collective-permute-start.1 = (f32[8,2,32,128]{3,2,1,0:T(8,128)S(1)}, f32[8,2,32,128]{3,2,1,0:T(8,128)S(1)}, u32[]{:S(2)}, u32[]{:S(2)}) collective-permute-start(f32[8,2,32,128]{3,2,1,0:T(8,128)S(1)} %slice_add_fusion.1), channel_id=1, source_target_pairs={{0,3},{1,4},{2,7},{3,0},{4,1},{5,6},{6,5},{7,2},{8,11},{9,12},{10,... | collective-permute-start | bytes 786440 | tf_op jit(solution)/shard_map/ppermute | solution.py:377
  13.3 13.6 %copy-start.1 = (f32[2,32,64,128]{3,2,1,0:T(8,128)S(1)}, f32[2,32,64,128]{3,2,1,0:T(8,128)}, u32[]{:S(2)}) copy-start(f32[2,32,64,128]{3,2,1,0:T(8,128)} %refs_5_.3) | copy-start | bytes 6291460
  17.0 33.7 %copy-start.2 = (f32[16,2,512,64]{2,3,1,0:T(8,128)S(1)}, f32[16,2,512,64]{2,3,1,0:T(8,128)}, u32[]{:S(2)}) copy-start(f32[16,2,512,64]{2,3,1,0:T(8,128)} %param.13) | copy-start | bytes 12582916
  17.0 33.7 %copy-start.4 = (bf16[256,512]{1,0:T(8,128)(2,1)S(1)}, bf16[256,512]{1,0:T(8,128)(2,1)}, u32[]{:S(2)}) copy-start(bf16[256,512]{1,0:T(8,128)(2,1)} %constant.11.clone.synth_ref) | copy-start | bytes 786436
  17.0 33.7 %copy-start.5 = (bf16[512,256]{1,0:T(8,128)(2,1)S(1)}, bf16[512,256]{1,0:T(8,128)(2,1)}, u32[]{:S(2)}) copy-start(bf16[512,256]{1,0:T(8,128)(2,1)} %constant.9.clone.table_ref) | copy-start | bytes 786436
  17.4 4.5 %collective-permute-start.2 = (f32[4,2,32,128]{3,2,1,0:T(8,128)S(1)}, f32[4,2,32,128]{3,2,1,0:T(8,128)S(1)}, u32[]{:S(2)}, u32[]{:S(2)}) collective-permute-start(f32[4,2,32,128]{3,2,1,0:T(8,128)S(1)} %fusion.1), channel_id=1, source_target_pairs={{0,5},{1,2},{2,1},{3,6},{4,7},{5,0},{6,3},{7,4},{8,13},{9,10},{10,... | collective-permute-start | bytes 393224 | tf_op jit(solution)/shard_map/ppermute | solution.py:377
  22.0 5.0 %collective-permute-start.3 = (f32[2,2,32,128]{3,2,1,0:T(8,128)S(1)}, f32[2,2,32,128]{3,2,1,0:T(8,128)S(1)}, u32[]{:S(2)}, u32[]{:S(2)}) collective-permute-start(f32[2,2,32,128]{3,2,1,0:T(8,128)S(1)} %slice_add_fusion.6), channel_id=1, source_target_pairs={{0,9},{1,8},{2,11},{3,10},{4,13},{5,12},{6,15},{7,14},{8,1},{9,0},... | collective-permute-start | bytes 196616 | tf_op jit(solution)/shard_map/ppermute | solution.py:377
  30.8 5.1 %collective-permute-start.4 = (f32[2,2,32,128]{3,2,1,0:T(8,128)S(1)}, f32[2,2,32,128]{3,2,1,0:T(8,128)S(1)}, u32[]{:S(2)}, u32[]{:S(2)}) collective-permute-start(f32[2,2,32,128]{3,2,1,0:T(8,128)S(1)} %get-tuple-element.25), channel_id=1, source_target_pairs={{0,9},{1,8},{2,11},{3,10},{4,13},{5,12},{6,15},{7,14},{8,1},{9,0},... | collective-permute-start | bytes 196616 | tf_op jit(solution)/shard_map/ppermute | solution.py:377
  36.0 5.7 %collective-permute-start.5 = (f32[4,2,32,128]{3,2,1,0:T(8,128)S(1)}, f32[4,2,32,128]{3,2,1,0:T(8,128)S(1)}, u32[]{:S(2)}, u32[]{:S(2)}) collective-permute-start(f32[4,2,32,128]{3,2,1,0:T(8,128)S(1)} %pad_maximum_fusion.2), channel_id=1, source_target_pairs={{0,5},{1,2},{2,1},{3,6},{4,7},{5,0},{6,3},{7,4},{8,13},{9,10},{10,... | collective-permute-start | bytes 393224 | tf_op jit(solution)/shard_map/ppermute | solution.py:377
  41.7 7.0 %collective-permute-start.6 = (f32[8,2,32,128]{3,2,1,0:T(8,128)S(1)}, f32[8,2,32,128]{3,2,1,0:T(8,128)S(1)}, u32[]{:S(2)}, u32[]{:S(2)}) collective-permute-start(f32[8,2,32,128]{3,2,1,0:T(8,128)S(1)} %pad_maximum_fusion), channel_id=1, source_target_pairs={{0,3},{1,4},{2,7},{3,0},{4,1},{5,6},{6,5},{7,2},{8,11},{9,12},{10,... | collective-permute-start | bytes 786440 | tf_op jit(solution)/shard_map/ppermute | solution.py:377
  48.7 2.0 %collective-permute-start.7 = (f32[16,2,32,128]{3,2,1,0:T(8,128)S(1)}, f32[16,2,32,128]{3,2,1,0:T(8,128)S(1)}, u32[]{:S(2)}, u32[]{:S(2)}) collective-permute-start(f32[16,2,32,128]{3,2,1,0:T(8,128)S(1)} %constant_dynamic-update-slice_fusion.front_ref), channel_id=1, source_target_pairs={{0,1},{1,0},{2,3},{3,2},{4,5},{5,4},{6,7},{7,6},{8,9},{9,8},{10,11... | collective-permute-start | bytes 1572872 | tf_op jit(solution)/shard_map/ppermute | solution.py:377
  62.1 1.9 %collective-permute-start.8 = (f32[16,2,32,128]{3,2,1,0:T(8,128)S(1)}, f32[16,2,32,128]{3,2,1,0:T(8,128)S(1)}, u32[]{:S(2)}, u32[]{:S(2)}) collective-permute-start(f32[16,2,32,128]{3,2,1,0:T(8,128)S(1)} %get-tuple-element.30), channel_id=1, source_target_pairs={{0,1},{1,0},{2,3},{3,2},{4,5},{5,4},{6,7},{7,6},{8,9},{9,8},{10,11... | collective-permute-start | bytes 1572872 | tf_op jit(solution)/shard_map/ppermute | solution.py:377
  64.1 5.9 %collective-permute-start.9 = (f32[8,2,32,128]{3,2,1,0:T(8,128)S(1)}, f32[8,2,32,128]{3,2,1,0:T(8,128)S(1)}, u32[]{:S(2)}, u32[]{:S(2)}) collective-permute-start(f32[8,2,32,128]{3,2,1,0:T(8,128)S(1)} %slice_add_fusion), channel_id=1, source_target_pairs={{0,3},{1,4},{2,7},{3,0},{4,1},{5,6},{6,5},{7,2},{8,11},{9,12},{10,... | collective-permute-start | bytes 786440 | tf_op jit(solution)/shard_map/ppermute | solution.py:377
  68.8 33.0 %copy-start.3 = (bf16[256,512]{1,0:T(8,128)(2,1)S(1)}, bf16[256,512]{1,0:T(8,128)(2,1)}, u32[]{:S(2)}) copy-start(bf16[256,512]{1,0:T(8,128)(2,1)} %constant.10.clone.synth_ref) | copy-start | bytes 786436
  70.0 4.5 %collective-permute-start.10 = (f32[4,2,32,128]{3,2,1,0:T(8,128)S(1)}, f32[4,2,32,128]{3,2,1,0:T(8,128)S(1)}, u32[]{:S(2)}, u32[]{:S(2)}) collective-permute-start(f32[4,2,32,128]{3,2,1,0:T(8,128)S(1)} %fusion), channel_id=1, source_target_pairs={{0,5},{1,2},{2,1},{3,6},{4,7},{5,0},{6,3},{7,4},{8,13},{9,10},{10,... | collective-permute-start | bytes 393224 | tf_op jit(solution)/shard_map/ppermute | solution.py:377
  74.4 6.4 %collective-permute-start.11 = (f32[2,2,32,128]{3,2,1,0:T(8,128)S(1)}, f32[2,2,32,128]{3,2,1,0:T(8,128)S(1)}, u32[]{:S(2)}, u32[]{:S(2)}) collective-permute-start(f32[2,2,32,128]{3,2,1,0:T(8,128)S(1)} %slice_add_fusion.4), channel_id=1, source_target_pairs={{0,9},{1,8},{2,11},{3,10},{4,13},{5,12},{6,15},{7,14},{8,1},{9,0},... | collective-permute-start | bytes 196616 | tf_op jit(solution)/shard_map/ppermute | solution.py:377
  82.9 6.5 %collective-permute-start.12 = (f32[2,2,32,128]{3,2,1,0:T(8,128)S(1)}, f32[2,2,32,128]{3,2,1,0:T(8,128)S(1)}, u32[]{:S(2)}, u32[]{:S(2)}) collective-permute-start(f32[2,2,32,128]{3,2,1,0:T(8,128)S(1)} %get-tuple-element.34), channel_id=1, source_target_pairs={{0,9},{1,8},{2,11},{3,10},{4,13},{5,12},{6,15},{7,14},{8,1},{9,0},... | collective-permute-start | bytes 196616 | tf_op jit(solution)/shard_map/ppermute | solution.py:377
  89.5 4.5 %collective-permute-start.13 = (f32[4,2,32,128]{3,2,1,0:T(8,128)S(1)}, f32[4,2,32,128]{3,2,1,0:T(8,128)S(1)}, u32[]{:S(2)}, u32[]{:S(2)}) collective-permute-start(f32[4,2,32,128]{3,2,1,0:T(8,128)S(1)} %pad_maximum_fusion.3), channel_id=1, source_target_pairs={{0,5},{1,2},{2,1},{3,6},{4,7},{5,0},{6,3},{7,4},{8,13},{9,10},{10,... | collective-permute-start | bytes 393224 | tf_op jit(solution)/shard_map/ppermute | solution.py:377
  93.9 5.9 %collective-permute-start.14 = (f32[8,2,32,128]{3,2,1,0:T(8,128)S(1)}, f32[8,2,32,128]{3,2,1,0:T(8,128)S(1)}, u32[]{:S(2)}, u32[]{:S(2)}) collective-permute-start(f32[8,2,32,128]{3,2,1,0:T(8,128)S(1)} %pad_maximum_fusion.1), channel_id=1, source_target_pairs={{0,3},{1,4},{2,7},{3,0},{4,1},{5,6},{6,5},{7,2},{8,11},{9,12},{10,... | collective-permute-start | bytes 786440 | tf_op jit(solution)/shard_map/ppermute | solution.py:377
  99.8 2.0 %collective-permute-start.15 = (f32[16,2,32,128]{3,2,1,0:T(8,128)S(1)}, f32[16,2,32,128]{3,2,1,0:T(8,128)S(1)}, u32[]{:S(2)}, u32[]{:S(2)}) collective-permute-start(f32[16,2,32,128]{3,2,1,0:T(8,128)S(1)} %constant_dynamic-update-slice_fusion.4.front_ref), channel_id=1, source_target_pairs={{0,1},{1,0},{2,3},{3,2},{4,5},{5,4},{6,7},{7,6},{8,9},{9,8},{10,11... | collective-permute-start | bytes 1572872 | tf_op jit(solution)/shard_map/ppermute | solution.py:377

commit v3 on v2

--- a/solution.py
+++ b/solution.py
@@ -14,6 +14,7 @@
 LANES = 128
 SUB = 8
 VMEM_LIMIT = 16 << 20
+STEP = 8
 
 
 def split_np(values):
@@ -133,11 +134,11 @@
         flipped = jnp.where(low_lane, pltpu.roll(low, LANES // 2, 1), high)
         for block in range(half // SUB):
             rows = slice(SUB * block, SUB * (block + 1))
-            coef_ref[block, pl.ds(pl.multiple_of((at + i) * SUB, SUB), SUB)] = plain[rows]
-            coef_ref[block, pl.ds(pl.multiple_of((cells + at + i) * SUB, SUB), SUB)] = flipped[rows]
-
-
-def to_modes(coef_ref, table_ref, keep_ref, send_ref):
+            coef_ref[block, pl.ds((at + i) * SUB, SUB)] = plain[rows]
+            coef_ref[block, pl.ds((cells + at + i) * SUB, SUB)] = flipped[rows]
+
+
+def to_modes(coef_ref, table_ref, keep_ref, send_ref, plane):
     modes = 2 * keep_ref.shape[0]
     for block in range(coef_ref.shape[0]):
         high, low = split(coef_ref[block])
@@ -145,11 +146,11 @@
         full = full[:, :LANES] + full[:, LANES:] + dot(table_ref[1], high)
         full = full.reshape(modes, SUB, LANES)
         rows = slice(SUB * block, SUB * (block + 1))
-        keep_ref[:, 0, rows] = full[: modes // 2]
-        send_ref[:, 0, rows] = full[modes // 2 :]
-
-
-def from_modes(front_ref, back_ref, table_ref, lhs_ref):
+        keep_ref[:, plane, rows] = full[: modes // 2]
+        send_ref[:, plane, rows] = full[modes // 2 :]
+
+
+def from_modes(front_ref, back_ref, table_ref, lhs_ref, plane):
     modes = 2 * front_ref.shape[0]
     cells, channels = lhs_ref.shape[:2]
     half = channels // 2
@@ -158,7 +159,7 @@
     low_lane = lane < LANES // 2
     for block in range(half // SUB):
         rows = slice(SUB * block, SUB * (block + 1))
-        values = jnp.concatenate([front_ref[:, 0, rows], back_ref[:, 0, rows]], axis=0)
+        values = jnp.concatenate([front_ref[:, plane, rows], back_ref[:, plane, rows]], axis=0)
         high, low = split(values.reshape(modes * SUB, LANES))
         full = dot(table_ref[0], jnp.concatenate([high, low], axis=1))
         full = full[:, :LANES] + full[:, LANES:] + dot(table_ref[1], high)
@@ -230,20 +231,31 @@
     return jnp.where(lane, rolled, -rolled)
 
 
-def spanwise_kernel(sizes, x_ref, table_ref, keep_ref, send_ref, down_ref, back_ref, coef_ref):
-    step = pl.program_id(1)
-    cells, _, channels, span = x_ref.shape
-
-    @pl.when((step == 0) & (pl.program_id(0) == 0))
-    def _():
-        make_tables(down_ref, back_ref, *sizes)
-
-    high, low = split(x_ref[...].reshape(cells * channels, span))
-    analyse(high, low, table_ref, step * cells, coef_ref)
-
-    @pl.when(step == pl.num_programs(1) - 1)
-    def _():
-        to_modes(coef_ref, down_ref, keep_ref, send_ref)
+def chunks(cells, planes):
+    return [(p, at) for p in range(planes) for at in range(0, cells, STEP)]
+
+
+def spanwise_kernel(
+    sizes, x_ref, table_hbm, keep_ref, send_ref, down_ref, back_ref,
+    table_ref, x_scr, coef_ref, sems,
+):
+    cells, planes, channels, span = x_ref.shape
+    work = chunks(cells, planes)
+    copies = [
+        pltpu.make_async_copy(x_ref.at[pl.ds(at, STEP), p], x_scr.at[i], sems.at[i])
+        for i, (p, at) in enumerate(work)
+    ]
+    copies.append(pltpu.make_async_copy(table_hbm, table_ref, sems.at[len(work)]))
+    for copy in copies[-1:] + copies[:-1]:
+        copy.start()
+    make_tables(down_ref, back_ref, *sizes)
+    copies[-1].wait()
+    for i, (p, at) in enumerate(work):
+        copies[i].wait()
+        high, low = split(x_scr[i].reshape(STEP * channels, span))
+        analyse(high, low, table_ref, at, coef_ref.at[p])
+    for p in range(planes):
+        to_modes(coef_ref.at[p], down_ref, keep_ref, send_ref, p)
 
 
 def pointwise_kernel(transposed, values_ref, local_ref, bias_ref, out_ref):
@@ -256,120 +268,167 @@
     if bias_ref is not None:
         row = jnp.broadcast_to(bias_ref[...], (channels, channels))
         column = row.T[:, :1]
-    for cell in range(values_ref.shape[0]):
-        high, low = split(values_ref[cell, 0])
-        full = dot(lhs, jnp.concatenate([high, low, high], axis=0))
-        out_ref[cell, 0] = full if bias_ref is None else full + column
+    cells, planes = values_ref.shape[:2]
+
+    def body(step, _):
+        for p in range(planes):
+            for cell in range(2):
+                at = 2 * step + cell
+                high, low = split(values_ref[at, p])
+                full = dot(lhs, jnp.concatenate([high, low, high], axis=0))
+                out_ref[at, p] = full if bias_ref is None else full + column
+        return 0
+
+    lax.fori_loop(0, cells // 2, body, 0)
+
+
+def total_of(piece_refs, j, plane):
+    total = piece_refs[0][j, plane]
+    for ref in piece_refs[1:]:
+        total = total + ref[j, plane]
+    return total
 
 
 def mix_kernel(*refs):
-    *piece_refs, w_ref, modes_ref, mixed_ref, first_scr, second_scr = refs
-    planes = modes_ref.shape[1]
-    kz_count = w_ref.shape[1]
-    quarter = LANES // 4
-    for plane in range(planes):
-        total = piece_refs[0][0, plane]
-        for ref in piece_refs[1:]:
-            total = total + ref[0, plane]
-        modes_ref[0, plane] = total
-        for kz in range(kz_count):
-            sums = [None, None]
-            for half in range(2):
-                weight = w_ref[0, kz, quarter * half : quarter * (half + 1)]
-                for part in range(2):
-                    at = half * (LANES // 2) + part * quarter + kz
-                    term = total[:, at : at + 1] * weight
-                    sums[part] = term if sums[part] is None else sums[part] + term
-            first_scr[kz : kz + 1] = jnp.sum(sums[0], axis=0, keepdims=True)
-            second_scr[kz : kz + 1] = jnp.sum(sums[1], axis=0, keepdims=True)
-        rows = first_scr[...] - turn_down(second_scr[...])
-        mixed_ref[0, plane] = transpose_out(rows)
+    *piece_refs, w_ref, modes_ref, mixed_ref = refs
+    owned, planes = modes_ref.shape[:2]
+    kz_count, channels = w_ref.shape[1:3]
+    wide = SUB * channels
+    low_lane = lax.broadcasted_iota(jnp.int32, (kz_count, LANES), 1) < channels
+    row = lax.broadcasted_iota(jnp.int32, (kz_count, wide), 0) & (SUB - 1)
+    own = lax.broadcasted_iota(jnp.int32, (kz_count, wide), 1) // channels == row
+
+    def body(j, _):
+        sides = []
+        for plane in range(planes):
+            total = total_of(piece_refs, j, plane)
+            modes_ref[j, plane] = total
+            rows = transpose_in(total)
+            rolled = pltpu.roll(rows, channels, 1)
+            for doubled in (jnp.where(low_lane, rows, rolled), jnp.where(low_lane, rolled, rows)):
+                tiled = jnp.concatenate([doubled] * (wide // LANES), axis=1)
+                sides.append(jnp.where(own, tiled, 0.0))
+        results = []
+        for at in range(0, kz_count, SUB):
+            left = jnp.concatenate([side[at : at + SUB] for side in sides], axis=0)
+            left = jnp.concatenate(split(left), axis=0)
+            right = w_ref[j, at : at + SUB].reshape(wide, LANES)
+            full = dot(left, jnp.concatenate(split(right), axis=1))
+            count = full.shape[0] // 2
+            full = full[:count, :LANES] + full[:count, LANES:] + full[count:, :LANES]
+            results.append(full.reshape(planes, 2, SUB, LANES))
+        for plane in range(planes):
+            first, second = (
+                jnp.concatenate([result[plane, part] for result in results], axis=0)
+                for part in range(2)
+            )
+            mixed_ref[j, plane] = transpose_out(first - turn_down(second))
+        return 0
+
+    lax.fori_loop(0, owned, body, 0)
 
 
 def middle_kernel(
-    local_ref, up_ref, front_ref, back_ref, synth_ref, table_ref, down_ref, back_table_ref, *rest
+    local_ref, up_ref, front_ref, back_ref, synth_ref, table_ref, down_ref, back_table_ref,
+    act_ref, dpre_ref, keep_ref, send_ref, lhs_ref, coef_ref,
 ):
-    act_ref, dpre_ref, keep_ref, send_ref, lhs_ref, coef_ref = rest[-6:]
-    step = pl.program_id(1)
-    cells, _, channels, span = up_ref.shape
-
-    @pl.when(step == 0)
-    def _():
-        from_modes(front_ref, back_ref, back_table_ref, lhs_ref)
-
-    spectral = synthesise(lhs_ref, step * cells, cells, synth_ref)
-    pre = spectral.reshape(cells, channels, span) + local_ref[:, 0]
-    cumulative, density = normal_parts(pre)
-    act_ref[:, 0] = pre * cumulative
-    dpre = up_ref[:, 0] * (cumulative + pre * density)
-    dpre_ref[:, 0] = dpre
-    high, low = split(dpre.reshape(cells * channels, span))
-    analyse(high, low, table_ref, step * cells, coef_ref)
-
-    @pl.when(step == pl.num_programs(1) - 1)
-    def _():
-        to_modes(coef_ref, down_ref, keep_ref, send_ref)
+    cells, planes, channels, span = up_ref.shape
+    for p in range(planes):
+        from_modes(front_ref, back_ref, back_table_ref, lhs_ref.at[p], p)
+    for p, at in chunks(cells, planes):
+        rows = pl.ds(at, STEP)
+        spectral = synthesise(lhs_ref.at[p], at, STEP, synth_ref)
+        pre = spectral.reshape(STEP, channels, span) + local_ref[rows, p]
+        cumulative, density = normal_parts(pre)
+        act_ref[rows, p] = pre * cumulative
+        dpre = up_ref[rows, p] * (cumulative + pre * density)
+        dpre_ref[rows, p] = dpre
+        high, low = split(dpre.reshape(STEP * channels, span))
+        analyse(high, low, table_ref, at, coef_ref.at[p])
+    for p in range(planes):
+        to_modes(coef_ref.at[p], down_ref, keep_ref, send_ref, p)
 
 
 def adjoint_kernel(*refs):
     *piece_refs, w_ref, dmixed_ref, dmodes_ref = refs
-    planes = dmixed_ref.shape[1]
+    owned, planes = dmixed_ref.shape[:2]
     kz_count, channels, width = w_ref.shape[1:]
     quarter = LANES // 4
-    weight = w_ref[0].reshape(kz_count * channels, width)
-    w_high, w_low = split(weight)
     lane = lax.broadcasted_iota(jnp.int32, (channels, LANES // 2), 1) % quarter
-    for plane in range(planes):
-        total = piece_refs[0][0, plane]
-        for ref in piece_refs[1:]:
-            total = total + ref[0, plane]
-        dmixed_ref[0, plane] = total
-        rows = transpose_in(total)
-        both = jnp.concatenate([rows, turn_down(rows)], axis=0)
-        high, low = split(both)
-        right = jnp.concatenate([high, low], axis=0).T
-        full = dot(w_high, right)
-        full = full[:, : LANES // 2] + full[:, LANES // 2 :] + dot(w_low, right[:, : LANES // 2])
-        full = full.reshape(kz_count, channels, LANES // 2)
-        result = jnp.zeros((channels, LANES // 2), F32)
+
+    def body(j, _):
+        w_high, w_low = split(w_ref[j].reshape(kz_count * channels, width))
+        for plane in range(planes):
+            total = total_of(piece_refs, j, plane)
+            dmixed_ref[j, plane] = total
+            rows = transpose_in(total)
+            both = jnp.concatenate([rows, turn_down(rows)], axis=0)
+            high, low = split(both)
+            right = jnp.concatenate([high, low], axis=0).T
+            full = dot(w_high, right)
+            full = (
+                full[:, : LANES // 2] + full[:, LANES // 2 :] + dot(w_low, right[:, : LANES // 2])
+            )
+            full = full.reshape(kz_count, channels, LANES // 2)
+            result = jnp.zeros((channels, LANES // 2), F32)
+            for kz in range(kz_count):
+                result = jnp.where(lane == kz, full[kz], result)
+            dmodes_ref[j, plane] = jnp.concatenate(
+                [result[: channels // 2], result[channels // 2 :]], axis=1
+            )
+        return 0
+
+    lax.fori_loop(0, owned, body, 0)
+
+
+def weight_grad_kernel(modes_ref, dmixed_ref, grad_ref):
+    owned, planes = modes_ref.shape[:2]
+    kz_count, channels = grad_ref.shape[1:3]
+    assert planes * channels == LANES
+    half = channels // 2
+    low_lane = lax.broadcasted_iota(jnp.int32, (half, LANES), 1) < channels
+    lane = lax.broadcasted_iota(jnp.int32, (2 * channels, LANES), 1) & (kz_count - 1)
+
+    def body(j, _):
+        right = []
+        for plane in range(planes):
+            rows = transpose_in(dmixed_ref[j, plane])
+            right += [rows, turn_down(rows)]
+        right = jnp.concatenate(split(jnp.concatenate(right, axis=0)), axis=1)
+        first, second = modes_ref[j, 0], modes_ref[j, 1]
+        left = jnp.concatenate(
+            [
+                jnp.where(low_lane, first, pltpu.roll(second, channels, 1)),
+                jnp.where(low_lane, pltpu.roll(first, channels, 1), second),
+            ],
+            axis=0,
+        )
+        left = jnp.concatenate(split(left), axis=0)
         for kz in range(kz_count):
-            result = jnp.where(lane == kz, full[kz], result)
-        dmodes_ref[0, plane] = jnp.concatenate(
-            [result[: channels // 2], result[channels // 2 :]], axis=1
-        )
-
-
-def weight_grad_kernel(modes_ref, dmixed_ref, grad_ref, rows_scr):
-    planes = modes_ref.shape[1]
-    kz_count = grad_ref.shape[1]
-    quarter = LANES // 4
-    for plane in range(planes):
-        rows = transpose_in(dmixed_ref[0, plane])
-        rows_scr[2 * plane] = rows
-        rows_scr[2 * plane + 1] = turn_down(rows)
-    for kz in range(kz_count):
-        for half in range(2):
-            total = None
-            for plane in range(planes):
-                for part in range(2):
-                    at = half * (LANES // 2) + part * quarter + kz
-                    column = modes_ref[0, plane, :, at : at + 1]
-                    term = column * rows_scr[2 * plane + part, kz : kz + 1]
-                    total = term if total is None else total + term
-            grad_ref[0, kz, quarter * half : quarter * (half + 1)] = total
-
-
-def input_grad_kernel(local_ref, front_ref, back_ref, synth_ref, back_table_ref, *rest):
-    out_ref, lhs_ref = rest[-2:]
-    step = pl.program_id(1)
-    cells, _, channels, span = local_ref.shape
-
-    @pl.when(step == 0)
-    def _():
-        from_modes(front_ref, back_ref, back_table_ref, lhs_ref)
-
-    spectral = synthesise(lhs_ref, step * cells, cells, synth_ref)
-    out_ref[:, 0] = spectral.reshape(cells, channels, span) + local_ref[:, 0]
+            full = dot(jnp.where(lane == kz, left, jnp.zeros_like(left)), right)
+            grad_ref[j, kz] = (
+                full[:channels, :LANES] + full[:channels, LANES:] + full[channels:, :LANES]
+            )
+        return 0
+
+    lax.fori_loop(0, owned, body, 0)
+
+
+def input_grad_kernel(
+    local_ref, front_ref, back_ref, synth_ref, back_table_ref, out_ref, out_scr, lhs_ref, sems
+):
+    cells, planes, channels, span = local_ref.shape
+    copies = []
+    for i, (p, at) in enumerate(chunks(cells, planes)):
+        if at == 0:
+            from_modes(front_ref, back_ref, back_table_ref, lhs_ref.at[p], p)
+        rows = pl.ds(at, STEP)
+        spectral = synthesise(lhs_ref.at[p], at, STEP, synth_ref)
+        out_scr[i] = spectral.reshape(STEP, channels, span) + local_ref[rows, p]
+        copies.append(pltpu.make_async_copy(out_scr.at[i], out_ref.at[rows, p], sems.at[i]))
+        copies[-1].start()
+    for copy in copies:
+        copy.wait()
 
 
 def swap(values, step):
@@ -427,37 +486,34 @@
     up = jnp.swapaxes(upstream, 2, 3)
     scale = float(cells * lax.axis_size("stream") * span)
     ana_fwd, ana_inv, syn_fwd, syn_inv = map(jnp.asarray, span_tables(span, kz_count, scale))
-    step_cells = 4
-    grid = (planes, cells // step_cells)
-    coef_scr = pltpu.VMEM((half_channels // SUB, 2 * cells * SUB, LANES), F32)
-    lhs_scr = pltpu.VMEM((cells, channels, LANES), F32)
+    pieces_of = len(chunks(cells, planes))
+    coef_scr = pltpu.VMEM((planes, half_channels // SUB, 2 * cells * SUB, LANES), F32)
+    lhs_scr = pltpu.VMEM((planes, cells, channels, LANES), F32)
+    span_scr = pltpu.VMEM((pieces_of, STEP, channels, span), F32)
+    sem_scr = pltpu.SemaphoreType.DMA((pieces_of + 1,))
     down = shape((2, total_modes * SUB, 2 * cells * SUB), BF16)
     back = shape((2, 2 * cells * SUB, total_modes * SUB), BF16)
-    grid_block = pl.BlockSpec((step_cells, 1, channels, span), lambda p, s: (s, p, 0, 0))
-    half_block = pl.BlockSpec((half_modes, 1, half_channels, LANES), lambda p, s: (0, p, 0, 0))
-    own_block = pl.BlockSpec((1, planes, half_channels, LANES), lambda j: (j, 0, 0, 0))
-    weight_block = pl.BlockSpec((1, kz_count, channels, 2 * channels), lambda j: (j, 0, 0, 0))
+    here = pl.BlockSpec(memory_space=pltpu.VMEM)
+    apart = pl.BlockSpec(memory_space=pl.ANY)
     own_shape = shape((owned, planes, half_channels, LANES), F32)
     half_shape = shape((half_modes, planes, half_channels, LANES), F32)
     grid_shape = shape(x.shape, F32)
 
     keep, send, down, back = pl.pallas_call(
         functools.partial(spanwise_kernel, (owned, total_modes, cells)),
-        grid=grid,
-        in_specs=[grid_block, whole(ana_fwd)],
-        out_specs=[half_block, half_block, whole(down), whole(back)],
+        in_specs=[apart, apart],
+        out_specs=[here] * 4,
         out_shape=[half_shape, half_shape, down, back],
-        scratch_shapes=[coef_scr],
+        scratch_shapes=[pltpu.VMEM(ana_fwd.shape, BF16), span_scr, coef_scr, sem_scr],
         compiler_params=params(),
         name="spanwise",
-    )(x, ana_fwd)
+    )(pltpu.with_memory_space_constraint(x, pltpu.HBM), pltpu.with_memory_space_constraint(ana_fwd, pltpu.HBM))
 
     def local_forward():
         return pl.pallas_call(
             functools.partial(pointwise_kernel, True),
-            grid=grid,
-            in_specs=[grid_block, whole(local_weight), whole(offset_bias[None])],
-            out_specs=grid_block,
+            in_specs=[here] * 3,
+            out_specs=here,
             out_shape=grid_shape,
             compiler_params=params(),
             name="local_forward",
@@ -466,23 +522,17 @@
     pieces, local = scatter_sum(keep, send, local_forward)
     modes, mixed = pl.pallas_call(
         mix_kernel,
-        grid=(owned,),
-        in_specs=[own_block] * len(pieces) + [weight_block],
-        out_specs=[own_block] * 2,
+        in_specs=[here] * (len(pieces) + 1),
+        out_specs=[here] * 2,
         out_shape=[own_shape] * 2,
-        scratch_shapes=[pltpu.VMEM((kz_count, LANES), F32)] * 2,
         compiler_params=params(),
         name="mix",
     )(*pieces, mode_weight)
     front, behind, _ = gather_all(mixed)
     act, dpre, keep, send = pl.pallas_call(
         middle_kernel,
-        grid=grid,
-        in_specs=[
-            grid_block, grid_block, half_block, half_block,
-            whole(syn_inv), whole(ana_inv), whole(down), whole(back),
-        ],
-        out_specs=[grid_block, grid_block, half_block, half_block],
+        in_specs=[here] * 8,
+        out_specs=[here] * 4,
         out_shape=[grid_shape, grid_shape, half_shape, half_shape],
         scratch_shapes=[lhs_scr, coef_scr],
         compiler_params=params(),
@@ -492,9 +542,8 @@
     def local_backward():
         return pl.pallas_call(
             lambda values, weight, out: pointwise_kernel(False, values, weight, None, out),
-            grid=grid,
-            in_specs=[grid_block, whole(local_weight)],
-            out_specs=grid_block,
+            in_specs=[here] * 2,
+            out_specs=here,
             out_shape=grid_shape,
             compiler_params=params(),
             name="local_backward",
@@ -503,9 +552,8 @@
     pieces, local = scatter_sum(keep, send, local_backward)
     dmixed, dmodes = pl.pallas_call(
         adjoint_kernel,
-        grid=(owned,),
-        in_specs=[own_block] * len(pieces) + [weight_block],
-        out_specs=[own_block] * 2,
+        in_specs=[here] * (len(pieces) + 1),
+        out_specs=[here] * 2,
         out_shape=[own_shape] * 2,
         compiler_params=params(),
         name="adjoint",
@@ -514,11 +562,9 @@
     def weight_grad():
         return pl.pallas_call(
             weight_grad_kernel,
-            grid=(owned,),
-            in_specs=[own_block] * 2,
-            out_specs=weight_block,
+            in_specs=[here] * 2,
+            out_specs=here,
             out_shape=shape(mode_weight.shape, F32),
-            scratch_shapes=[pltpu.VMEM((2 * planes, kz_count, LANES), F32)],
             compiler_params=params(),
             name="weight_grad",
         )(modes, dmixed)
@@ -526,11 +572,10 @@
     front, behind, grad_modes = gather_all(dmodes, weight_grad)
     grad_snapshot = pl.pallas_call(
         input_grad_kernel,
-        grid=grid,
-        in_specs=[grid_block, half_block, half_block, whole(syn_fwd), whole(back)],
-        out_specs=grid_block,
+        in_specs=[here] * 5,
+        out_specs=apart,
         out_shape=grid_shape,
-        scratch_shapes=[lhs_scr],
+        scratch_shapes=[span_scr, lhs_scr, sem_scr],
         compiler_params=params(),
         name="input_grad",
     )(local, front, behind, syn_fwd, back)

time: 108 us -> 95.2 us (0.88)
  Pallas kernels: 38.7 us -> 26 us
  local copies, waits for them, and re-layouts: 3.26 us -> 0.12 us
  waiting for transfers between devices: 41.1 us -> 44.1 us
    pallas_call x6, Pallas kernels: 31 us -> 19.8 us  [the longest x1 7.6 us: per_device(): pl.pallas_call(middle_kernel, in_specs=[here] * 8, out_specs=[here] * 4,...]
    unnamed x24 -> x22, local copies, waits for them, and re-layouts: 3.22 us -> 0.09 us
    ppermute x16, waiting for transfers between devices: 41.1 us -> 44.1 us  [swap(): lax.ppermute(values, 'stream', [(i, i ^ stage_mask(i, step)) for i in ran...]
  transfers between devices with their start and end apart: 16 -> 16, of which waited for: 15 -> 16; matrix products, arithmetic and copies ran while one was open for 0% -> 0% of each run, Pallas kernels for 10% -> 8%
where the time goes in v3:
time: 95.2 us; the launch traced here: 95.1 us
  waiting for transfers between devices  44.1 us (46%)
  Pallas kernels  26 us (27%)
  starting transfers between devices  23.6 us (25%)
  between operations  0.97 us (1%)
    ppermute x16, waiting for transfers between devices, swap(): lax.ppermute(values, 'stream', [(i, i ^ stage_mask(i, step)) for i in ran...  44.1 us
    ppermute x16, starting transfers between devices, swap(): lax.ppermute(values, 'stream', [(i, i ^ stage_mask(i, step)) for i in ran...  23.6 us
    pallas_call x1, Pallas kernels, per_device(): pl.pallas_call(middle_kernel, in_specs=[here] * 8, out_specs=[here] * 4,...  7.6 us
    pallas_call x1, Pallas kernels, per_device(): pl.pallas_call(functools.partial(spanwise_kernel, (owned, total_modes, ce...  4.04 us
    pallas_call x1, Pallas kernels, per_device(): pl.pallas_call(input_grad_kernel, in_specs=[here] * 5, out_specs=apart, o...  3.37 us
    pallas_call x1, Pallas kernels, weight_grad(): pl.pallas_call(weight_grad_kernel, in_specs=[here] * 2, out_specs=here, o...  3.05 us
    pallas_call x1, Pallas kernels, local_forward(): pl.pallas_call(functools.partial(pointwise_kernel, True), in_specs=[here]...  2.46 us
    pallas_call x1, Pallas kernels, local_backward(): pl.pallas_call(lambda values, weight, out: pointwise_kernel(False, values...  2.15 us
  transfers between devices with their start and end apart: 16, of which 16 were waited for; matrix products, arithmetic and copies ran while one was open for 0% of the time, Pallas kernels for 8%

profile of v3, /device:TPU:0, one launch (start us, length us, event | category | flops | bytes accessed | tf_op | source)
XLA Modules:
  0.0 95.1 jit_solution(17860749689744609878)
XLA Ops:
  0.6 0.0 copy-start
  0.6 0.0 copy-start.6
  0.7 0.0 copy-start.7
  0.7 4.0 %spanwise.1 = (f32[16,2,32,128]{3,2,1,0:T(8,128)S(1)}, f32[16,2,32,128]{3,2,1,0:T(8,128)S(1)}, bf16[2,256,256]{2,1,0:T(8,128)(2,1)S(1)}, bf16[2,256,256]{2,1,0:T(8,128)(2,1)S(1)}) custom-call(f32[16,2,64,512]{3,2,1,0:T(8,128)} %bitcast.5, bf16[512,256]{1,0:T(8,128)(2,1)} %constant.8.clone.table_hbm), custom_call_target="tpu_custom_call" | custom-call | tf_op jit(solution)/shard_map/spanwise/pallas_call | solution.py:502
  4.7 0.5 collective-permute-start
  5.2 1.5 %collective-permute-done.refs_1_ = f32[16,2,32,128]{3,2,1,0:T(8,128)S(1)} collective-permute-done((f32[16,2,32,128]{3,2,1,0:T(8,128)S(1)}, f32[16,2,32,128]{3,2,1,0:T(8,128)S(1)}, u32[]{:S(2)}, u32[]{:S(2)}) %collective-permute-start) | collective-permute-done | bytes 524320 | tf_op jit(solution)/shard_map/ppermute | solution.py:436
  6.8 2.7 %collective-permute-start.1 = (f32[8,2,32,128]{3,2,1,0:T(8,128)S(1)}, f32[8,2,32,128]{3,2,1,0:T(8,128)S(1)}, u32[]{:S(2)}, u32[]{:S(2)}) collective-permute-start(f32[8,2,32,128]{3,2,1,0:T(8,128)S(1)} %slice_add_fusion.1), channel_id=1, source_target_pairs={{0,3},{1,4},{2,7},{3,0},{4,1},{5,6},{6,5},{7,2},{8,11},{9,12},{10,... | collective-permute-start | bytes 786440 | tf_op jit(solution)/shard_map/ppermute | solution.py:436
  9.5 0.0 copy-done
  9.5 0.0 copy-done.6
  9.5 0.0 copy-done.7
  9.5 0.0 copy-start.1
  9.5 2.5 %local_forward.1.local_ref = f32[16,2,64,512]{3,2,1,0:T(8,128)S(1)} custom-call(f32[16,2,64,512]{3,2,1,0:T(8,128)S(1)} %bitcast.6, f32[64,64]{1,0:T(8,128)S(1)} %copy-done.6, f32[1,64]{1,0:T(1,128)S(1)} %bitcast.8), custom_call_target="tpu_custom_call" | custom-call | tf_op jit(solution)/shard_map/local_forward/pallas_call | solution.py:513
  12.0 0.0 copy-start.2
  12.0 0.0 copy-start.4
  12.0 0.0 copy-start.5
  12.0 1.5 %collective-permute-done.1.refs_2_ = f32[8,2,32,128]{3,2,1,0:T(8,128)S(1)} collective-permute-done((f32[8,2,32,128]{3,2,1,0:T(8,128)S(1)}, f32[8,2,32,128]{3,2,1,0:T(8,128)S(1)}, u32[]{:S(2)}, u32[]{:S(2)}) %collective-permute-start.1) | collective-permute-done | bytes 262176 | tf_op jit(solution)/shard_map/ppermute | solution.py:436
  13.6 1.9 %collective-permute-start.2 = (f32[4,2,32,128]{3,2,1,0:T(8,128)S(1)}, f32[4,2,32,128]{3,2,1,0:T(8,128)S(1)}, u32[]{:S(2)}, u32[]{:S(2)}) collective-permute-start(f32[4,2,32,128]{3,2,1,0:T(8,128)S(1)} %fusion.1), channel_id=1, source_target_pairs={{0,5},{1,2},{2,1},{3,6},{4,7},{5,0},{6,3},{7,4},{8,13},{9,10},{10,... | collective-permute-start | bytes 393224 | tf_op jit(solution)/shard_map/ppermute | solution.py:436
  15.5 2.7 %collective-permute-done.2.refs_3_ = f32[4,2,32,128]{3,2,1,0:T(8,128)S(1)} collective-permute-done((f32[4,2,32,128]{3,2,1,0:T(8,128)S(1)}, f32[4,2,32,128]{3,2,1,0:T(8,128)S(1)}, u32[]{:S(2)}, u32[]{:S(2)}) %collective-permute-start.2) | collective-permute-done | bytes 131104 | tf_op jit(solution)/shard_map/ppermute | solution.py:436
  18.1 2.8 %collective-permute-start.3 = (f32[2,2,32,128]{3,2,1,0:T(8,128)S(1)}, f32[2,2,32,128]{3,2,1,0:T(8,128)S(1)}, u32[]{:S(2)}, u32[]{:S(2)}) collective-permute-start(f32[2,2,32,128]{3,2,1,0:T(8,128)S(1)} %slice_add_fusion.6), channel_id=1, source_target_pairs={{0,9},{1,8},{2,11},{3,10},{4,13},{5,12},{6,15},{7,14},{8,1},{9,0},... | collective-permute-start | bytes 196616 | tf_op jit(solution)/shard_map/ppermute | solution.py:436
  20.9 2.2 %collective-permute-done.3.refs_4_ = f32[2,2,32,128]{3,2,1,0:T(8,128)S(1)} collective-permute-done((f32[2,2,32,128]{3,2,1,0:T(8,128)S(1)}, f32[2,2,32,128]{3,2,1,0:T(8,128)S(1)}, u32[]{:S(2)}, u32[]{:S(2)}) %collective-permute-start.3) | collective-permute-done | bytes 65568 | tf_op jit(solution)/shard_map/ppermute | solution.py:436
  23.1 0.0 copy-done.1
  23.1 1.3 %mix.1 = (f32[2,2,32,128]{3,2,1,0:T(8,128)S(1)}, f32[2,2,32,128]{3,2,1,0:T(8,128)S(1)}) custom-call(f32[16,2,32,128]{3,2,1,0:T(8,128)S(1)} %get-tuple-element.21.refs_0_, f32[16,2,32,128]{3,2,1,0:T(8,128)S(1)} %collective-permute-done.refs_1_, f32[8,2,32,128]{3,2,1,0:T(8,128)S(1)} %collective-permute-done.1.refs_2_, ...), custom_call_target="tpu_custom_call" | custom-call | tf_op jit(solution)/shard_map/mix/pallas_call | solution.py:523
  24.4 3.0 %collective-permute-start.4 = (f32[2,2,32,128]{3,2,1,0:T(8,128)S(1)}, f32[2,2,32,128]{3,2,1,0:T(8,128)S(1)}, u32[]{:S(2)}, u32[]{:S(2)}) collective-permute-start(f32[2,2,32,128]{3,2,1,0:T(8,128)S(1)} %get-tuple-element.25), channel_id=1, source_target_pairs={{0,9},{1,8},{2,11},{3,10},{4,13},{5,12},{6,15},{7,14},{8,1},{9,0},... | collective-permute-start | bytes 196616 | tf_op jit(solution)/shard_map/ppermute | solution.py:436
  27.4 2.2 %collective-permute-done.4 = f32[2,2,32,128]{3,2,1,0:T(8,128)S(1)} collective-permute-done((f32[2,2,32,128]{3,2,1,0:T(8,128)S(1)}, f32[2,2,32,128]{3,2,1,0:T(8,128)S(1)}, u32[]{:S(2)}, u32[]{:S(2)}) %collective-permute-start.4) | collective-permute-done | bytes 65568 | tf_op jit(solution)/shard_map/ppermute | solution.py:436
  29.6 3.0 %collective-permute-start.5 = (f32[4,2,32,128]{3,2,1,0:T(8,128)S(1)}, f32[4,2,32,128]{3,2,1,0:T(8,128)S(1)}, u32[]{:S(2)}, u32[]{:S(2)}) collective-permute-start(f32[4,2,32,128]{3,2,1,0:T(8,128)S(1)} %pad_maximum_fusion.2), channel_id=1, source_target_pairs={{0,5},{1,2},{2,1},{3,6},{4,7},{5,0},{6,3},{7,4},{8,13},{9,10},{10,... | collective-permute-start | bytes 393224 | tf_op jit(solution)/shard_map/ppermute | solution.py:436
  32.6 2.7 %collective-permute-done.5 = f32[4,2,32,128]{3,2,1,0:T(8,128)S(1)} collective-permute-done((f32[4,2,32,128]{3,2,1,0:T(8,128)S(1)}, f32[4,2,32,128]{3,2,1,0:T(8,128)S(1)}, u32[]{:S(2)}, u32[]{:S(2)}) %collective-permute-start.5) | collective-permute-done | bytes 131104 | tf_op jit(solution)/shard_map/ppermute | solution.py:436
  35.3 2.9 %collective-permute-start.6 = (f32[8,2,32,128]{3,2,1,0:T(8,128)S(1)}, f32[8,2,32,128]{3,2,1,0:T(8,128)S(1)}, u32[]{:S(2)}, u32[]{:S(2)}) collective-permute-start(f32[8,2,32,128]{3,2,1,0:T(8,128)S(1)} %pad_maximum_fusion), channel_id=1, source_target_pairs={{0,3},{1,4},{2,7},{3,0},{4,1},{5,6},{6,5},{7,2},{8,11},{9,12},{10,... | collective-permute-start | bytes 786440 | tf_op jit(solution)/shard_map/ppermute | solution.py:436
  38.2 4.0 %collective-permute-done.6 = f32[8,2,32,128]{3,2,1,0:T(8,128)S(1)} collective-permute-done((f32[8,2,32,128]{3,2,1,0:T(8,128)S(1)}, f32[8,2,32,128]{3,2,1,0:T(8,128)S(1)}, u32[]{:S(2)}, u32[]{:S(2)}) %collective-permute-start.6) | collective-permute-done | bytes 262176 | tf_op jit(solution)/shard_map/ppermute | solution.py:436
  42.3 0.1 collective-permute-start.7
  42.3 1.9 %collective-permute-done.7.back_ref = f32[16,2,32,128]{3,2,1,0:T(8,128)S(1)} collective-permute-done((f32[16,2,32,128]{3,2,1,0:T(8,128)S(1)}, f32[16,2,32,128]{3,2,1,0:T(8,128)S(1)}, u32[]{:S(2)}, u32[]{:S(2)}) %collective-permute-start.7) | collective-permute-done | bytes 524320 | tf_op jit(solution)/shard_map/ppermute | solution.py:436
  44.2 0.0 copy-done.2
  44.2 0.0 copy-done.4
  44.2 0.0 copy-done.5
  44.2 7.6 %middle.1 = (f32[16,2,64,512]{3,2,1,0:T(8,128)}, f32[16,2,64,512]{3,2,1,0:T(8,128)S(1)}, f32[16,2,32,128]{3,2,1,0:T(8,128)S(1)}, f32[16,2,32,128]{3,2,1,0:T(8,128)S(1)}) custom-call(f32[16,2,64,512]{3,2,1,0:T(8,128)S(1)} %local_forward.1.local_ref, f32[16,2,64,512]{3,2,1,0:T(8,128)S(1)} %bitcast.7, ...), custom_call_target="tpu_custom_call" | custom-call | tf_op jit(solution)/shard_map/middle/pallas_call | solution.py:532
  51.8 0.1 collective-permute-start.8
  52.0 1.8 %collective-permute-done.8.refs_1_ = f32[16,2,32,128]{3,2,1,0:T(8,128)S(1)} collective-permute-done((f32[16,2,32,128]{3,2,1,0:T(8,128)S(1)}, f32[16,2,32,128]{3,2,1,0:T(8,128)S(1)}, u32[]{:S(2)}, u32[]{:S(2)}) %collective-permute-start.8) | collective-permute-done | bytes 524320 | tf_op jit(solution)/shard_map/ppermute | solution.py:436
  53.8 1.8 %collective-permute-start.9 = (f32[8,2,32,128]{3,2,1,0:T(8,128)S(1)}, f32[8,2,32,128]{3,2,1,0:T(8,128)S(1)}, u32[]{:S(2)}, u32[]{:S(2)}) collective-permute-start(f32[8,2,32,128]{3,2,1,0:T(8,128)S(1)} %slice_add_fusion), channel_id=1, source_target_pairs={{0,3},{1,4},{2,7},{3,0},{4,1},{5,6},{6,5},{7,2},{8,11},{9,12},{10,... | collective-permute-start | bytes 786440 | tf_op jit(solution)/shard_map/ppermute | solution.py:436
  55.6 2.1 %local_backward.1.local_ref = f32[16,2,64,512]{3,2,1,0:T(8,128)S(1)} custom-call(f32[16,2,64,512]{3,2,1,0:T(8,128)S(1)} %get-tuple-element.31.values, f32[64,64]{1,0:T(8,128)S(1)} %copy-done.6), custom_call_target="tpu_custom_call" | custom-call | tf_op jit(solution)/shard_map/local_backward/pallas_call | solution.py:543
  57.8 0.0 copy-start.3
  57.8 1.9 %collective-permute-done.9.refs_2_ = f32[8,2,32,128]{3,2,1,0:T(8,128)S(1)} collective-permute-done((f32[8,2,32,128]{3,2,1,0:T(8,128)S(1)}, f32[8,2,32,128]{3,2,1,0:T(8,128)S(1)}, u32[]{:S(2)}, u32[]{:S(2)}) %collective-permute-start.9) | collective-permute-done | bytes 262176 | tf_op jit(solution)/shard_map/ppermute | solution.py:436
  59.7 0.7 collective-permute-start.10
  60.4 3.8 %collective-permute-done.10.refs_3_ = f32[4,2,32,128]{3,2,1,0:T(8,128)S(1)} collective-permute-done((f32[4,2,32,128]{3,2,1,0:T(8,128)S(1)}, f32[4,2,32,128]{3,2,1,0:T(8,128)S(1)}, u32[]{:S(2)}, u32[]{:S(2)}) %collective-permute-start.10) | collective-permute-done | bytes 131104 | tf_op jit(solution)/shard_map/ppermute | solution.py:436
  64.2 1.9 %collective-permute-start.11 = (f32[2,2,32,128]{3,2,1,0:T(8,128)S(1)}, f32[2,2,32,128]{3,2,1,0:T(8,128)S(1)}, u32[]{:S(2)}, u32[]{:S(2)}) collective-permute-start(f32[2,2,32,128]{3,2,1,0:T(8,128)S(1)} %slice_add_fusion.4), channel_id=1, source_target_pairs={{0,9},{1,8},{2,11},{3,10},{4,13},{5,12},{6,15},{7,14},{8,1},{9,0},... | collective-permute-start | bytes 196616 | tf_op jit(solution)/shard_map/ppermute | solution.py:436
  66.0 4.6 %collective-permute-done.11.refs_4_ = f32[2,2,32,128]{3,2,1,0:T(8,128)S(1)} collective-permute-done((f32[2,2,32,128]{3,2,1,0:T(8,128)S(1)}, f32[2,2,32,128]{3,2,1,0:T(8,128)S(1)}, u32[]{:S(2)}, u32[]{:S(2)}) %collective-permute-start.11) | collective-permute-done | bytes 65568 | tf_op jit(solution)/shard_map/ppermute | solution.py:436
  70.6 2.0 %adjoint.1 = (f32[2,2,32,128]{3,2,1,0:T(8,128)S(1)}, f32[2,2,32,128]{3,2,1,0:T(8,128)S(1)}) custom-call(f32[16,2,32,128]{3,2,1,0:T(8,128)S(1)} %get-tuple-element.29.refs_0_, f32[16,2,32,128]{3,2,1,0:T(8,128)S(1)} %collective-permute-done.8.refs_1_, f32[8,2,32,128]{3,2,1,0:T(8,128)S(1)} %collective-permute-done.9.refs_2_, ...), custom_call_target="tpu_custom_call" | custom-call | tf_op jit(solution)/shard_map/adjoint/pallas_call | solution.py:553
  72.6 0.3 collective-permute-start.12
  73.0 6.2 %collective-permute-done.12 = f32[2,2,32,128]{3,2,1,0:T(8,128)S(1)} collective-permute-done((f32[2,2,32,128]{3,2,1,0:T(8,128)S(1)}, f32[2,2,32,128]{3,2,1,0:T(8,128)S(1)}, u32[]{:S(2)}, u32[]{:S(2)}) %collective-permute-start.12) | collective-permute-done | bytes 65568 | tf_op jit(solution)/shard_map/ppermute | solution.py:436
  79.2 0.1 collective-permute-start.13
  79.3 4.4 %collective-permute-done.13 = f32[4,2,32,128]{3,2,1,0:T(8,128)S(1)} collective-permute-done((f32[4,2,32,128]{3,2,1,0:T(8,128)S(1)}, f32[4,2,32,128]{3,2,1,0:T(8,128)S(1)}, u32[]{:S(2)}, u32[]{:S(2)}) %collective-permute-start.13) | collective-permute-done | bytes 131104 | tf_op jit(solution)/shard_map/ppermute | solution.py:436
  83.7 1.6 %collective-permute-start.14 = (f32[8,2,32,128]{3,2,1,0:T(8,128)S(1)}, f32[8,2,32,128]{3,2,1,0:T(8,128)S(1)}, u32[]{:S(2)}, u32[]{:S(2)}) collective-permute-start(f32[8,2,32,128]{3,2,1,0:T(8,128)S(1)} %pad_maximum_fusion.1), channel_id=1, source_target_pairs={{0,3},{1,4},{2,7},{3,0},{4,1},{5,6},{6,5},{7,2},{8,11},{9,12},{10,... | collective-permute-start | bytes 786440 | tf_op jit(solution)/shard_map/ppermute | solution.py:436
  85.3 3.0 %weight_grad.1 = f32[2,32,64,128]{3,2,1,0:T(8,128)} custom-call(f32[2,2,32,128]{3,2,1,0:T(8,128)S(1)} %get-tuple-element.35.modes_ref, f32[2,2,32,128]{3,2,1,0:T(8,128)S(1)} %get-tuple-element.36.dmixed_ref), custom_call_target="tpu_custom_call" | custom-call | tf_op jit(solution)/shard_map/weight_grad/pallas_call | solution.py:563
  88.3 1.2 %collective-permute-done.14 = f32[8,2,32,128]{3,2,1,0:T(8,128)S(1)} collective-permute-done((f32[8,2,32,128]{3,2,1,0:T(8,128)S(1)}, f32[8,2,32,128]{3,2,1,0:T(8,128)S(1)}, u32[]{:S(2)}, u32[]{:S(2)}) %collective-permute-start.14) | collective-permute-done | bytes 262176 | tf_op jit(solution)/shard_map/ppermute | solution.py:436
  89.5 0.3 collective-permute-start.15
  89.8 1.7 %collective-permute-done.15.back_ref = f32[16,2,32,128]{3,2,1,0:T(8,128)S(1)} collective-permute-done((f32[16,2,32,128]{3,2,1,0:T(8,128)S(1)}, f32[16,2,32,128]{3,2,1,0:T(8,128)S(1)}, u32[]{:S(2)}, u32[]{:S(2)}) %collective-permute-start.15) | collective-permute-done | bytes 524320 | tf_op jit(solution)/shard_map/ppermute | solution.py:436
  91.5 0.0 copy-done.3
  91.5 3.4 %input_grad.1 = f32[16,2,64,512]{3,2,1,0:T(8,128)} custom-call(f32[16,2,64,512]{3,2,1,0:T(8,128)S(1)} %local_backward.1.local_ref, f32[16,2,32,128]{3,2,1,0:T(8,128)S(1)} %constant_dynamic-update-slice_fusion.4.front_ref, f32[16,2,32,128]{3,2,1,0:T(8,128)S(1)} %collective-permute-done.15.back_ref, bf16[256,512]{1,0:T(8,128)(2,1)S(1)} %copy-done.3, ...), custom_call_target="tpu_custom_call" | custom-call | tf_op jit(solution)/shard_map/input_grad/pallas_call | solution.py:573
  (18 shorter events, 0.3 us)
Async XLA Ops:
  0.6 8.9 %copy-start = (f32[16,2,512,64]{2,3,1,0:T(8,128)S(1)}, f32[16,2,512,64]{2,3,1,0:T(8,128)}, u32[]{:S(2)}) copy-start(f32[16,2,512,64]{2,3,1,0:T(8,128)} %param.9) | copy-start | bytes 12582916
  0.6 8.9 %copy-start.6 = (f32[64,64]{1,0:T(8,128)S(1)}, f32[64,64]{1,0:T(8,128)}, u32[]{:S(2)}) copy-start(f32[64,64]{1,0:T(8,128)} %weight.1) | copy-start | bytes 49156
  0.7 8.9 %copy-start.7 = (f32[64]{0:T(128)S(1)}, f32[64]{0:T(128)}, u32[]{:S(2)}) copy-start(f32[64]{0:T(128)} %param.12) | copy-start | bytes 772
  4.7 2.1 %collective-permute-start = (f32[16,2,32,128]{3,2,1,0:T(8,128)S(1)}, f32[16,2,32,128]{3,2,1,0:T(8,128)S(1)}, u32[]{:S(2)}, u32[]{:S(2)}) collective-permute-start(f32[16,2,32,128]{3,2,1,0:T(8,128)S(1)} %get-tuple-element.22), channel_id=1, source_target_pairs={{0,1},{1,0},{2,3},{3,2},{4,5},{5,4},{6,7},{7,6},{8,9},{9,8},{10,11... | collective-permute-start | bytes 1572872 | tf_op jit(solution)/shard_map/ppermute | solution.py:436
  6.8 6.8 %collective-permute-start.1 = (f32[8,2,32,128]{3,2,1,0:T(8,128)S(1)}, f32[8,2,32,128]{3,2,1,0:T(8,128)S(1)}, u32[]{:S(2)}, u32[]{:S(2)}) collective-permute-start(f32[8,2,32,128]{3,2,1,0:T(8,128)S(1)} %slice_add_fusion.1), channel_id=1, source_target_pairs={{0,3},{1,4},{2,7},{3,0},{4,1},{5,6},{6,5},{7,2},{8,11},{9,12},{10,... | collective-permute-start | bytes 786440 | tf_op jit(solution)/shard_map/ppermute | solution.py:436
  9.5 13.6 %copy-start.1 = (f32[2,32,64,128]{3,2,1,0:T(8,128)S(1)}, f32[2,32,64,128]{3,2,1,0:T(8,128)}, u32[]{:S(2)}) copy-start(f32[2,32,64,128]{3,2,1,0:T(8,128)} %refs_5_.3) | copy-start | bytes 6291460
  12.0 32.3 %copy-start.2 = (f32[16,2,512,64]{2,3,1,0:T(8,128)S(1)}, f32[16,2,512,64]{2,3,1,0:T(8,128)}, u32[]{:S(2)}) copy-start(f32[16,2,512,64]{2,3,1,0:T(8,128)} %param.13) | copy-start | bytes 12582916
  12.0 32.3 %copy-start.4 = (bf16[256,512]{1,0:T(8,128)(2,1)S(1)}, bf16[256,512]{1,0:T(8,128)(2,1)}, u32[]{:S(2)}) copy-start(bf16[256,512]{1,0:T(8,128)(2,1)} %constant.11.clone.synth_ref) | copy-start | bytes 786436
  12.0 32.2 %copy-start.5 = (bf16[512,256]{1,0:T(8,128)(2,1)S(1)}, bf16[512,256]{1,0:T(8,128)(2,1)}, u32[]{:S(2)}) copy-start(bf16[512,256]{1,0:T(8,128)(2,1)} %constant.9.clone.table_ref) | copy-start | bytes 786436
  13.6 4.5 %collective-permute-start.2 = (f32[4,2,32,128]{3,2,1,0:T(8,128)S(1)}, f32[4,2,32,128]{3,2,1,0:T(8,128)S(1)}, u32[]{:S(2)}, u32[]{:S(2)}) collective-permute-start(f32[4,2,32,128]{3,2,1,0:T(8,128)S(1)} %fusion.1), channel_id=1, source_target_pairs={{0,5},{1,2},{2,1},{3,6},{4,7},{5,0},{6,3},{7,4},{8,13},{9,10},{10,... | collective-permute-start | bytes 393224 | tf_op jit(solution)/shard_map/ppermute | solution.py:436
  18.1 5.0 %collective-permute-start.3 = (f32[2,2,32,128]{3,2,1,0:T(8,128)S(1)}, f32[2,2,32,128]{3,2,1,0:T(8,128)S(1)}, u32[]{:S(2)}, u32[]{:S(2)}) collective-permute-start(f32[2,2,32,128]{3,2,1,0:T(8,128)S(1)} %slice_add_fusion.6), channel_id=1, source_target_pairs={{0,9},{1,8},{2,11},{3,10},{4,13},{5,12},{6,15},{7,14},{8,1},{9,0},... | collective-permute-start | bytes 196616 | tf_op jit(solution)/shard_map/ppermute | solution.py:436
  24.4 5.1 %collective-permute-start.4 = (f32[2,2,32,128]{3,2,1,0:T(8,128)S(1)}, f32[2,2,32,128]{3,2,1,0:T(8,128)S(1)}, u32[]{:S(2)}, u32[]{:S(2)}) collective-permute-start(f32[2,2,32,128]{3,2,1,0:T(8,128)S(1)} %get-tuple-element.25), channel_id=1, source_target_pairs={{0,9},{1,8},{2,11},{3,10},{4,13},{5,12},{6,15},{7,14},{8,1},{9,0},... | collective-permute-start | bytes 196616 | tf_op jit(solution)/shard_map/ppermute | solution.py:436
  29.6 5.7 %collective-permute-start.5 = (f32[4,2,32,128]{3,2,1,0:T(8,128)S(1)}, f32[4,2,32,128]{3,2,1,0:T(8,128)S(1)}, u32[]{:S(2)}, u32[]{:S(2)}) collective-permute-start(f32[4,2,32,128]{3,2,1,0:T(8,128)S(1)} %pad_maximum_fusion.2), channel_id=1, source_target_pairs={{0,5},{1,2},{2,1},{3,6},{4,7},{5,0},{6,3},{7,4},{8,13},{9,10},{10,... | collective-permute-start | bytes 393224 | tf_op jit(solution)/shard_map/ppermute | solution.py:436
  35.3 7.0 %collective-permute-start.6 = (f32[8,2,32,128]{3,2,1,0:T(8,128)S(1)}, f32[8,2,32,128]{3,2,1,0:T(8,128)S(1)}, u32[]{:S(2)}, u32[]{:S(2)}) collective-permute-start(f32[8,2,32,128]{3,2,1,0:T(8,128)S(1)} %pad_maximum_fusion), channel_id=1, source_target_pairs={{0,3},{1,4},{2,7},{3,0},{4,1},{5,6},{6,5},{7,2},{8,11},{9,12},{10,... | collective-permute-start | bytes 786440 | tf_op jit(solution)/shard_map/ppermute | solution.py:436
  42.3 2.0 %collective-permute-start.7 = (f32[16,2,32,128]{3,2,1,0:T(8,128)S(1)}, f32[16,2,32,128]{3,2,1,0:T(8,128)S(1)}, u32[]{:S(2)}, u32[]{:S(2)}) collective-permute-start(f32[16,2,32,128]{3,2,1,0:T(8,128)S(1)} %constant_dynamic-update-slice_fusion.front_ref), channel_id=1, source_target_pairs={{0,1},{1,0},{2,3},{3,2},{4,5},{5,4},{6,7},{7,6},{8,9},{9,8},{10,11... | collective-permute-start | bytes 1572872 | tf_op jit(solution)/shard_map/ppermute | solution.py:436
  51.8 1.9 %collective-permute-start.8 = (f32[16,2,32,128]{3,2,1,0:T(8,128)S(1)}, f32[16,2,32,128]{3,2,1,0:T(8,128)S(1)}, u32[]{:S(2)}, u32[]{:S(2)}) collective-permute-start(f32[16,2,32,128]{3,2,1,0:T(8,128)S(1)} %get-tuple-element.30), channel_id=1, source_target_pairs={{0,1},{1,0},{2,3},{3,2},{4,5},{5,4},{6,7},{7,6},{8,9},{9,8},{10,11... | collective-permute-start | bytes 1572872 | tf_op jit(solution)/shard_map/ppermute | solution.py:436
  53.8 5.9 %collective-permute-start.9 = (f32[8,2,32,128]{3,2,1,0:T(8,128)S(1)}, f32[8,2,32,128]{3,2,1,0:T(8,128)S(1)}, u32[]{:S(2)}, u32[]{:S(2)}) collective-permute-start(f32[8,2,32,128]{3,2,1,0:T(8,128)S(1)} %slice_add_fusion), channel_id=1, source_target_pairs={{0,3},{1,4},{2,7},{3,0},{4,1},{5,6},{6,5},{7,2},{8,11},{9,12},{10,... | collective-permute-start | bytes 786440 | tf_op jit(solution)/shard_map/ppermute | solution.py:436
  57.8 33.8 %copy-start.3 = (bf16[256,512]{1,0:T(8,128)(2,1)S(1)}, bf16[256,512]{1,0:T(8,128)(2,1)}, u32[]{:S(2)}) copy-start(bf16[256,512]{1,0:T(8,128)(2,1)} %constant.10.clone.synth_ref) | copy-start | bytes 786436
  59.7 4.5 %collective-permute-start.10 = (f32[4,2,32,128]{3,2,1,0:T(8,128)S(1)}, f32[4,2,32,128]{3,2,1,0:T(8,128)S(1)}, u32[]{:S(2)}, u32[]{:S(2)}) collective-permute-start(f32[4,2,32,128]{3,2,1,0:T(8,128)S(1)} %fusion), channel_id=1, source_target_pairs={{0,5},{1,2},{2,1},{3,6},{4,7},{5,0},{6,3},{7,4},{8,13},{9,10},{10,... | collective-permute-start | bytes 393224 | tf_op jit(solution)/shard_map/ppermute | solution.py:436
  64.2 6.4 %collective-permute-start.11 = (f32[2,2,32,128]{3,2,1,0:T(8,128)S(1)}, f32[2,2,32,128]{3,2,1,0:T(8,128)S(1)}, u32[]{:S(2)}, u32[]{:S(2)}) collective-permute-start(f32[2,2,32,128]{3,2,1,0:T(8,128)S(1)} %slice_add_fusion.4), channel_id=1, source_target_pairs={{0,9},{1,8},{2,11},{3,10},{4,13},{5,12},{6,15},{7,14},{8,1},{9,0},... | collective-permute-start | bytes 196616 | tf_op jit(solution)/shard_map/ppermute | solution.py:436
  72.6 6.5 %collective-permute-start.12 = (f32[2,2,32,128]{3,2,1,0:T(8,128)S(1)}, f32[2,2,32,128]{3,2,1,0:T(8,128)S(1)}, u32[]{:S(2)}, u32[]{:S(2)}) collective-permute-start(f32[2,2,32,128]{3,2,1,0:T(8,128)S(1)} %get-tuple-element.34), channel_id=1, source_target_pairs={{0,9},{1,8},{2,11},{3,10},{4,13},{5,12},{6,15},{7,14},{8,1},{9,0},... | collective-permute-start | bytes 196616 | tf_op jit(solution)/shard_map/ppermute | solution.py:436
  79.2 4.5 %collective-permute-start.13 = (f32[4,2,32,128]{3,2,1,0:T(8,128)S(1)}, f32[4,2,32,128]{3,2,1,0:T(8,128)S(1)}, u32[]{:S(2)}, u32[]{:S(2)}) collective-permute-start(f32[4,2,32,128]{3,2,1,0:T(8,128)S(1)} %pad_maximum_fusion.3), channel_id=1, source_target_pairs={{0,5},{1,2},{2,1},{3,6},{4,7},{5,0},{6,3},{7,4},{8,13},{9,10},{10,... | collective-permute-start | bytes 393224 | tf_op jit(solution)/shard_map/ppermute | solution.py:436
  83.7 5.9 %collective-permute-start.14 = (f32[8,2,32,128]{3,2,1,0:T(8,128)S(1)}, f32[8,2,32,128]{3,2,1,0:T(8,128)S(1)}, u32[]{:S(2)}, u32[]{:S(2)}) collective-permute-start(f32[8,2,32,128]{3,2,1,0:T(8,128)S(1)} %pad_maximum_fusion.1), channel_id=1, source_target_pairs={{0,3},{1,4},{2,7},{3,0},{4,1},{5,6},{6,5},{7,2},{8,11},{9,12},{10,... | collective-permute-start | bytes 786440 | tf_op jit(solution)/shard_map/ppermute | solution.py:436
  89.5 2.0 %collective-permute-start.15 = (f32[16,2,32,128]{3,2,1,0:T(8,128)S(1)}, f32[16,2,32,128]{3,2,1,0:T(8,128)S(1)}, u32[]{:S(2)}, u32[]{:S(2)}) collective-permute-start(f32[16,2,32,128]{3,2,1,0:T(8,128)S(1)} %constant_dynamic-update-slice_fusion.4.front_ref), channel_id=1, source_target_pairs={{0,1},{1,0},{2,3},{3,2},{4,5},{5,4},{6,7},{7,6},{8,9},{9,8},{10,11... | collective-permute-start | bytes 1572872 | tf_op jit(solution)/shard_map/ppermute | solution.py:436

commit v4 on v3

--- a/solution.py
+++ b/solution.py
@@ -45,19 +45,8 @@
 def stage_masks():
     count = lax.axis_size("stream")
     bits = count.bit_length() - 1
-    assert 1 << bits == count
-    return [1] + [1 << i | 1 for i in range(1, bits)]
-
-
-def stage_class(index):
-    return (index ^ index >> 1 ^ index >> 2) & 1
-
-
-def stage_mask(index, step):
-    masks = stage_masks()
-    if len(masks) > 2 and step in (1, 2) and stage_class(index):
-        step = 3 - step
-    return masks[step]
+    assert 1 << bits == count and bits >= 3
+    return [1, 4, 2] + [1 << i for i in range(3, bits)]
 
 
 def mode_angles(position, inner, cell, owned, total_modes, cells):
@@ -67,12 +56,6 @@
     length = cells * (1 << steps)
     assert length & (length - 1) == 0
     bits = [position >> (steps - 1 - step) & 1 for step in range(steps)]
-    if steps > 2:
-        other = (bits[0] ^ stage_class(me)) & 1
-        bits[1], bits[2] = (
-            jnp.where(other == 1, bits[2], bits[1]),
-            jnp.where(other == 1, bits[1], bits[2]),
-        )
     block = jnp.zeros_like(position) + me
     for bit, mask in zip(bits, masks):
         block = block ^ bit * mask
@@ -431,39 +414,43 @@
         copy.wait()
 
 
-def swap(values, step):
+def swap(values, mask):
     count = lax.axis_size("stream")
-    return lax.ppermute(values, "stream", [(i, i ^ stage_mask(i, step)) for i in range(count)])
-
-
-def beside(first, second):
-    return lax.optimization_barrier((first, second))
+    return lax.ppermute(values, "stream", [(i, i ^ mask) for i in range(count)])
+
+
+def beside(moved, work):
+    return lax.optimization_barrier((moved, work()))
 
 
 def scatter_sum(keep, send, work):
-    pieces = [keep, swap(send, 0)]
-    half = keep.shape[0]
+    pieces = [keep, swap(send, 1)]
+
+    def part(first, count):
+        total = pieces[0][first : first + count]
+        for piece in pieces[1:]:
+            total = total + piece[first : first + count]
+        return total
+
+    quarter = keep.shape[0] // 4
+    moved = [swap(part(quarter * place, quarter), 2 * place) for place in (2, 3, 1)]
+    moved, done = beside(moved, work)
+    pieces += moved
+    for mask in stage_masks()[3:]:
+        quarter //= 2
+        pieces.append(swap(part(quarter, quarter), mask))
+    return pieces, done
+
+
+def gather_all(values, work=None):
+    for mask in reversed(stage_masks()[3:]):
+        values = jnp.concatenate([values, swap(values, mask)], axis=0)
+    moved = [swap(values, 2 * place) for place in (3, 2, 1)]
     done = None
-    for step in range(1, len(stage_masks())):
-        half //= 2
-        part = pieces[0][half : 2 * half]
-        for piece in pieces[1:]:
-            part = part + piece[half : 2 * half]
-        moved = swap(part, step)
-        if step == 1:
-            moved, done = beside(moved, work())
-        pieces.append(moved)
-    return pieces, done
-
-
-def gather_all(values, work=None):
-    done = None
-    for step in reversed(range(1, len(stage_masks()))):
-        moved = swap(values, step)
-        if step == 1 and work is not None:
-            moved, done = beside(moved, work())
-        values = jnp.concatenate([values, moved], axis=0)
-    return values, swap(values, 0), done
+    if work is not None:
+        moved, done = beside(moved, work)
+    values = jnp.concatenate([values] + moved[::-1], axis=0)
+    return values, swap(values, 1), done
 
 
 def params():

time: 95.2 us -> 87 us (0.914)
  waiting for transfers between devices: 44.1 us -> 32.5 us
  starting transfers between devices: 23.6 us -> 27.1 us
    ppermute x16 -> x20, waiting for transfers between devices: 44.1 us -> 32.5 us  [swap(): return lax.ppermute(values, 'stream', [(i, i ^ mask) for i in range(count)])]
    ppermute x16 -> x20, starting transfers between devices: 23.6 us -> 27.1 us  [swap(): return lax.ppermute(values, 'stream', [(i, i ^ mask) for i in range(count)])]
  transfers between devices with their start and end apart: 16 -> 20, of which waited for: 16 -> 17; matrix products, arithmetic and copies ran while one was open for 0% -> 0% of each run, Pallas kernels for 8% -> 9%
where the time goes in v4:
time: 87 us; the launch traced here: 86.9 us
  waiting for transfers between devices  32.5 us (37%)
  starting transfers between devices  27.1 us (31%)
  Pallas kernels  26 us (30%)
  between operations  0.98 us (1%)
    ppermute x20, waiting for transfers between devices, swap(): return lax.ppermute(values, 'stream', [(i, i ^ mask) for i in range(count)])  32.5 us
    ppermute x20, starting transfers between devices, swap(): return lax.ppermute(values, 'stream', [(i, i ^ mask) for i in range(count)])  27.1 us
    pallas_call x1, Pallas kernels, per_device(): pl.pallas_call(middle_kernel, in_specs=[here] * 8, out_specs=[here] * 4,...  7.6 us
    pallas_call x1, Pallas kernels, per_device(): pl.pallas_call(functools.partial(spanwise_kernel, (owned, total_modes, ce...  4.04 us
    pallas_call x1, Pallas kernels, per_device(): pl.pallas_call(input_grad_kernel, in_specs=[here] * 5, out_specs=apart, o...  3.37 us
    pallas_call x1, Pallas kernels, weight_grad(): pl.pallas_call(weight_grad_kernel, in_specs=[here] * 2, out_specs=here, o...  3.05 us
    pallas_call x1, Pallas kernels, local_forward(): pl.pallas_call(functools.partial(pointwise_kernel, True), in_specs=[here]...  2.46 us
    pallas_call x1, Pallas kernels, local_backward(): pl.pallas_call(lambda values, weight, out: pointwise_kernel(False, values...  2.15 us
  transfers between devices with their start and end apart: 20, of which 17 were waited for; matrix products, arithmetic and copies ran while one was open for 0% of the time, Pallas kernels for 9%

profile of v4, /device:TPU:0, one launch (start us, length us, event | category | flops | bytes accessed | tf_op | source)
XLA Modules:
  0.0 86.9 jit_solution(5389859600358511398)
XLA Ops:
  0.6 0.0 copy-start
  0.6 0.0 copy-start.6
  0.7 0.0 copy-start.7
  0.7 4.0 %spanwise.1 = (f32[16,2,32,128]{3,2,1,0:T(8,128)S(1)}, f32[16,2,32,128]{3,2,1,0:T(8,128)S(1)}, bf16[2,256,256]{2,1,0:T(8,128)(2,1)S(1)}, bf16[2,256,256]{2,1,0:T(8,128)(2,1)S(1)}) custom-call(f32[16,2,64,512]{3,2,1,0:T(8,128)} %bitcast.5, bf16[512,256]{1,0:T(8,128)(2,1)} %constant.8.clone.table_hbm), custom_call_target="tpu_custom_call" | custom-call | tf_op jit(solution)/shard_map/spanwise/pallas_call | solution.py:489
  4.7 0.5 collective-permute-start
  5.2 1.5 %collective-permute-done.refs_1_ = f32[16,2,32,128]{3,2,1,0:T(8,128)S(1)} collective-permute-done((f32[16,2,32,128]{3,2,1,0:T(8,128)S(1)}, f32[16,2,32,128]{3,2,1,0:T(8,128)S(1)}, u32[]{:S(2)}, u32[]{:S(2)}) %collective-permute-start) | collective-permute-done | bytes 524320 | tf_op jit(solution)/shard_map/ppermute | solution.py:419
  6.8 0.1 slice_add_fusion.3
  6.8 3.0 %collective-permute-start.3 = (f32[4,2,32,128]{3,2,1,0:T(8,128)S(1)}, f32[4,2,32,128]{3,2,1,0:T(8,128)S(1)}, u32[]{:S(2)}, u32[]{:S(2)}) collective-permute-start(f32[4,2,32,128]{3,2,1,0:T(8,128)S(1)} %get-tuple-element.54), channel_id=1, source_target_pairs={{0,2},{1,3},{2,0},{3,1},{4,6},{5,7},{6,4},{7,5},{8,10},{9,11},{10,... | collective-permute-start | bytes 393224 | tf_op jit(solution)/shard_map/ppermute | solution.py:419
  9.8 1.5 %collective-permute-start.2 = (f32[4,2,32,128]{3,2,1,0:T(8,128)S(1)}, f32[4,2,32,128]{3,2,1,0:T(8,128)S(1)}, u32[]{:S(2)}, u32[]{:S(2)}) collective-permute-start(f32[4,2,32,128]{3,2,1,0:T(8,128)S(1)} %get-tuple-element.55), channel_id=1, source_target_pairs={{0,6},{1,7},{2,4},{3,5},{4,2},{5,3},{6,0},{7,1},{8,14},{9,15},{10,... | collective-permute-start | bytes 393224 | tf_op jit(solution)/shard_map/ppermute | solution.py:419
  11.3 0.1 collective-permute-start.1
  11.4 0.0 copy-done
  11.4 0.0 copy-done.6
  11.4 0.0 copy-done.7
  11.4 2.5 %local_forward.1.local_ref = f32[16,2,64,512]{3,2,1,0:T(8,128)S(1)} custom-call(f32[16,2,64,512]{3,2,1,0:T(8,128)S(1)} %bitcast.6, f32[64,64]{1,0:T(8,128)S(1)} %copy-done.6, f32[1,64]{1,0:T(1,128)S(1)} %bitcast.8), custom_call_target="tpu_custom_call" | custom-call | tf_op jit(solution)/shard_map/local_forward/pallas_call | solution.py:500
  13.8 0.0 copy-start.2
  13.8 0.0 copy-start.4
  13.9 0.0 copy-start.5
  13.9 1.8 %collective-permute-done.3.refs_4_ = f32[4,2,32,128]{3,2,1,0:T(8,128)S(1)} collective-permute-done((f32[4,2,32,128]{3,2,1,0:T(8,128)S(1)}, f32[4,2,32,128]{3,2,1,0:T(8,128)S(1)}, u32[]{:S(2)}, u32[]{:S(2)}) %collective-permute-start.3) | collective-permute-done | bytes 131104 | tf_op jit(solution)/shard_map/ppermute | solution.py:419
  15.7 1.4 %collective-permute-done.2.refs_3_ = f32[4,2,32,128]{3,2,1,0:T(8,128)S(1)} collective-permute-done((f32[4,2,32,128]{3,2,1,0:T(8,128)S(1)}, f32[4,2,32,128]{3,2,1,0:T(8,128)S(1)}, u32[]{:S(2)}, u32[]{:S(2)}) %collective-permute-start.2) | collective-permute-done | bytes 131104 | tf_op jit(solution)/shard_map/ppermute | solution.py:419
  17.1 0.7 collective-permute-done.1.refs_2_
  17.7 2.8 %collective-permute-start.4 = (f32[2,2,32,128]{3,2,1,0:T(8,128)S(1)}, f32[2,2,32,128]{3,2,1,0:T(8,128)S(1)}, u32[]{:S(2)}, u32[]{:S(2)}) collective-permute-start(f32[2,2,32,128]{3,2,1,0:T(8,128)S(1)} %fusion.5), channel_id=1, source_target_pairs={{0,8},{1,9},{2,10},{3,11},{4,12},{5,13},{6,14},{7,15},{8,0},{9,1},... | collective-permute-start | bytes 196616 | tf_op jit(solution)/shard_map/ppermute | solution.py:419
  20.5 2.5 %collective-permute-done.4.refs_5_ = f32[2,2,32,128]{3,2,1,0:T(8,128)S(1)} collective-permute-done((f32[2,2,32,128]{3,2,1,0:T(8,128)S(1)}, f32[2,2,32,128]{3,2,1,0:T(8,128)S(1)}, u32[]{:S(2)}, u32[]{:S(2)}) %collective-permute-start.4) | collective-permute-done | bytes 65568 | tf_op jit(solution)/shard_map/ppermute | solution.py:419
  23.0 0.0 copy-done.1
  23.0 1.3 %mix.1 = (f32[2,2,32,128]{3,2,1,0:T(8,128)S(1)}, f32[2,2,32,128]{3,2,1,0:T(8,128)S(1)}) custom-call(f32[16,2,32,128]{3,2,1,0:T(8,128)S(1)} %get-tuple-element.27.refs_0_, f32[16,2,32,128]{3,2,1,0:T(8,128)S(1)} %collective-permute-done.refs_1_, f32[4,2,32,128]{3,2,1,0:T(8,128)S(1)} %collective-permute-done.1.refs_2_, ...), custom_call_target="tpu_custom_call" | custom-call | tf_op jit(solution)/shard_map/mix/pallas_call | solution.py:510
  24.3 2.8 %collective-permute-start.5 = (f32[2,2,32,128]{3,2,1,0:T(8,128)S(1)}, f32[2,2,32,128]{3,2,1,0:T(8,128)S(1)}, u32[]{:S(2)}, u32[]{:S(2)}) collective-permute-start(f32[2,2,32,128]{3,2,1,0:T(8,128)S(1)} %get-tuple-element.33), channel_id=1, source_target_pairs={{0,8},{1,9},{2,10},{3,11},{4,12},{5,13},{6,14},{7,15},{8,0},{9,1},... | collective-permute-start | bytes 196616 | tf_op jit(solution)/shard_map/ppermute | solution.py:419
  27.1 2.4 %collective-permute-done.5 = f32[2,2,32,128]{3,2,1,0:T(8,128)S(1)} collective-permute-done((f32[2,2,32,128]{3,2,1,0:T(8,128)S(1)}, f32[2,2,32,128]{3,2,1,0:T(8,128)S(1)}, u32[]{:S(2)}, u32[]{:S(2)}) %collective-permute-start.5) | collective-permute-done | bytes 65568 | tf_op jit(solution)/shard_map/ppermute | solution.py:419
  29.5 1.7 %collective-permute-start.6 = (f32[4,2,32,128]{3,2,1,0:T(8,128)S(1)}, f32[4,2,32,128]{3,2,1,0:T(8,128)S(1)}, u32[]{:S(2)}, u32[]{:S(2)}) collective-permute-start(f32[4,2,32,128]{3,2,1,0:T(8,128)S(1)} %get-tuple-element.61), channel_id=1, source_target_pairs={{0,2},{1,3},{2,0},{3,1},{4,6},{5,7},{6,4},{7,5},{8,10},{9,11},{10,... | collective-permute-start | bytes 393224 | tf_op jit(solution)/shard_map/ppermute | solution.py:419
  31.2 1.8 %collective-permute-start.7 = (f32[4,2,32,128]{3,2,1,0:T(8,128)S(1)}, f32[4,2,32,128]{3,2,1,0:T(8,128)S(1)}, u32[]{:S(2)}, u32[]{:S(2)}) collective-permute-start(f32[4,2,32,128]{3,2,1,0:T(8,128)S(1)} %get-tuple-element.61), channel_id=1, source_target_pairs={{0,4},{1,5},{2,6},{3,7},{4,0},{5,1},{6,2},{7,3},{8,12},{9,13},{10,... | collective-permute-start | bytes 393224 | tf_op jit(solution)/shard_map/ppermute | solution.py:419
  33.1 0.0 collective-permute-start.8
  33.1 2.7 %collective-permute-done.6 = f32[4,2,32,128]{3,2,1,0:T(8,128)S(1)} collective-permute-done((f32[4,2,32,128]{3,2,1,0:T(8,128)S(1)}, f32[4,2,32,128]{3,2,1,0:T(8,128)S(1)}, u32[]{:S(2)}, u32[]{:S(2)}) %collective-permute-start.6) | collective-permute-done | bytes 131104 | tf_op jit(solution)/shard_map/ppermute | solution.py:419
  35.8 0.4 collective-permute-done.7
  36.2 2.7 %collective-permute-done.8 = f32[4,2,32,128]{3,2,1,0:T(8,128)S(1)} collective-permute-done((f32[4,2,32,128]{3,2,1,0:T(8,128)S(1)}, f32[4,2,32,128]{3,2,1,0:T(8,128)S(1)}, u32[]{:S(2)}, u32[]{:S(2)}) %collective-permute-start.8) | collective-permute-done | bytes 131104 | tf_op jit(solution)/shard_map/ppermute | solution.py:419
  38.9 0.1 collective-permute-start.9
  39.0 1.9 %collective-permute-done.9.back_ref = f32[16,2,32,128]{3,2,1,0:T(8,128)S(1)} collective-permute-done((f32[16,2,32,128]{3,2,1,0:T(8,128)S(1)}, f32[16,2,32,128]{3,2,1,0:T(8,128)S(1)}, u32[]{:S(2)}, u32[]{:S(2)}) %collective-permute-start.9) | collective-permute-done | bytes 524320 | tf_op jit(solution)/shard_map/ppermute | solution.py:419
  40.9 0.0 copy-done.2
  40.9 0.0 copy-done.4
  40.9 0.0 copy-done.5
  40.9 7.6 %middle.1 = (f32[16,2,64,512]{3,2,1,0:T(8,128)}, f32[16,2,64,512]{3,2,1,0:T(8,128)S(1)}, f32[16,2,32,128]{3,2,1,0:T(8,128)S(1)}, f32[16,2,32,128]{3,2,1,0:T(8,128)S(1)}) custom-call(f32[16,2,64,512]{3,2,1,0:T(8,128)S(1)} %local_forward.1.local_ref, f32[16,2,64,512]{3,2,1,0:T(8,128)S(1)} %bitcast.7, ...), custom_call_target="tpu_custom_call" | custom-call | tf_op jit(solution)/shard_map/middle/pallas_call | solution.py:519
  48.5 0.1 collective-permute-start.10
  48.7 1.8 %collective-permute-done.10.refs_1_ = f32[16,2,32,128]{3,2,1,0:T(8,128)S(1)} collective-permute-done((f32[16,2,32,128]{3,2,1,0:T(8,128)S(1)}, f32[16,2,32,128]{3,2,1,0:T(8,128)S(1)}, u32[]{:S(2)}, u32[]{:S(2)}) %collective-permute-start.10) | collective-permute-done | bytes 524320 | tf_op jit(solution)/shard_map/ppermute | solution.py:419
  50.4 0.1 slice_add_fusion
  50.5 0.6 collective-permute-start.13
  51.1 1.4 %collective-permute-start.12 = (f32[4,2,32,128]{3,2,1,0:T(8,128)S(1)}, f32[4,2,32,128]{3,2,1,0:T(8,128)S(1)}, u32[]{:S(2)}, u32[]{:S(2)}) collective-permute-start(f32[4,2,32,128]{3,2,1,0:T(8,128)S(1)} %get-tuple-element.52), channel_id=1, source_target_pairs={{0,6},{1,7},{2,4},{3,5},{4,2},{5,3},{6,0},{7,1},{8,14},{9,15},{10,... | collective-permute-start | bytes 393224 | tf_op jit(solution)/shard_map/ppermute | solution.py:419
  52.5 1.6 %collective-permute-start.11 = (f32[4,2,32,128]{3,2,1,0:T(8,128)S(1)}, f32[4,2,32,128]{3,2,1,0:T(8,128)S(1)}, u32[]{:S(2)}, u32[]{:S(2)}) collective-permute-start(f32[4,2,32,128]{3,2,1,0:T(8,128)S(1)} %get-tuple-element.53), channel_id=1, source_target_pairs={{0,4},{1,5},{2,6},{3,7},{4,0},{5,1},{6,2},{7,3},{8,12},{9,13},{10,... | collective-permute-start | bytes 393224 | tf_op jit(solution)/shard_map/ppermute | solution.py:419
  54.0 2.2 %local_backward.1.local_ref = f32[16,2,64,512]{3,2,1,0:T(8,128)S(1)} custom-call(f32[16,2,64,512]{3,2,1,0:T(8,128)S(1)} %get-tuple-element.39.values, f32[64,64]{1,0:T(8,128)S(1)} %copy-done.6), custom_call_target="tpu_custom_call" | custom-call | tf_op jit(solution)/shard_map/local_backward/pallas_call | solution.py:530
  56.2 0.0 copy-start.3
  56.2 2.7 %collective-permute-done.13.refs_4_ = f32[4,2,32,128]{3,2,1,0:T(8,128)S(1)} collective-permute-done((f32[4,2,32,128]{3,2,1,0:T(8,128)S(1)}, f32[4,2,32,128]{3,2,1,0:T(8,128)S(1)}, u32[]{:S(2)}, u32[]{:S(2)}) %collective-permute-start.13) | collective-permute-done | bytes 131104 | tf_op jit(solution)/shard_map/ppermute | solution.py:419
  58.9 0.0 collective-permute-done.12.refs_3_
  58.9 1.2 %collective-permute-done.11.refs_2_ = f32[4,2,32,128]{3,2,1,0:T(8,128)S(1)} collective-permute-done((f32[4,2,32,128]{3,2,1,0:T(8,128)S(1)}, f32[4,2,32,128]{3,2,1,0:T(8,128)S(1)}, u32[]{:S(2)}, u32[]{:S(2)}) %collective-permute-start.11) | collective-permute-done | bytes 131104 | tf_op jit(solution)/shard_map/ppermute | solution.py:419
  60.2 3.1 %collective-permute-start.14 = (f32[2,2,32,128]{3,2,1,0:T(8,128)S(1)}, f32[2,2,32,128]{3,2,1,0:T(8,128)S(1)}, u32[]{:S(2)}, u32[]{:S(2)}) collective-permute-start(f32[2,2,32,128]{3,2,1,0:T(8,128)S(1)} %fusion.2), channel_id=1, source_target_pairs={{0,8},{1,9},{2,10},{3,11},{4,12},{5,13},{6,14},{7,15},{8,0},{9,1},... | collective-permute-start | bytes 196616 | tf_op jit(solution)/shard_map/ppermute | solution.py:419
  63.2 2.8 %collective-permute-done.14.refs_5_ = f32[2,2,32,128]{3,2,1,0:T(8,128)S(1)} collective-permute-done((f32[2,2,32,128]{3,2,1,0:T(8,128)S(1)}, f32[2,2,32,128]{3,2,1,0:T(8,128)S(1)}, u32[]{:S(2)}, u32[]{:S(2)}) %collective-permute-start.14) | collective-permute-done | bytes 65568 | tf_op jit(solution)/shard_map/ppermute | solution.py:419
  66.0 2.0 %adjoint.1 = (f32[2,2,32,128]{3,2,1,0:T(8,128)S(1)}, f32[2,2,32,128]{3,2,1,0:T(8,128)S(1)}) custom-call(f32[16,2,32,128]{3,2,1,0:T(8,128)S(1)} %get-tuple-element.37.refs_0_, f32[16,2,32,128]{3,2,1,0:T(8,128)S(1)} %collective-permute-done.10.refs_1_, f32[4,2,32,128]{3,2,1,0:T(8,128)S(1)} %collective-permute-done.11.refs_2_, ...), custom_call_target="tpu_custom_call" | custom-call | tf_op jit(solution)/shard_map/adjoint/pallas_call | solution.py:540
  68.1 2.4 %collective-permute-start.15 = (f32[2,2,32,128]{3,2,1,0:T(8,128)S(1)}, f32[2,2,32,128]{3,2,1,0:T(8,128)S(1)}, u32[]{:S(2)}, u32[]{:S(2)}) collective-permute-start(f32[2,2,32,128]{3,2,1,0:T(8,128)S(1)} %get-tuple-element.44), channel_id=1, source_target_pairs={{0,8},{1,9},{2,10},{3,11},{4,12},{5,13},{6,14},{7,15},{8,0},{9,1},... | collective-permute-start | bytes 196616 | tf_op jit(solution)/shard_map/ppermute | solution.py:419
  70.5 2.9 %collective-permute-done.15 = f32[2,2,32,128]{3,2,1,0:T(8,128)S(1)} collective-permute-done((f32[2,2,32,128]{3,2,1,0:T(8,128)S(1)}, f32[2,2,32,128]{3,2,1,0:T(8,128)S(1)}, u32[]{:S(2)}, u32[]{:S(2)}) %collective-permute-start.15) | collective-permute-done | bytes 65568 | tf_op jit(solution)/shard_map/ppermute | solution.py:419
  73.4 0.1 collective-permute-start.18
  73.4 2.0 %collective-permute-start.17 = (f32[4,2,32,128]{3,2,1,0:T(8,128)S(1)}, f32[4,2,32,128]{3,2,1,0:T(8,128)S(1)}, u32[]{:S(2)}, u32[]{:S(2)}) collective-permute-start(f32[4,2,32,128]{3,2,1,0:T(8,128)S(1)} %get-tuple-element.57), channel_id=1, source_target_pairs={{0,4},{1,5},{2,6},{3,7},{4,0},{5,1},{6,2},{7,3},{8,12},{9,13},{10,... | collective-permute-start | bytes 393224 | tf_op jit(solution)/shard_map/ppermute | solution.py:419
  75.4 1.5 %collective-permute-start.16 = (f32[4,2,32,128]{3,2,1,0:T(8,128)S(1)}, f32[4,2,32,128]{3,2,1,0:T(8,128)S(1)}, u32[]{:S(2)}, u32[]{:S(2)}) collective-permute-start(f32[4,2,32,128]{3,2,1,0:T(8,128)S(1)} %get-tuple-element.57), channel_id=1, source_target_pairs={{0,6},{1,7},{2,4},{3,5},{4,2},{5,3},{6,0},{7,1},{8,14},{9,15},{10,... | collective-permute-start | bytes 393224 | tf_op jit(solution)/shard_map/ppermute | solution.py:419
  76.9 3.0 %weight_grad.1 = f32[2,32,64,128]{3,2,1,0:T(8,128)} custom-call(f32[2,2,32,128]{3,2,1,0:T(8,128)S(1)} %get-tuple-element.45.modes_ref, f32[2,2,32,128]{3,2,1,0:T(8,128)S(1)} %get-tuple-element.46.dmixed_ref), custom_call_target="tpu_custom_call" | custom-call | tf_op jit(solution)/shard_map/weight_grad/pallas_call | solution.py:550
  80.0 0.0 collective-permute-done.18
  80.0 0.0 collective-permute-done.17
  80.0 1.3 %collective-permute-done.16 = f32[4,2,32,128]{3,2,1,0:T(8,128)S(1)} collective-permute-done((f32[4,2,32,128]{3,2,1,0:T(8,128)S(1)}, f32[4,2,32,128]{3,2,1,0:T(8,128)S(1)}, u32[]{:S(2)}, u32[]{:S(2)}) %collective-permute-start.16) | collective-permute-done | bytes 131104 | tf_op jit(solution)/shard_map/ppermute | solution.py:419
  81.4 0.1 collective-permute-start.19
  81.4 1.9 %collective-permute-done.19.back_ref = f32[16,2,32,128]{3,2,1,0:T(8,128)S(1)} collective-permute-done((f32[16,2,32,128]{3,2,1,0:T(8,128)S(1)}, f32[16,2,32,128]{3,2,1,0:T(8,128)S(1)}, u32[]{:S(2)}, u32[]{:S(2)}) %collective-permute-start.19) | collective-permute-done | bytes 524320 | tf_op jit(solution)/shard_map/ppermute | solution.py:419
  83.3 3.4 %input_grad.1 = f32[16,2,64,512]{3,2,1,0:T(8,128)} custom-call(f32[16,2,64,512]{3,2,1,0:T(8,128)S(1)} %local_backward.1.local_ref, f32[16,2,32,128]{3,2,1,0:T(8,128)S(1)} %constant_dynamic-update-slice_fusion.9.front_ref, f32[16,2,32,128]{3,2,1,0:T(8,128)S(1)} %collective-permute-done.19.back_ref, bf16[256,512]{1,0:T(8,128)(2,1)S(1)} %copy-done.3, ...), custom_call_target="tpu_custom_call" | custom-call | tf_op jit(solution)/shard_map/input_grad/pallas_call | solution.py:560
  (14 shorter events, 0.2 us)
Async XLA Ops:
  0.6 10.7 %copy-start = (f32[16,2,512,64]{2,3,1,0:T(8,128)S(1)}, f32[16,2,512,64]{2,3,1,0:T(8,128)}, u32[]{:S(2)}) copy-start(f32[16,2,512,64]{2,3,1,0:T(8,128)} %param.9) | copy-start | bytes 12582916
  0.6 10.7 %copy-start.6 = (f32[64,64]{1,0:T(8,128)S(1)}, f32[64,64]{1,0:T(8,128)}, u32[]{:S(2)}) copy-start(f32[64,64]{1,0:T(8,128)} %weight.1) | copy-start | bytes 49156
  0.7 10.7 %copy-start.7 = (f32[64]{0:T(128)S(1)}, f32[64]{0:T(128)}, u32[]{:S(2)}) copy-start(f32[64]{0:T(128)} %param.12) | copy-start | bytes 772
  4.7 2.1 %collective-permute-start = (f32[16,2,32,128]{3,2,1,0:T(8,128)S(1)}, f32[16,2,32,128]{3,2,1,0:T(8,128)S(1)}, u32[]{:S(2)}, u32[]{:S(2)}) collective-permute-start(f32[16,2,32,128]{3,2,1,0:T(8,128)S(1)} %get-tuple-element.28), channel_id=1, source_target_pairs={{0,1},{1,0},{2,3},{3,2},{4,5},{5,4},{6,7},{7,6},{8,9},{9,8},{10,11... | collective-permute-start | bytes 1572872 | tf_op jit(solution)/shard_map/ppermute | solution.py:419
  6.8 8.9 %collective-permute-start.3 = (f32[4,2,32,128]{3,2,1,0:T(8,128)S(1)}, f32[4,2,32,128]{3,2,1,0:T(8,128)S(1)}, u32[]{:S(2)}, u32[]{:S(2)}) collective-permute-start(f32[4,2,32,128]{3,2,1,0:T(8,128)S(1)} %get-tuple-element.54), channel_id=1, source_target_pairs={{0,2},{1,3},{2,0},{3,1},{4,6},{5,7},{6,4},{7,5},{8,10},{9,11},{10,... | collective-permute-start | bytes 393224 | tf_op jit(solution)/shard_map/ppermute | solution.py:419
  9.8 7.3 %collective-permute-start.2 = (f32[4,2,32,128]{3,2,1,0:T(8,128)S(1)}, f32[4,2,32,128]{3,2,1,0:T(8,128)S(1)}, u32[]{:S(2)}, u32[]{:S(2)}) collective-permute-start(f32[4,2,32,128]{3,2,1,0:T(8,128)S(1)} %get-tuple-element.55), channel_id=1, source_target_pairs={{0,6},{1,7},{2,4},{3,5},{4,2},{5,3},{6,0},{7,1},{8,14},{9,15},{10,... | collective-permute-start | bytes 393224 | tf_op jit(solution)/shard_map/ppermute | solution.py:419
  11.3 6.4 %collective-permute-start.1 = (f32[4,2,32,128]{3,2,1,0:T(8,128)S(1)}, f32[4,2,32,128]{3,2,1,0:T(8,128)S(1)}, u32[]{:S(2)}, u32[]{:S(2)}) collective-permute-start(f32[4,2,32,128]{3,2,1,0:T(8,128)S(1)} %get-tuple-element.56), channel_id=1, source_target_pairs={{0,4},{1,5},{2,6},{3,7},{4,0},{5,1},{6,2},{7,3},{8,12},{9,13},{10,... | collective-permute-start | bytes 393224 | tf_op jit(solution)/shard_map/ppermute | solution.py:419
  11.4 11.6 %copy-start.1 = (f32[2,32,64,128]{3,2,1,0:T(8,128)S(1)}, f32[2,32,64,128]{3,2,1,0:T(8,128)}, u32[]{:S(2)}) copy-start(f32[2,32,64,128]{3,2,1,0:T(8,128)} %refs_6_.3) | copy-start | bytes 6291460
  13.8 27.1 %copy-start.2 = (f32[16,2,512,64]{2,3,1,0:T(8,128)S(1)}, f32[16,2,512,64]{2,3,1,0:T(8,128)}, u32[]{:S(2)}) copy-start(f32[16,2,512,64]{2,3,1,0:T(8,128)} %param.13) | copy-start | bytes 12582916
  13.8 27.1 %copy-start.4 = (bf16[256,512]{1,0:T(8,128)(2,1)S(1)}, bf16[256,512]{1,0:T(8,128)(2,1)}, u32[]{:S(2)}) copy-start(bf16[256,512]{1,0:T(8,128)(2,1)} %constant.11.clone.synth_ref) | copy-start | bytes 786436
  13.9 27.1 %copy-start.5 = (bf16[512,256]{1,0:T(8,128)(2,1)S(1)}, bf16[512,256]{1,0:T(8,128)(2,1)}, u32[]{:S(2)}) copy-start(bf16[512,256]{1,0:T(8,128)(2,1)} %constant.9.clone.table_ref) | copy-start | bytes 786436
  17.7 5.2 %collective-permute-start.4 = (f32[2,2,32,128]{3,2,1,0:T(8,128)S(1)}, f32[2,2,32,128]{3,2,1,0:T(8,128)S(1)}, u32[]{:S(2)}, u32[]{:S(2)}) collective-permute-start(f32[2,2,32,128]{3,2,1,0:T(8,128)S(1)} %fusion.5), channel_id=1, source_target_pairs={{0,8},{1,9},{2,10},{3,11},{4,12},{5,13},{6,14},{7,15},{8,0},{9,1},... | collective-permute-start | bytes 196616 | tf_op jit(solution)/shard_map/ppermute | solution.py:419
  24.3 5.2 %collective-permute-start.5 = (f32[2,2,32,128]{3,2,1,0:T(8,128)S(1)}, f32[2,2,32,128]{3,2,1,0:T(8,128)S(1)}, u32[]{:S(2)}, u32[]{:S(2)}) collective-permute-start(f32[2,2,32,128]{3,2,1,0:T(8,128)S(1)} %get-tuple-element.33), channel_id=1, source_target_pairs={{0,8},{1,9},{2,10},{3,11},{4,12},{5,13},{6,14},{7,15},{8,0},{9,1},... | collective-permute-start | bytes 196616 | tf_op jit(solution)/shard_map/ppermute | solution.py:419
  29.5 6.3 %collective-permute-start.6 = (f32[4,2,32,128]{3,2,1,0:T(8,128)S(1)}, f32[4,2,32,128]{3,2,1,0:T(8,128)S(1)}, u32[]{:S(2)}, u32[]{:S(2)}) collective-permute-start(f32[4,2,32,128]{3,2,1,0:T(8,128)S(1)} %get-tuple-element.61), channel_id=1, source_target_pairs={{0,2},{1,3},{2,0},{3,1},{4,6},{5,7},{6,4},{7,5},{8,10},{9,11},{10,... | collective-permute-start | bytes 393224 | tf_op jit(solution)/shard_map/ppermute | solution.py:419
  31.2 5.0 %collective-permute-start.7 = (f32[4,2,32,128]{3,2,1,0:T(8,128)S(1)}, f32[4,2,32,128]{3,2,1,0:T(8,128)S(1)}, u32[]{:S(2)}, u32[]{:S(2)}) collective-permute-start(f32[4,2,32,128]{3,2,1,0:T(8,128)S(1)} %get-tuple-element.61), channel_id=1, source_target_pairs={{0,4},{1,5},{2,6},{3,7},{4,0},{5,1},{6,2},{7,3},{8,12},{9,13},{10,... | collective-permute-start | bytes 393224 | tf_op jit(solution)/shard_map/ppermute | solution.py:419
  33.1 5.9 %collective-permute-start.8 = (f32[4,2,32,128]{3,2,1,0:T(8,128)S(1)}, f32[4,2,32,128]{3,2,1,0:T(8,128)S(1)}, u32[]{:S(2)}, u32[]{:S(2)}) collective-permute-start(f32[4,2,32,128]{3,2,1,0:T(8,128)S(1)} %get-tuple-element.61), channel_id=1, source_target_pairs={{0,6},{1,7},{2,4},{3,5},{4,2},{5,3},{6,0},{7,1},{8,14},{9,15},{10,... | collective-permute-start | bytes 393224 | tf_op jit(solution)/shard_map/ppermute | solution.py:419
  38.9 2.0 %collective-permute-start.9 = (f32[16,2,32,128]{3,2,1,0:T(8,128)S(1)}, f32[16,2,32,128]{3,2,1,0:T(8,128)S(1)}, u32[]{:S(2)}, u32[]{:S(2)}) collective-permute-start(f32[16,2,32,128]{3,2,1,0:T(8,128)S(1)} %constant_dynamic-update-slice_fusion.2.front_ref), channel_id=1, source_target_pairs={{0,1},{1,0},{2,3},{3,2},{4,5},{5,4},{6,7},{7,6},{8,9},{9,8},{10,11... | collective-permute-start | bytes 1572872 | tf_op jit(solution)/shard_map/ppermute | solution.py:419
  48.5 1.9 %collective-permute-start.10 = (f32[16,2,32,128]{3,2,1,0:T(8,128)S(1)}, f32[16,2,32,128]{3,2,1,0:T(8,128)S(1)}, u32[]{:S(2)}, u32[]{:S(2)}) collective-permute-start(f32[16,2,32,128]{3,2,1,0:T(8,128)S(1)} %get-tuple-element.38), channel_id=1, source_target_pairs={{0,1},{1,0},{2,3},{3,2},{4,5},{5,4},{6,7},{7,6},{8,9},{9,8},{10,11... | collective-permute-start | bytes 1572872 | tf_op jit(solution)/shard_map/ppermute | solution.py:419
  50.5 8.4 %collective-permute-start.13 = (f32[4,2,32,128]{3,2,1,0:T(8,128)S(1)}, f32[4,2,32,128]{3,2,1,0:T(8,128)S(1)}, u32[]{:S(2)}, u32[]{:S(2)}) collective-permute-start(f32[4,2,32,128]{3,2,1,0:T(8,128)S(1)} %get-tuple-element.51), channel_id=1, source_target_pairs={{0,2},{1,3},{2,0},{3,1},{4,6},{5,7},{6,4},{7,5},{8,10},{9,11},{10,... | collective-permute-start | bytes 393224 | tf_op jit(solution)/shard_map/ppermute | solution.py:419
  51.1 7.8 %collective-permute-start.12 = (f32[4,2,32,128]{3,2,1,0:T(8,128)S(1)}, f32[4,2,32,128]{3,2,1,0:T(8,128)S(1)}, u32[]{:S(2)}, u32[]{:S(2)}) collective-permute-start(f32[4,2,32,128]{3,2,1,0:T(8,128)S(1)} %get-tuple-element.52), channel_id=1, source_target_pairs={{0,6},{1,7},{2,4},{3,5},{4,2},{5,3},{6,0},{7,1},{8,14},{9,15},{10,... | collective-permute-start | bytes 393224 | tf_op jit(solution)/shard_map/ppermute | solution.py:419
  52.5 7.7 %collective-permute-start.11 = (f32[4,2,32,128]{3,2,1,0:T(8,128)S(1)}, f32[4,2,32,128]{3,2,1,0:T(8,128)S(1)}, u32[]{:S(2)}, u32[]{:S(2)}) collective-permute-start(f32[4,2,32,128]{3,2,1,0:T(8,128)S(1)} %get-tuple-element.53), channel_id=1, source_target_pairs={{0,4},{1,5},{2,6},{3,7},{4,0},{5,1},{6,2},{7,3},{8,12},{9,13},{10,... | collective-permute-start | bytes 393224 | tf_op jit(solution)/shard_map/ppermute | solution.py:419
  56.2 27.1 %copy-start.3 = (bf16[256,512]{1,0:T(8,128)(2,1)S(1)}, bf16[256,512]{1,0:T(8,128)(2,1)}, u32[]{:S(2)}) copy-start(bf16[256,512]{1,0:T(8,128)(2,1)} %constant.10.clone.synth_ref) | copy-start | bytes 786436
  60.2 5.9 %collective-permute-start.14 = (f32[2,2,32,128]{3,2,1,0:T(8,128)S(1)}, f32[2,2,32,128]{3,2,1,0:T(8,128)S(1)}, u32[]{:S(2)}, u32[]{:S(2)}) collective-permute-start(f32[2,2,32,128]{3,2,1,0:T(8,128)S(1)} %fusion.2), channel_id=1, source_target_pairs={{0,8},{1,9},{2,10},{3,11},{4,12},{5,13},{6,14},{7,15},{8,0},{9,1},... | collective-permute-start | bytes 196616 | tf_op jit(solution)/shard_map/ppermute | solution.py:419
  68.1 5.3 %collective-permute-start.15 = (f32[2,2,32,128]{3,2,1,0:T(8,128)S(1)}, f32[2,2,32,128]{3,2,1,0:T(8,128)S(1)}, u32[]{:S(2)}, u32[]{:S(2)}) collective-permute-start(f32[2,2,32,128]{3,2,1,0:T(8,128)S(1)} %get-tuple-element.44), channel_id=1, source_target_pairs={{0,8},{1,9},{2,10},{3,11},{4,12},{5,13},{6,14},{7,15},{8,0},{9,1},... | collective-permute-start | bytes 196616 | tf_op jit(solution)/shard_map/ppermute | solution.py:419
  73.4 6.6 %collective-permute-start.18 = (f32[4,2,32,128]{3,2,1,0:T(8,128)S(1)}, f32[4,2,32,128]{3,2,1,0:T(8,128)S(1)}, u32[]{:S(2)}, u32[]{:S(2)}) collective-permute-start(f32[4,2,32,128]{3,2,1,0:T(8,128)S(1)} %get-tuple-element.57), channel_id=1, source_target_pairs={{0,2},{1,3},{2,0},{3,1},{4,6},{5,7},{6,4},{7,5},{8,10},{9,11},{10,... | collective-permute-start | bytes 393224 | tf_op jit(solution)/shard_map/ppermute | solution.py:419
  73.4 6.5 %collective-permute-start.17 = (f32[4,2,32,128]{3,2,1,0:T(8,128)S(1)}, f32[4,2,32,128]{3,2,1,0:T(8,128)S(1)}, u32[]{:S(2)}, u32[]{:S(2)}) collective-permute-start(f32[4,2,32,128]{3,2,1,0:T(8,128)S(1)} %get-tuple-element.57), channel_id=1, source_target_pairs={{0,4},{1,5},{2,6},{3,7},{4,0},{5,1},{6,2},{7,3},{8,12},{9,13},{10,... | collective-permute-start | bytes 393224 | tf_op jit(solution)/shard_map/ppermute | solution.py:419
  75.4 5.9 %collective-permute-start.16 = (f32[4,2,32,128]{3,2,1,0:T(8,128)S(1)}, f32[4,2,32,128]{3,2,1,0:T(8,128)S(1)}, u32[]{:S(2)}, u32[]{:S(2)}) collective-permute-start(f32[4,2,32,128]{3,2,1,0:T(8,128)S(1)} %get-tuple-element.57), channel_id=1, source_target_pairs={{0,6},{1,7},{2,4},{3,5},{4,2},{5,3},{6,0},{7,1},{8,14},{9,15},{10,... | collective-permute-start | bytes 393224 | tf_op jit(solution)/shard_map/ppermute | solution.py:419
  81.4 2.0 %collective-permute-start.19 = (f32[16,2,32,128]{3,2,1,0:T(8,128)S(1)}, f32[16,2,32,128]{3,2,1,0:T(8,128)S(1)}, u32[]{:S(2)}, u32[]{:S(2)}) collective-permute-start(f32[16,2,32,128]{3,2,1,0:T(8,128)S(1)} %constant_dynamic-update-slice_fusion.9.front_ref), channel_id=1, source_target_pairs={{0,1},{1,0},{2,3},{3,2},{4,5},{5,4},{6,7},{7,6},{8,9},{9,8},{10,11... | collective-permute-start | bytes 1572872 | tf_op jit(solution)/shard_map/ppermute | solution.py:419

commit v5 on v4

--- a/solution.py
+++ b/solution.py
@@ -15,6 +15,7 @@
 SUB = 8
 VMEM_LIMIT = 16 << 20
 STEP = 8
+PART = 2
 
 
 def split_np(values):
@@ -121,42 +122,47 @@
             coef_ref[block, pl.ds((cells + at + i) * SUB, SUB)] = flipped[rows]
 
 
-def to_modes(coef_ref, table_ref, keep_ref, send_ref, plane):
-    modes = 2 * keep_ref.shape[0]
-    for block in range(coef_ref.shape[0]):
-        high, low = split(coef_ref[block])
-        full = dot(table_ref[0], jnp.concatenate([high, low], axis=1))
-        full = full[:, :LANES] + full[:, LANES:] + dot(table_ref[1], high)
-        full = full.reshape(modes, SUB, LANES)
-        rows = slice(SUB * block, SUB * (block + 1))
-        keep_ref[:, plane, rows] = full[: modes // 2]
-        send_ref[:, plane, rows] = full[modes // 2 :]
-
-
-def from_modes(front_ref, back_ref, table_ref, lhs_ref, plane):
-    modes = 2 * front_ref.shape[0]
-    cells, channels = lhs_ref.shape[:2]
+def to_modes(coef_ref, table_ref, out_ref, upper):
+    modes, planes = out_ref.shape[:2]
+    count = modes * SUB
+    rows = slice(count * upper, count * (upper + 1))
+    for plane in range(planes):
+        for block in range(coef_ref.shape[1]):
+            high, low = split(coef_ref[plane, block])
+            full = dot(table_ref[0, rows], jnp.concatenate([high, low], axis=1))
+            full = full[:, :LANES] + full[:, LANES:] + dot(table_ref[1, rows], high)
+            out_ref[:, plane, SUB * block : SUB * (block + 1)] = full.reshape(modes, SUB, LANES)
+
+
+def from_modes(modes_ref, table_ref, upper, plane, block):
+    count = modes_ref.shape[0] * SUB
+    lanes = slice(count * upper, count * (upper + 1))
+    half = table_ref.shape[1] // 2
+    lane = lax.broadcasted_iota(jnp.int32, (half, LANES), 1)
+    real = lane % (LANES // 2) < LANES // 4
+    values = modes_ref[:, plane, SUB * block : SUB * (block + 1)]
+    high, low = split(values.reshape(count, LANES))
+    full = dot(table_ref[0, :, lanes], jnp.concatenate([high, low], axis=1))
+    full = full[:, :LANES] + full[:, LANES:] + dot(table_ref[1, :, lanes], high)
+    plain, other = full[:half], full[half:]
+    turned = jnp.where(
+        real, -pltpu.roll(other, 3 * LANES // 4, 1), pltpu.roll(other, LANES // 4, 1)
+    )
+    return plain + turned
+
+
+def finish_modes(modes_ref, table_ref, inv_ref, lhs_ref, plane):
+    cells, channels = lhs_ref.shape[1:3]
     half = channels // 2
-    lane = lax.broadcasted_iota(jnp.int32, (cells * SUB, LANES), 1)
-    real = lane % (LANES // 2) < LANES // 4
-    low_lane = lane < LANES // 2
+    low_lane = lax.broadcasted_iota(jnp.int32, (cells * SUB, LANES), 1) < LANES // 2
     for block in range(half // SUB):
-        rows = slice(SUB * block, SUB * (block + 1))
-        values = jnp.concatenate([front_ref[:, plane, rows], back_ref[:, plane, rows]], axis=0)
-        high, low = split(values.reshape(modes * SUB, LANES))
-        full = dot(table_ref[0], jnp.concatenate([high, low], axis=1))
-        full = full[:, :LANES] + full[:, LANES:] + dot(table_ref[1], high)
-        plain, other = full[: cells * SUB], full[cells * SUB :]
-        turned = jnp.where(
-            real, -pltpu.roll(other, 3 * LANES // 4, 1), pltpu.roll(other, LANES // 4, 1)
-        )
-        inv = plain + turned
+        inv = inv_ref[plane, block] + from_modes(modes_ref, table_ref, 1, plane, block)
         swapped = pltpu.roll(inv, LANES // 2, 1)
         for at, doubled in (
             (0, jnp.where(low_lane, inv, swapped)),
             (half, jnp.where(low_lane, swapped, inv)),
         ):
-            lhs_ref[:, at + SUB * block : at + SUB * (block + 1)] = doubled.reshape(
+            lhs_ref[plane, :, at + SUB * block : at + SUB * (block + 1)] = doubled.reshape(
                 cells, SUB, LANES
             )
 
@@ -167,24 +173,31 @@
     return dot(jnp.concatenate([high, low], axis=1), table_ref[...])
 
 
-TAIL = (
-    0.11650589762013625,
-    0.06758867364360233,
-    0.2686846227283619,
-    -0.23671861048677273,
-    0.38970758618179535,
-    -0.10576817864886755,
+TAIL_AT = 1.0 / 0.28
+TAIL = tuple(
+    math.sqrt(2.0 * math.pi) * factor * TAIL_AT ** (power + 1)
+    for power, factor in enumerate(
+        (
+            0.11650589762013625,
+            0.06758867364360233,
+            0.2686846227283619,
+            -0.23671861048677273,
+            0.38970758618179535,
+            -0.10576817864886755,
+        )
+    )
 )
+BELL = (-0.5 * math.log2(math.e), -0.5 * math.log2(2.0 * math.pi))
 
 
 def normal_parts(values):
-    bell = jnp.exp(-0.5 * values * values)
-    inner = 1.0 / (1.0 + 0.28 * jnp.abs(values))
+    density = jnp.exp2(values * values * BELL[0] + BELL[1])
+    inner = 1.0 / (TAIL_AT + jnp.abs(values))
     tail = TAIL[-1] * inner
     for factor in TAIL[-2::-1]:
         tail = (tail + factor) * inner
-    tail = tail * bell
-    return jnp.where(values >= 0.0, 1.0 - tail, tail), bell * (1.0 / math.sqrt(2.0 * math.pi))
+    tail = tail * density
+    return jnp.where(values >= 0.0, 1.0 - tail, tail), density
 
 
 def transpose_out(rows):
@@ -219,26 +232,40 @@
 
 
 def spanwise_kernel(
-    sizes, x_ref, table_hbm, keep_ref, send_ref, down_ref, back_ref,
-    table_ref, x_scr, coef_ref, sems,
+    sizes, x_ref, table_hbm, send_ref, coef_ref, down_ref, back_ref, table_ref, x_scr, sems
 ):
     cells, planes, channels, span = x_ref.shape
     work = chunks(cells, planes)
-    copies = [
-        pltpu.make_async_copy(x_ref.at[pl.ds(at, STEP), p], x_scr.at[i], sems.at[i])
-        for i, (p, at) in enumerate(work)
-    ]
-    copies.append(pltpu.make_async_copy(table_hbm, table_ref, sems.at[len(work)]))
-    for copy in copies[-1:] + copies[:-1]:
+    copies = [pltpu.make_async_copy(table_hbm, table_ref, sems.at[len(work) * STEP // PART])]
+    for i, (p, at) in enumerate(work):
+        for j in range(0, STEP, PART):
+            copies.append(
+                pltpu.make_async_copy(
+                    x_ref.at[pl.ds(at + j, PART), p],
+                    x_scr.at[i, pl.ds(j, PART)],
+                    sems.at[(i * STEP + j) // PART],
+                )
+            )
+    for copy in copies:
         copy.start()
     make_tables(down_ref, back_ref, *sizes)
-    copies[-1].wait()
+    copies.pop(0).wait()
     for i, (p, at) in enumerate(work):
-        copies[i].wait()
+        for j in range(0, STEP, PART):
+            copies.pop(0).wait()
         high, low = split(x_scr[i].reshape(STEP * channels, span))
         analyse(high, low, table_ref, at, coef_ref.at[p])
-    for p in range(planes):
-        to_modes(coef_ref.at[p], down_ref, keep_ref, send_ref, p)
+    to_modes(coef_ref, down_ref, send_ref, 1)
+
+
+def keep_kernel(coef_ref, down_ref, keep_ref):
+    to_modes(coef_ref, down_ref, keep_ref, 0)
+
+
+def front_kernel(front_ref, back_table_ref, inv_ref):
+    for plane in range(inv_ref.shape[0]):
+        for block in range(inv_ref.shape[1]):
+            inv_ref[plane, block] = from_modes(front_ref, back_table_ref, 0, plane, block)
 
 
 def pointwise_kernel(transposed, values_ref, local_ref, bias_ref, out_ref):
@@ -312,12 +339,12 @@
 
 
 def middle_kernel(
-    local_ref, up_ref, front_ref, back_ref, synth_ref, table_ref, down_ref, back_table_ref,
-    act_ref, dpre_ref, keep_ref, send_ref, lhs_ref, coef_ref,
+    local_ref, up_ref, behind_ref, inv_ref, synth_ref, table_ref, down_ref, back_table_ref,
+    act_ref, dpre_ref, send_ref, coef_ref, lhs_ref,
 ):
     cells, planes, channels, span = up_ref.shape
     for p in range(planes):
-        from_modes(front_ref, back_ref, back_table_ref, lhs_ref.at[p], p)
+        finish_modes(behind_ref, back_table_ref, inv_ref, lhs_ref, p)
     for p, at in chunks(cells, planes):
         rows = pl.ds(at, STEP)
         spectral = synthesise(lhs_ref.at[p], at, STEP, synth_ref)
@@ -328,37 +355,36 @@
         dpre_ref[rows, p] = dpre
         high, low = split(dpre.reshape(STEP * channels, span))
         analyse(high, low, table_ref, at, coef_ref.at[p])
-    for p in range(planes):
-        to_modes(coef_ref.at[p], down_ref, keep_ref, send_ref, p)
+    to_modes(coef_ref, down_ref, send_ref, 1)
 
 
 def adjoint_kernel(*refs):
     *piece_refs, w_ref, dmixed_ref, dmodes_ref = refs
     owned, planes = dmixed_ref.shape[:2]
     kz_count, channels, width = w_ref.shape[1:]
-    quarter = LANES // 4
-    lane = lax.broadcasted_iota(jnp.int32, (channels, LANES // 2), 1) % quarter
+    assert planes * channels == LANES
+    half = channels // 2
+    lane = lax.broadcasted_iota(jnp.int32, (channels, LANES), 1) & (kz_count - 1)
+    low_lane = lax.broadcasted_iota(jnp.int32, (half, LANES), 1) < channels
 
     def body(j, _):
         w_high, w_low = split(w_ref[j].reshape(kz_count * channels, width))
+        sides = []
         for plane in range(planes):
             total = total_of(piece_refs, j, plane)
             dmixed_ref[j, plane] = total
             rows = transpose_in(total)
-            both = jnp.concatenate([rows, turn_down(rows)], axis=0)
-            high, low = split(both)
-            right = jnp.concatenate([high, low], axis=0).T
-            full = dot(w_high, right)
-            full = (
-                full[:, : LANES // 2] + full[:, LANES // 2 :] + dot(w_low, right[:, : LANES // 2])
-            )
-            full = full.reshape(kz_count, channels, LANES // 2)
-            result = jnp.zeros((channels, LANES // 2), F32)
-            for kz in range(kz_count):
-                result = jnp.where(lane == kz, full[kz], result)
-            dmodes_ref[j, plane] = jnp.concatenate(
-                [result[: channels // 2], result[channels // 2 :]], axis=1
-            )
+            sides += [rows, turn_down(rows)]
+        right = jnp.concatenate(split(jnp.concatenate(sides, axis=0)), axis=0).T
+        full = dot(w_high, right)
+        full = full[:, :LANES] + full[:, LANES:] + dot(w_low, right[:, :LANES])
+        full = full.reshape(kz_count, channels, LANES)
+        result = full[0]
+        for kz in range(1, kz_count):
+            result = jnp.where(lane == kz, full[kz], result)
+        low, high = result[:half], result[half:]
+        dmodes_ref[j, 0] = jnp.where(low_lane, low, pltpu.roll(high, channels, 1))
+        dmodes_ref[j, 1] = jnp.where(low_lane, pltpu.roll(low, channels, 1), high)
         return 0
 
     lax.fori_loop(0, owned, body, 0)
@@ -398,13 +424,13 @@
 
 
 def input_grad_kernel(
-    local_ref, front_ref, back_ref, synth_ref, back_table_ref, out_ref, out_scr, lhs_ref, sems
+    local_ref, behind_ref, inv_ref, synth_ref, back_table_ref, out_ref, out_scr, lhs_ref, sems
 ):
     cells, planes, channels, span = local_ref.shape
     copies = []
     for i, (p, at) in enumerate(chunks(cells, planes)):
         if at == 0:
-            from_modes(front_ref, back_ref, back_table_ref, lhs_ref.at[p], p)
+            finish_modes(behind_ref, back_table_ref, inv_ref, lhs_ref, p)
         rows = pl.ds(at, STEP)
         spectral = synthesise(lhs_ref.at[p], at, STEP, synth_ref)
         out_scr[i] = spectral.reshape(STEP, channels, span) + local_ref[rows, p]
@@ -423,8 +449,9 @@
     return lax.optimization_barrier((moved, work()))
 
 
-def scatter_sum(keep, send, work):
-    pieces = [keep, swap(send, 1)]
+def scatter_sum(send, keep_work, work):
+    moved, keep = beside(swap(send, 1), keep_work)
+    pieces = [keep, moved]
 
     def part(first, count):
         total = pieces[0][first : first + count]
@@ -433,7 +460,7 @@
         return total
 
     quarter = keep.shape[0] // 4
-    moved = [swap(part(quarter * place, quarter), 2 * place) for place in (2, 3, 1)]
+    moved = [swap(part(quarter * place, quarter), 2 * place) for place in (3, 2, 1)]
     moved, done = beside(moved, work)
     pieces += moved
     for mask in stage_masks()[3:]:
@@ -442,15 +469,16 @@
     return pieces, done
 
 
-def gather_all(values, work=None):
+def gather_all(values, front_work, work=None):
     for mask in reversed(stage_masks()[3:]):
         values = jnp.concatenate([values, swap(values, mask)], axis=0)
-    moved = [swap(values, 2 * place) for place in (3, 2, 1)]
+    moved = {place: swap(values, 2 * place) for place in (3, 1, 2)}
     done = None
     if work is not None:
         moved, done = beside(moved, work)
-    values = jnp.concatenate([values] + moved[::-1], axis=0)
-    return values, swap(values, 1), done
+    values = jnp.concatenate([values, moved[1], moved[2], moved[3]], axis=0)
+    behind, inv = beside(swap(values, 1), lambda: front_work(values))
+    return behind, inv, done
 
 
 def params():
@@ -474,10 +502,11 @@
     scale = float(cells * lax.axis_size("stream") * span)
     ana_fwd, ana_inv, syn_fwd, syn_inv = map(jnp.asarray, span_tables(span, kz_count, scale))
     pieces_of = len(chunks(cells, planes))
-    coef_scr = pltpu.VMEM((planes, half_channels // SUB, 2 * cells * SUB, LANES), F32)
+    coef_shape = shape((planes, half_channels // SUB, 2 * cells * SUB, LANES), F32)
+    inv_shape = shape((planes, half_channels // SUB, cells * SUB, LANES), F32)
     lhs_scr = pltpu.VMEM((planes, cells, channels, LANES), F32)
     span_scr = pltpu.VMEM((pieces_of, STEP, channels, span), F32)
-    sem_scr = pltpu.SemaphoreType.DMA((pieces_of + 1,))
+    sem_scr = pltpu.SemaphoreType.DMA((pieces_of * STEP // PART + 1,))
     down = shape((2, total_modes * SUB, 2 * cells * SUB), BF16)
     back = shape((2, 2 * cells * SUB, total_modes * SUB), BF16)
     here = pl.BlockSpec(memory_space=pltpu.VMEM)
@@ -486,15 +515,35 @@
     half_shape = shape((half_modes, planes, half_channels, LANES), F32)
     grid_shape = shape(x.shape, F32)
 
-    keep, send, down, back = pl.pallas_call(
+    send, coef, down, back = pl.pallas_call(
         functools.partial(spanwise_kernel, (owned, total_modes, cells)),
         in_specs=[apart, apart],
         out_specs=[here] * 4,
-        out_shape=[half_shape, half_shape, down, back],
-        scratch_shapes=[pltpu.VMEM(ana_fwd.shape, BF16), span_scr, coef_scr, sem_scr],
+        out_shape=[half_shape, coef_shape, down, back],
+        scratch_shapes=[pltpu.VMEM(ana_fwd.shape, BF16), span_scr, sem_scr],
         compiler_params=params(),
         name="spanwise",
     )(pltpu.with_memory_space_constraint(x, pltpu.HBM), pltpu.with_memory_space_constraint(ana_fwd, pltpu.HBM))
+
+    def keep_part(coef):
+        return lambda: pl.pallas_call(
+            keep_kernel,
+            in_specs=[here] * 2,
+            out_specs=here,
+            out_shape=half_shape,
+            compiler_params=params(),
+            name="keep_part",
+        )(coef, down)
+
+    def front_part(front):
+        return pl.pallas_call(
+            front_kernel,
+            in_specs=[here] * 2,
+            out_specs=here,
+            out_shape=inv_shape,
+            compiler_params=params(),
+            name="front_part",
+        )(front, back)
 
     def local_forward():
         return pl.pallas_call(
@@ -506,7 +555,7 @@
             name="local_forward",
         )(x, local_weight, offset_bias[None])
 
-    pieces, local = scatter_sum(keep, send, local_forward)
+    pieces, local = scatter_sum(send, keep_part(coef), local_forward)
     modes, mixed = pl.pallas_call(
         mix_kernel,
         in_specs=[here] * (len(pieces) + 1),
@@ -515,16 +564,16 @@
         compiler_params=params(),
         name="mix",
     )(*pieces, mode_weight)
-    front, behind, _ = gather_all(mixed)
-    act, dpre, keep, send = pl.pallas_call(
+    behind, inv, _ = gather_all(mixed, front_part)
+    act, dpre, send, coef = pl.pallas_call(
         middle_kernel,
         in_specs=[here] * 8,
         out_specs=[here] * 4,
-        out_shape=[grid_shape, grid_shape, half_shape, half_shape],
-        scratch_shapes=[lhs_scr, coef_scr],
+        out_shape=[grid_shape, grid_shape, half_shape, coef_shape],
+        scratch_shapes=[lhs_scr],
         compiler_params=params(),
         name="middle",
-    )(local, up, front, behind, syn_inv, ana_inv, down, back)
+    )(local, up, behind, inv, syn_inv, ana_inv, down, back)
 
     def local_backward():
         return pl.pallas_call(
@@ -536,7 +585,7 @@
             name="local_backward",
         )(dpre, local_weight)
 
-    pieces, local = scatter_sum(keep, send, local_backward)
+    pieces, local = scatter_sum(send, keep_part(coef), local_backward)
     dmixed, dmodes = pl.pallas_call(
         adjoint_kernel,
         in_specs=[here] * (len(pieces) + 1),
@@ -556,7 +605,7 @@
             name="weight_grad",
         )(modes, dmixed)
 
-    front, behind, grad_modes = gather_all(dmodes, weight_grad)
+    behind, inv, grad_modes = gather_all(dmodes, front_part, weight_grad)
     grad_snapshot = pl.pallas_call(
         input_grad_kernel,
         in_specs=[here] * 5,
@@ -565,7 +614,7 @@
         scratch_shapes=[span_scr, lhs_scr, sem_scr],
         compiler_params=params(),
         name="input_grad",
-    )(local, front, behind, syn_fwd, back)
+    )(local, behind, inv, syn_fwd, back)
     return jnp.swapaxes(act, 2, 3), jnp.swapaxes(grad_snapshot, 2, 3), grad_modes
 
 

time: 87 us -> 85.7 us (0.985)
  waiting for transfers between devices: 32.5 us -> 29.4 us
  Pallas kernels: 26 us -> 27.6 us
    ppermute x20, waiting for transfers between devices: 32.5 us -> 29.4 us  [swap(): return lax.ppermute(values, 'stream', [(i, i ^ mask) for i in range(count)])]
    pallas_call x0 -> x4, Pallas kernels: none -> 2.17 us  [the longest x2 1.3 us: front_part(): pl.pallas_call(front_kernel, in_specs=[here] * 2, out_specs=here, out_sha...]
  transfers between devices with their start and end apart: 20 -> 20, of which waited for: 17 -> 16; matrix products, arithmetic and copies ran while one was open for 0% -> 0% of each run, Pallas kernels for 9% -> 12%
where the time goes in v5:
time: 85.7 us; the launch traced here: 85.5 us
  waiting for transfers between devices  29.4 us (34%)
  Pallas kernels  27.6 us (32%)
  starting transfers between devices  27.1 us (32%)
  between operations  1.06 us (1%)
    ppermute x20, waiting for transfers between devices, swap(): return lax.ppermute(values, 'stream', [(i, i ^ mask) for i in range(count)])  29.4 us
    ppermute x20, starting transfers between devices, swap(): return lax.ppermute(values, 'stream', [(i, i ^ mask) for i in range(count)])  27.1 us
    pallas_call x1, Pallas kernels, per_device(): pl.pallas_call(middle_kernel, in_specs=[here] * 8, out_specs=[here] * 4,...  7.28 us
    pallas_call x1, Pallas kernels, per_device(): pl.pallas_call(functools.partial(spanwise_kernel, (owned, total_modes, ce...  3.93 us
    pallas_call x1, Pallas kernels, per_device(): pl.pallas_call(input_grad_kernel, in_specs=[here] * 5, out_specs=apart, o...  3.4 us
    pallas_call x1, Pallas kernels, weight_grad(): pl.pallas_call(weight_grad_kernel, in_specs=[here] * 2, out_specs=here, o...  3.26 us
    pallas_call x1, Pallas kernels, local_forward(): pl.pallas_call(functools.partial(pointwise_kernel, True), in_specs=[here]...  2.46 us
    pallas_call x1, Pallas kernels, local_backward(): pl.pallas_call(lambda values, weight, out: pointwise_kernel(False, values...  2.15 us
  transfers between devices with their start and end apart: 20, of which 16 were waited for; matrix products, arithmetic and copies ran while one was open for 0% of the time, Pallas kernels for 12%

profile of v5, /device:TPU:0, one launch (start us, length us, event | category | flops | bytes accessed | tf_op | source)
XLA Modules:
  0.0 85.5 jit_solution(16364620457826370132)
XLA Ops:
  0.6 0.0 copy-start
  0.6 0.0 copy-start.6
  0.7 0.0 copy-start.7
  0.7 3.9 %spanwise.1 = (f32[16,2,32,128]{3,2,1,0:T(8,128)S(1)}, f32[2,4,256,128]{3,2,1,0:T(8,128)S(1)}, bf16[2,256,256]{2,1,0:T(8,128)(2,1)S(1)}, bf16[2,256,256]{2,1,0:T(8,128)(2,1)S(1)}) custom-call(f32[16,2,64,512]{3,2,1,0:T(8,128)} %bitcast.5, bf16[512,256]{1,0:T(8,128)(2,1)} %constant.8.clone.table_hbm), custom_call_target="tpu_custom_call" | custom-call | tf_op jit(solution)/shard_map/spanwise/pallas_call | solution.py:518
  4.6 0.5 collective-permute-start
  5.1 0.4 keep_part.2.refs_0_
  5.6 1.1 %collective-permute-done.refs_1_ = f32[16,2,32,128]{3,2,1,0:T(8,128)S(1)} collective-permute-done((f32[16,2,32,128]{3,2,1,0:T(8,128)S(1)}, f32[16,2,32,128]{3,2,1,0:T(8,128)S(1)}, u32[]{:S(2)}, u32[]{:S(2)}) %collective-permute-start) | collective-permute-done | bytes 524320 | tf_op jit(solution)/shard_map/ppermute | solution.py:445
  6.7 0.1 slice_add_fusion.3
  6.7 3.0 %collective-permute-start.3 = (f32[4,2,32,128]{3,2,1,0:T(8,128)S(1)}, f32[4,2,32,128]{3,2,1,0:T(8,128)S(1)}, u32[]{:S(2)}, u32[]{:S(2)}) collective-permute-start(f32[4,2,32,128]{3,2,1,0:T(8,128)S(1)} %get-tuple-element.70), channel_id=1, source_target_pairs={{0,2},{1,3},{2,0},{3,1},{4,6},{5,7},{6,4},{7,5},{8,10},{9,11},{10,... | collective-permute-start | bytes 393224 | tf_op jit(solution)/shard_map/ppermute | solution.py:445
  9.7 1.6 %collective-permute-start.2 = (f32[4,2,32,128]{3,2,1,0:T(8,128)S(1)}, f32[4,2,32,128]{3,2,1,0:T(8,128)S(1)}, u32[]{:S(2)}, u32[]{:S(2)}) collective-permute-start(f32[4,2,32,128]{3,2,1,0:T(8,128)S(1)} %get-tuple-element.71), channel_id=1, source_target_pairs={{0,4},{1,5},{2,6},{3,7},{4,0},{5,1},{6,2},{7,3},{8,12},{9,13},{10,... | collective-permute-start | bytes 393224 | tf_op jit(solution)/shard_map/ppermute | solution.py:445
  11.2 0.0 collective-permute-start.1
  11.3 0.0 copy-done.7
  11.3 0.0 copy-start.1
  11.3 2.5 %local_forward.1.local_ref = f32[16,2,64,512]{3,2,1,0:T(8,128)S(1)} custom-call(f32[16,2,64,512]{3,2,1,0:T(8,128)S(1)} %bitcast.6, f32[64,64]{1,0:T(8,128)S(1)} %copy-done.6, f32[1,64]{1,0:T(1,128)S(1)} %bitcast.8), custom_call_target="tpu_custom_call" | custom-call | tf_op jit(solution)/shard_map/local_forward/pallas_call | solution.py:549
  13.7 0.0 copy-start.2
  13.8 0.0 copy-start.4
  13.8 0.0 copy-start.5
  13.8 0.0 collective-permute-done.3.refs_4_
  13.8 2.3 %collective-permute-done.2.refs_3_ = f32[4,2,32,128]{3,2,1,0:T(8,128)S(1)} collective-permute-done((f32[4,2,32,128]{3,2,1,0:T(8,128)S(1)}, f32[4,2,32,128]{3,2,1,0:T(8,128)S(1)}, u32[]{:S(2)}, u32[]{:S(2)}) %collective-permute-start.2) | collective-permute-done | bytes 131104 | tf_op jit(solution)/shard_map/ppermute | solution.py:445
  16.1 1.5 %collective-permute-done.1.refs_2_ = f32[4,2,32,128]{3,2,1,0:T(8,128)S(1)} collective-permute-done((f32[4,2,32,128]{3,2,1,0:T(8,128)S(1)}, f32[4,2,32,128]{3,2,1,0:T(8,128)S(1)}, u32[]{:S(2)}, u32[]{:S(2)}) %collective-permute-start.1) | collective-permute-done | bytes 131104 | tf_op jit(solution)/shard_map/ppermute | solution.py:445
  17.6 2.8 %collective-permute-start.4 = (f32[2,2,32,128]{3,2,1,0:T(8,128)S(1)}, f32[2,2,32,128]{3,2,1,0:T(8,128)S(1)}, u32[]{:S(2)}, u32[]{:S(2)}) collective-permute-start(f32[2,2,32,128]{3,2,1,0:T(8,128)S(1)} %slice_add_fusion.7), channel_id=1, source_target_pairs={{0,8},{1,9},{2,10},{3,11},{4,12},{5,13},{6,14},{7,15},{8,0},{9,1},... | collective-permute-start | bytes 196616 | tf_op jit(solution)/shard_map/ppermute | solution.py:445
  20.4 2.4 %collective-permute-done.4.refs_5_ = f32[2,2,32,128]{3,2,1,0:T(8,128)S(1)} collective-permute-done((f32[2,2,32,128]{3,2,1,0:T(8,128)S(1)}, f32[2,2,32,128]{3,2,1,0:T(8,128)S(1)}, u32[]{:S(2)}, u32[]{:S(2)}) %collective-permute-start.4) | collective-permute-done | bytes 65568 | tf_op jit(solution)/shard_map/ppermute | solution.py:445
  22.8 1.3 %mix.1 = (f32[2,2,32,128]{3,2,1,0:T(8,128)S(1)}, f32[2,2,32,128]{3,2,1,0:T(8,128)S(1)}) custom-call(f32[16,2,32,128]{3,2,1,0:T(8,128)S(1)} %keep_part.2.refs_0_, f32[16,2,32,128]{3,2,1,0:T(8,128)S(1)} %collective-permute-done.refs_1_, f32[4,2,32,128]{3,2,1,0:T(8,128)S(1)} %collective-permute-done.1.refs_2_, ...), custom_call_target="tpu_custom_call" | custom-call | tf_op jit(solution)/shard_map/mix/pallas_call | solution.py:559
  24.1 2.9 %collective-permute-start.5 = (f32[2,2,32,128]{3,2,1,0:T(8,128)S(1)}, f32[2,2,32,128]{3,2,1,0:T(8,128)S(1)}, u32[]{:S(2)}, u32[]{:S(2)}) collective-permute-start(f32[2,2,32,128]{3,2,1,0:T(8,128)S(1)} %get-tuple-element.44), channel_id=1, source_target_pairs={{0,8},{1,9},{2,10},{3,11},{4,12},{5,13},{6,14},{7,15},{8,0},{9,1},... | collective-permute-start | bytes 196616 | tf_op jit(solution)/shard_map/ppermute | solution.py:445
  27.0 2.4 %collective-permute-done.5 = f32[2,2,32,128]{3,2,1,0:T(8,128)S(1)} collective-permute-done((f32[2,2,32,128]{3,2,1,0:T(8,128)S(1)}, f32[2,2,32,128]{3,2,1,0:T(8,128)S(1)}, u32[]{:S(2)}, u32[]{:S(2)}) %collective-permute-start.5) | collective-permute-done | bytes 65568 | tf_op jit(solution)/shard_map/ppermute | solution.py:445
  29.3 1.7 %collective-permute-start.6 = (f32[4,2,32,128]{3,2,1,0:T(8,128)S(1)}, f32[4,2,32,128]{3,2,1,0:T(8,128)S(1)}, u32[]{:S(2)}, u32[]{:S(2)}) collective-permute-start(f32[4,2,32,128]{3,2,1,0:T(8,128)S(1)} %get-tuple-element.77), channel_id=1, source_target_pairs={{0,2},{1,3},{2,0},{3,1},{4,6},{5,7},{6,4},{7,5},{8,10},{9,11},{10,... | collective-permute-start | bytes 393224 | tf_op jit(solution)/shard_map/ppermute | solution.py:445
  31.1 1.8 %collective-permute-start.7 = (f32[4,2,32,128]{3,2,1,0:T(8,128)S(1)}, f32[4,2,32,128]{3,2,1,0:T(8,128)S(1)}, u32[]{:S(2)}, u32[]{:S(2)}) collective-permute-start(f32[4,2,32,128]{3,2,1,0:T(8,128)S(1)} %get-tuple-element.77), channel_id=1, source_target_pairs={{0,4},{1,5},{2,6},{3,7},{4,0},{5,1},{6,2},{7,3},{8,12},{9,13},{10,... | collective-permute-start | bytes 393224 | tf_op jit(solution)/shard_map/ppermute | solution.py:445
  32.9 0.0 collective-permute-start.8
  32.9 2.7 %collective-permute-done.6 = f32[4,2,32,128]{3,2,1,0:T(8,128)S(1)} collective-permute-done((f32[4,2,32,128]{3,2,1,0:T(8,128)S(1)}, f32[4,2,32,128]{3,2,1,0:T(8,128)S(1)}, u32[]{:S(2)}, u32[]{:S(2)}) %collective-permute-start.6) | collective-permute-done | bytes 131104 | tf_op jit(solution)/shard_map/ppermute | solution.py:445
  35.6 0.4 collective-permute-done.7
  36.1 2.7 %collective-permute-done.8 = f32[4,2,32,128]{3,2,1,0:T(8,128)S(1)} collective-permute-done((f32[4,2,32,128]{3,2,1,0:T(8,128)S(1)}, f32[4,2,32,128]{3,2,1,0:T(8,128)S(1)}, u32[]{:S(2)}, u32[]{:S(2)}) %collective-permute-start.8) | collective-permute-done | bytes 131104 | tf_op jit(solution)/shard_map/ppermute | solution.py:445
  38.8 0.1 collective-permute-start.9
  38.9 0.7 front_part.2.inv_ref
  39.5 1.2 %collective-permute-done.9.behind_ref = f32[16,2,32,128]{3,2,1,0:T(8,128)S(1)} collective-permute-done((f32[16,2,32,128]{3,2,1,0:T(8,128)S(1)}, f32[16,2,32,128]{3,2,1,0:T(8,128)S(1)}, u32[]{:S(2)}, u32[]{:S(2)}) %collective-permute-start.9) | collective-permute-done | bytes 524320 | tf_op jit(solution)/shard_map/ppermute | solution.py:445
  40.8 0.0 copy-done.5
  40.8 7.3 %middle.1 = (f32[16,2,64,512]{3,2,1,0:T(8,128)}, f32[16,2,64,512]{3,2,1,0:T(8,128)S(1)}, f32[16,2,32,128]{3,2,1,0:T(8,128)S(1)}, f32[2,4,256,128]{3,2,1,0:T(8,128)S(1)}) custom-call(f32[16,2,64,512]{3,2,1,0:T(8,128)S(1)} %local_forward.1.local_ref, f32[16,2,64,512]{3,2,1,0:T(8,128)S(1)} %bitcast.7, f32[16,2,32,128]{3,2,1,0:T(8,128)S(1)} %collective-permute-done.9.behind_ref, ...), custom_call_target="tpu_custom_call" | custom-call | tf_op jit(solution)/shard_map/middle/pallas_call | solution.py:568
  48.0 0.1 collective-permute-start.10
  48.2 0.4 keep_part.3.refs_0_
  48.6 1.3 %collective-permute-done.10.refs_1_ = f32[16,2,32,128]{3,2,1,0:T(8,128)S(1)} collective-permute-done((f32[16,2,32,128]{3,2,1,0:T(8,128)S(1)}, f32[16,2,32,128]{3,2,1,0:T(8,128)S(1)}, u32[]{:S(2)}, u32[]{:S(2)}) %collective-permute-start.10) | collective-permute-done | bytes 524320 | tf_op jit(solution)/shard_map/ppermute | solution.py:445
  50.0 0.1 slice_add_fusion
  50.0 0.6 collective-permute-start.13
  50.6 1.5 %collective-permute-start.12 = (f32[4,2,32,128]{3,2,1,0:T(8,128)S(1)}, f32[4,2,32,128]{3,2,1,0:T(8,128)S(1)}, u32[]{:S(2)}, u32[]{:S(2)}) collective-permute-start(f32[4,2,32,128]{3,2,1,0:T(8,128)S(1)} %get-tuple-element.68), channel_id=1, source_target_pairs={{0,4},{1,5},{2,6},{3,7},{4,0},{5,1},{6,2},{7,3},{8,12},{9,13},{10,... | collective-permute-start | bytes 393224 | tf_op jit(solution)/shard_map/ppermute | solution.py:445
  52.1 1.5 %collective-permute-start.11 = (f32[4,2,32,128]{3,2,1,0:T(8,128)S(1)}, f32[4,2,32,128]{3,2,1,0:T(8,128)S(1)}, u32[]{:S(2)}, u32[]{:S(2)}) collective-permute-start(f32[4,2,32,128]{3,2,1,0:T(8,128)S(1)} %get-tuple-element.69), channel_id=1, source_target_pairs={{0,6},{1,7},{2,4},{3,5},{4,2},{5,3},{6,0},{7,1},{8,14},{9,15},{10,... | collective-permute-start | bytes 393224 | tf_op jit(solution)/shard_map/ppermute | solution.py:445
  53.6 2.2 %local_backward.1.local_ref = f32[16,2,64,512]{3,2,1,0:T(8,128)S(1)} custom-call(f32[16,2,64,512]{3,2,1,0:T(8,128)S(1)} %get-tuple-element.53.values, f32[64,64]{1,0:T(8,128)S(1)} %copy-done.6), custom_call_target="tpu_custom_call" | custom-call | tf_op jit(solution)/shard_map/local_backward/pallas_call | solution.py:579
  55.7 0.0 collective-permute-done.13.refs_4_
  55.7 1.2 %collective-permute-done.12.refs_3_ = f32[4,2,32,128]{3,2,1,0:T(8,128)S(1)} collective-permute-done((f32[4,2,32,128]{3,2,1,0:T(8,128)S(1)}, f32[4,2,32,128]{3,2,1,0:T(8,128)S(1)}, u32[]{:S(2)}, u32[]{:S(2)}) %collective-permute-start.12) | collective-permute-done | bytes 131104 | tf_op jit(solution)/shard_map/ppermute | solution.py:445
  57.0 2.6 %collective-permute-done.11.refs_2_ = f32[4,2,32,128]{3,2,1,0:T(8,128)S(1)} collective-permute-done((f32[4,2,32,128]{3,2,1,0:T(8,128)S(1)}, f32[4,2,32,128]{3,2,1,0:T(8,128)S(1)}, u32[]{:S(2)}, u32[]{:S(2)}) %collective-permute-start.11) | collective-permute-done | bytes 131104 | tf_op jit(solution)/shard_map/ppermute | solution.py:445
  59.6 0.0 copy-start.3
  59.7 3.1 %collective-permute-start.14 = (f32[2,2,32,128]{3,2,1,0:T(8,128)S(1)}, f32[2,2,32,128]{3,2,1,0:T(8,128)S(1)}, u32[]{:S(2)}, u32[]{:S(2)}) collective-permute-start(f32[2,2,32,128]{3,2,1,0:T(8,128)S(1)} %slice_add_fusion.6), channel_id=1, source_target_pairs={{0,8},{1,9},{2,10},{3,11},{4,12},{5,13},{6,14},{7,15},{8,0},{9,1},... | collective-permute-start | bytes 196616 | tf_op jit(solution)/shard_map/ppermute | solution.py:445
  62.7 2.8 %collective-permute-done.14.refs_5_ = f32[2,2,32,128]{3,2,1,0:T(8,128)S(1)} collective-permute-done((f32[2,2,32,128]{3,2,1,0:T(8,128)S(1)}, f32[2,2,32,128]{3,2,1,0:T(8,128)S(1)}, u32[]{:S(2)}, u32[]{:S(2)}) %collective-permute-start.14) | collective-permute-done | bytes 65568 | tf_op jit(solution)/shard_map/ppermute | solution.py:445
  65.5 1.7 %adjoint.1 = (f32[2,2,32,128]{3,2,1,0:T(8,128)S(1)}, f32[2,2,32,128]{3,2,1,0:T(8,128)S(1)}) custom-call(f32[16,2,32,128]{3,2,1,0:T(8,128)S(1)} %keep_part.3.refs_0_, f32[16,2,32,128]{3,2,1,0:T(8,128)S(1)} %collective-permute-done.10.refs_1_, f32[4,2,32,128]{3,2,1,0:T(8,128)S(1)} %collective-permute-done.11.refs_2_, ...), custom_call_target="tpu_custom_call" | custom-call | tf_op jit(solution)/shard_map/adjoint/pallas_call | solution.py:589
  67.2 2.4 %collective-permute-start.15 = (f32[2,2,32,128]{3,2,1,0:T(8,128)S(1)}, f32[2,2,32,128]{3,2,1,0:T(8,128)S(1)}, u32[]{:S(2)}, u32[]{:S(2)}) collective-permute-start(f32[2,2,32,128]{3,2,1,0:T(8,128)S(1)} %get-tuple-element.58), channel_id=1, source_target_pairs={{0,8},{1,9},{2,10},{3,11},{4,12},{5,13},{6,14},{7,15},{8,0},{9,1},... | collective-permute-start | bytes 196616 | tf_op jit(solution)/shard_map/ppermute | solution.py:445
  69.6 3.0 %collective-permute-done.15 = f32[2,2,32,128]{3,2,1,0:T(8,128)S(1)} collective-permute-done((f32[2,2,32,128]{3,2,1,0:T(8,128)S(1)}, f32[2,2,32,128]{3,2,1,0:T(8,128)S(1)}, u32[]{:S(2)}, u32[]{:S(2)}) %collective-permute-start.15) | collective-permute-done | bytes 65568 | tf_op jit(solution)/shard_map/ppermute | solution.py:445
  72.6 1.4 %collective-permute-start.18 = (f32[4,2,32,128]{3,2,1,0:T(8,128)S(1)}, f32[4,2,32,128]{3,2,1,0:T(8,128)S(1)}, u32[]{:S(2)}, u32[]{:S(2)}) collective-permute-start(f32[4,2,32,128]{3,2,1,0:T(8,128)S(1)} %get-tuple-element.73), channel_id=1, source_target_pairs={{0,6},{1,7},{2,4},{3,5},{4,2},{5,3},{6,0},{7,1},{8,14},{9,15},{10,... | collective-permute-start | bytes 393224 | tf_op jit(solution)/shard_map/ppermute | solution.py:445
  74.0 0.2 collective-permute-start.17
  74.2 1.9 %collective-permute-start.16 = (f32[4,2,32,128]{3,2,1,0:T(8,128)S(1)}, f32[4,2,32,128]{3,2,1,0:T(8,128)S(1)}, u32[]{:S(2)}, u32[]{:S(2)}) collective-permute-start(f32[4,2,32,128]{3,2,1,0:T(8,128)S(1)} %get-tuple-element.73), channel_id=1, source_target_pairs={{0,2},{1,3},{2,0},{3,1},{4,6},{5,7},{6,4},{7,5},{8,10},{9,11},{10,... | collective-permute-start | bytes 393224 | tf_op jit(solution)/shard_map/ppermute | solution.py:445
  76.1 3.3 %weight_grad.1 = f32[2,32,64,128]{3,2,1,0:T(8,128)} custom-call(f32[2,2,32,128]{3,2,1,0:T(8,128)S(1)} %get-tuple-element.59.modes_ref, f32[2,2,32,128]{3,2,1,0:T(8,128)S(1)} %get-tuple-element.60.dmixed_ref), custom_call_target="tpu_custom_call" | custom-call | tf_op jit(solution)/shard_map/weight_grad/pallas_call | solution.py:599
  79.4 0.0 collective-permute-done.18
  79.4 0.0 collective-permute-done.17
  79.4 0.5 collective-permute-done.16
  80.0 0.1 collective-permute-start.19
  80.0 0.7 front_part.3.inv_ref
  80.7 1.2 %collective-permute-done.19.behind_ref = f32[16,2,32,128]{3,2,1,0:T(8,128)S(1)} collective-permute-done((f32[16,2,32,128]{3,2,1,0:T(8,128)S(1)}, f32[16,2,32,128]{3,2,1,0:T(8,128)S(1)}, u32[]{:S(2)}, u32[]{:S(2)}) %collective-permute-start.19) | collective-permute-done | bytes 524320 | tf_op jit(solution)/shard_map/ppermute | solution.py:445
  81.9 3.4 %input_grad.1 = f32[16,2,64,512]{3,2,1,0:T(8,128)} custom-call(f32[16,2,64,512]{3,2,1,0:T(8,128)S(1)} %local_backward.1.local_ref, f32[16,2,32,128]{3,2,1,0:T(8,128)S(1)} %collective-permute-done.19.behind_ref, f32[2,4,128,128]{3,2,1,0:T(8,128)S(1)} %front_part.3.inv_ref, bf16[256,512]{1,0:T(8,128)(2,1)S(1)} %copy-done.3, ...), custom_call_target="tpu_custom_call" | custom-call | tf_op jit(solution)/shard_map/input_grad/pallas_call | solution.py:609
  (18 shorter events, 0.2 us)
Async XLA Ops:
  0.6 10.6 %copy-start = (f32[16,2,512,64]{2,3,1,0:T(8,128)S(1)}, f32[16,2,512,64]{2,3,1,0:T(8,128)}, u32[]{:S(2)}) copy-start(f32[16,2,512,64]{2,3,1,0:T(8,128)} %param.9) | copy-start | bytes 12582916
  0.6 10.6 %copy-start.6 = (f32[64,64]{1,0:T(8,128)S(1)}, f32[64,64]{1,0:T(8,128)}, u32[]{:S(2)}) copy-start(f32[64,64]{1,0:T(8,128)} %weight.1) | copy-start | bytes 49156
  0.7 10.6 %copy-start.7 = (f32[64]{0:T(128)S(1)}, f32[64]{0:T(128)}, u32[]{:S(2)}) copy-start(f32[64]{0:T(128)} %param.12) | copy-start | bytes 772
  4.6 2.1 %collective-permute-start = (f32[16,2,32,128]{3,2,1,0:T(8,128)S(1)}, f32[16,2,32,128]{3,2,1,0:T(8,128)S(1)}, u32[]{:S(2)}, u32[]{:S(2)}) collective-permute-start(f32[16,2,32,128]{3,2,1,0:T(8,128)S(1)} %get-tuple-element.35), channel_id=1, source_target_pairs={{0,1},{1,0},{2,3},{3,2},{4,5},{5,4},{6,7},{7,6},{8,9},{9,8},{10,11... | collective-permute-start | bytes 1572872 | tf_op jit(solution)/shard_map/ppermute | solution.py:445
  6.7 7.1 %collective-permute-start.3 = (f32[4,2,32,128]{3,2,1,0:T(8,128)S(1)}, f32[4,2,32,128]{3,2,1,0:T(8,128)S(1)}, u32[]{:S(2)}, u32[]{:S(2)}) collective-permute-start(f32[4,2,32,128]{3,2,1,0:T(8,128)S(1)} %get-tuple-element.70), channel_id=1, source_target_pairs={{0,2},{1,3},{2,0},{3,1},{4,6},{5,7},{6,4},{7,5},{8,10},{9,11},{10,... | collective-permute-start | bytes 393224 | tf_op jit(solution)/shard_map/ppermute | solution.py:445
  9.7 6.4 %collective-permute-start.2 = (f32[4,2,32,128]{3,2,1,0:T(8,128)S(1)}, f32[4,2,32,128]{3,2,1,0:T(8,128)S(1)}, u32[]{:S(2)}, u32[]{:S(2)}) collective-permute-start(f32[4,2,32,128]{3,2,1,0:T(8,128)S(1)} %get-tuple-element.71), channel_id=1, source_target_pairs={{0,4},{1,5},{2,6},{3,7},{4,0},{5,1},{6,2},{7,3},{8,12},{9,13},{10,... | collective-permute-start | bytes 393224 | tf_op jit(solution)/shard_map/ppermute | solution.py:445
  11.2 6.3 %collective-permute-start.1 = (f32[4,2,32,128]{3,2,1,0:T(8,128)S(1)}, f32[4,2,32,128]{3,2,1,0:T(8,128)S(1)}, u32[]{:S(2)}, u32[]{:S(2)}) collective-permute-start(f32[4,2,32,128]{3,2,1,0:T(8,128)S(1)} %get-tuple-element.72), channel_id=1, source_target_pairs={{0,6},{1,7},{2,4},{3,5},{4,2},{5,3},{6,0},{7,1},{8,14},{9,15},{10,... | collective-permute-start | bytes 393224 | tf_op jit(solution)/shard_map/ppermute | solution.py:445
  11.3 11.5 %copy-start.1 = (f32[2,32,64,128]{3,2,1,0:T(8,128)S(1)}, f32[2,32,64,128]{3,2,1,0:T(8,128)}, u32[]{:S(2)}) copy-start(f32[2,32,64,128]{3,2,1,0:T(8,128)} %refs_6_.3) | copy-start | bytes 6291460
  13.7 27.0 %copy-start.2 = (f32[16,2,512,64]{2,3,1,0:T(8,128)S(1)}, f32[16,2,512,64]{2,3,1,0:T(8,128)}, u32[]{:S(2)}) copy-start(f32[16,2,512,64]{2,3,1,0:T(8,128)} %param.13) | copy-start | bytes 12582916
  13.8 27.0 %copy-start.4 = (bf16[256,512]{1,0:T(8,128)(2,1)S(1)}, bf16[256,512]{1,0:T(8,128)(2,1)}, u32[]{:S(2)}) copy-start(bf16[256,512]{1,0:T(8,128)(2,1)} %constant.11.clone.synth_ref) | copy-start | bytes 786436
  13.8 27.0 %copy-start.5 = (bf16[512,256]{1,0:T(8,128)(2,1)S(1)}, bf16[512,256]{1,0:T(8,128)(2,1)}, u32[]{:S(2)}) copy-start(bf16[512,256]{1,0:T(8,128)(2,1)} %constant.9.clone.table_ref) | copy-start | bytes 786436
  17.6 5.2 %collective-permute-start.4 = (f32[2,2,32,128]{3,2,1,0:T(8,128)S(1)}, f32[2,2,32,128]{3,2,1,0:T(8,128)S(1)}, u32[]{:S(2)}, u32[]{:S(2)}) collective-permute-start(f32[2,2,32,128]{3,2,1,0:T(8,128)S(1)} %slice_add_fusion.7), channel_id=1, source_target_pairs={{0,8},{1,9},{2,10},{3,11},{4,12},{5,13},{6,14},{7,15},{8,0},{9,1},... | collective-permute-start | bytes 196616 | tf_op jit(solution)/shard_map/ppermute | solution.py:445
  24.1 5.2 %collective-permute-start.5 = (f32[2,2,32,128]{3,2,1,0:T(8,128)S(1)}, f32[2,2,32,128]{3,2,1,0:T(8,128)S(1)}, u32[]{:S(2)}, u32[]{:S(2)}) collective-permute-start(f32[2,2,32,128]{3,2,1,0:T(8,128)S(1)} %get-tuple-element.44), channel_id=1, source_target_pairs={{0,8},{1,9},{2,10},{3,11},{4,12},{5,13},{6,14},{7,15},{8,0},{9,1},... | collective-permute-start | bytes 196616 | tf_op jit(solution)/shard_map/ppermute | solution.py:445
  29.3 6.3 %collective-permute-start.6 = (f32[4,2,32,128]{3,2,1,0:T(8,128)S(1)}, f32[4,2,32,128]{3,2,1,0:T(8,128)S(1)}, u32[]{:S(2)}, u32[]{:S(2)}) collective-permute-start(f32[4,2,32,128]{3,2,1,0:T(8,128)S(1)} %get-tuple-element.77), channel_id=1, source_target_pairs={{0,2},{1,3},{2,0},{3,1},{4,6},{5,7},{6,4},{7,5},{8,10},{9,11},{10,... | collective-permute-start | bytes 393224 | tf_op jit(solution)/shard_map/ppermute | solution.py:445
  31.1 5.0 %collective-permute-start.7 = (f32[4,2,32,128]{3,2,1,0:T(8,128)S(1)}, f32[4,2,32,128]{3,2,1,0:T(8,128)S(1)}, u32[]{:S(2)}, u32[]{:S(2)}) collective-permute-start(f32[4,2,32,128]{3,2,1,0:T(8,128)S(1)} %get-tuple-element.77), channel_id=1, source_target_pairs={{0,4},{1,5},{2,6},{3,7},{4,0},{5,1},{6,2},{7,3},{8,12},{9,13},{10,... | collective-permute-start | bytes 393224 | tf_op jit(solution)/shard_map/ppermute | solution.py:445
  32.9 5.9 %collective-permute-start.8 = (f32[4,2,32,128]{3,2,1,0:T(8,128)S(1)}, f32[4,2,32,128]{3,2,1,0:T(8,128)S(1)}, u32[]{:S(2)}, u32[]{:S(2)}) collective-permute-start(f32[4,2,32,128]{3,2,1,0:T(8,128)S(1)} %get-tuple-element.77), channel_id=1, source_target_pairs={{0,6},{1,7},{2,4},{3,5},{4,2},{5,3},{6,0},{7,1},{8,14},{9,15},{10,... | collective-permute-start | bytes 393224 | tf_op jit(solution)/shard_map/ppermute | solution.py:445
  38.8 2.0 %collective-permute-start.9 = (f32[16,2,32,128]{3,2,1,0:T(8,128)S(1)}, f32[16,2,32,128]{3,2,1,0:T(8,128)S(1)}, u32[]{:S(2)}, u32[]{:S(2)}) collective-permute-start(f32[16,2,32,128]{3,2,1,0:T(8,128)S(1)} %constant_dynamic-update-slice_fusion.2.front_ref), channel_id=1, source_target_pairs={{0,1},{1,0},{2,3},{3,2},{4,5},{5,4},{6,7},{7,6},{8,9},{9,8},{10,11... | collective-permute-start | bytes 1572872 | tf_op jit(solution)/shard_map/ppermute | solution.py:445
  48.0 1.9 %collective-permute-start.10 = (f32[16,2,32,128]{3,2,1,0:T(8,128)S(1)}, f32[16,2,32,128]{3,2,1,0:T(8,128)S(1)}, u32[]{:S(2)}, u32[]{:S(2)}) collective-permute-start(f32[16,2,32,128]{3,2,1,0:T(8,128)S(1)} %get-tuple-element.49), channel_id=1, source_target_pairs={{0,1},{1,0},{2,3},{3,2},{4,5},{5,4},{6,7},{7,6},{8,9},{9,8},{10,11... | collective-permute-start | bytes 1572872 | tf_op jit(solution)/shard_map/ppermute | solution.py:445
  50.0 5.7 %collective-permute-start.13 = (f32[4,2,32,128]{3,2,1,0:T(8,128)S(1)}, f32[4,2,32,128]{3,2,1,0:T(8,128)S(1)}, u32[]{:S(2)}, u32[]{:S(2)}) collective-permute-start(f32[4,2,32,128]{3,2,1,0:T(8,128)S(1)} %get-tuple-element.67), channel_id=1, source_target_pairs={{0,2},{1,3},{2,0},{3,1},{4,6},{5,7},{6,4},{7,5},{8,10},{9,11},{10,... | collective-permute-start | bytes 393224 | tf_op jit(solution)/shard_map/ppermute | solution.py:445
  50.6 6.4 %collective-permute-start.12 = (f32[4,2,32,128]{3,2,1,0:T(8,128)S(1)}, f32[4,2,32,128]{3,2,1,0:T(8,128)S(1)}, u32[]{:S(2)}, u32[]{:S(2)}) collective-permute-start(f32[4,2,32,128]{3,2,1,0:T(8,128)S(1)} %get-tuple-element.68), channel_id=1, source_target_pairs={{0,4},{1,5},{2,6},{3,7},{4,0},{5,1},{6,2},{7,3},{8,12},{9,13},{10,... | collective-permute-start | bytes 393224 | tf_op jit(solution)/shard_map/ppermute | solution.py:445
  52.1 7.6 %collective-permute-start.11 = (f32[4,2,32,128]{3,2,1,0:T(8,128)S(1)}, f32[4,2,32,128]{3,2,1,0:T(8,128)S(1)}, u32[]{:S(2)}, u32[]{:S(2)}) collective-permute-start(f32[4,2,32,128]{3,2,1,0:T(8,128)S(1)} %get-tuple-element.69), channel_id=1, source_target_pairs={{0,6},{1,7},{2,4},{3,5},{4,2},{5,3},{6,0},{7,1},{8,14},{9,15},{10,... | collective-permute-start | bytes 393224 | tf_op jit(solution)/shard_map/ppermute | solution.py:445
  59.6 22.3 %copy-start.3 = (bf16[256,512]{1,0:T(8,128)(2,1)S(1)}, bf16[256,512]{1,0:T(8,128)(2,1)}, u32[]{:S(2)}) copy-start(bf16[256,512]{1,0:T(8,128)(2,1)} %constant.10.clone.synth_ref) | copy-start | bytes 786436
  59.7 5.9 %collective-permute-start.14 = (f32[2,2,32,128]{3,2,1,0:T(8,128)S(1)}, f32[2,2,32,128]{3,2,1,0:T(8,128)S(1)}, u32[]{:S(2)}, u32[]{:S(2)}) collective-permute-start(f32[2,2,32,128]{3,2,1,0:T(8,128)S(1)} %slice_add_fusion.6), channel_id=1, source_target_pairs={{0,8},{1,9},{2,10},{3,11},{4,12},{5,13},{6,14},{7,15},{8,0},{9,1},... | collective-permute-start | bytes 196616 | tf_op jit(solution)/shard_map/ppermute | solution.py:445
  67.2 5.4 %collective-permute-start.15 = (f32[2,2,32,128]{3,2,1,0:T(8,128)S(1)}, f32[2,2,32,128]{3,2,1,0:T(8,128)S(1)}, u32[]{:S(2)}, u32[]{:S(2)}) collective-permute-start(f32[2,2,32,128]{3,2,1,0:T(8,128)S(1)} %get-tuple-element.58), channel_id=1, source_target_pairs={{0,8},{1,9},{2,10},{3,11},{4,12},{5,13},{6,14},{7,15},{8,0},{9,1},... | collective-permute-start | bytes 196616 | tf_op jit(solution)/shard_map/ppermute | solution.py:445
  72.6 6.8 %collective-permute-start.18 = (f32[4,2,32,128]{3,2,1,0:T(8,128)S(1)}, f32[4,2,32,128]{3,2,1,0:T(8,128)S(1)}, u32[]{:S(2)}, u32[]{:S(2)}) collective-permute-start(f32[4,2,32,128]{3,2,1,0:T(8,128)S(1)} %get-tuple-element.73), channel_id=1, source_target_pairs={{0,6},{1,7},{2,4},{3,5},{4,2},{5,3},{6,0},{7,1},{8,14},{9,15},{10,... | collective-permute-start | bytes 393224 | tf_op jit(solution)/shard_map/ppermute | solution.py:445
  74.0 5.4 %collective-permute-start.17 = (f32[4,2,32,128]{3,2,1,0:T(8,128)S(1)}, f32[4,2,32,128]{3,2,1,0:T(8,128)S(1)}, u32[]{:S(2)}, u32[]{:S(2)}) collective-permute-start(f32[4,2,32,128]{3,2,1,0:T(8,128)S(1)} %get-tuple-element.73), channel_id=1, source_target_pairs={{0,4},{1,5},{2,6},{3,7},{4,0},{5,1},{6,2},{7,3},{8,12},{9,13},{10,... | collective-permute-start | bytes 393224 | tf_op jit(solution)/shard_map/ppermute | solution.py:445
  74.2 5.7 %collective-permute-start.16 = (f32[4,2,32,128]{3,2,1,0:T(8,128)S(1)}, f32[4,2,32,128]{3,2,1,0:T(8,128)S(1)}, u32[]{:S(2)}, u32[]{:S(2)}) collective-permute-start(f32[4,2,32,128]{3,2,1,0:T(8,128)S(1)} %get-tuple-element.73), channel_id=1, source_target_pairs={{0,2},{1,3},{2,0},{3,1},{4,6},{5,7},{6,4},{7,5},{8,10},{9,11},{10,... | collective-permute-start | bytes 393224 | tf_op jit(solution)/shard_map/ppermute | solution.py:445
  80.0 2.0 %collective-permute-start.19 = (f32[16,2,32,128]{3,2,1,0:T(8,128)S(1)}, f32[16,2,32,128]{3,2,1,0:T(8,128)S(1)}, u32[]{:S(2)}, u32[]{:S(2)}) collective-permute-start(f32[16,2,32,128]{3,2,1,0:T(8,128)S(1)} %constant_dynamic-update-slice_fusion.9.front_ref), channel_id=1, source_target_pairs={{0,1},{1,0},{2,3},{3,2},{4,5},{5,4},{6,7},{7,6},{8,9},{9,8},{10,11... | collective-permute-start | bytes 1572872 | tf_op jit(solution)/shard_map/ppermute | solution.py:445

commit v6 on v5

--- a/solution.py
+++ b/solution.py
@@ -460,7 +460,7 @@
         return total
 
     quarter = keep.shape[0] // 4
-    moved = [swap(part(quarter * place, quarter), 2 * place) for place in (3, 2, 1)]
+    moved = [swap(part(quarter * place, quarter), 2 * place) for place in (3, 1, 2)]
     moved, done = beside(moved, work)
     pieces += moved
     for mask in stage_masks()[3:]:
@@ -472,7 +472,8 @@
 def gather_all(values, front_work, work=None):
     for mask in reversed(stage_masks()[3:]):
         values = jnp.concatenate([values, swap(values, mask)], axis=0)
-    moved = {place: swap(values, 2 * place) for place in (3, 1, 2)}
+    order = (1, 3, 2) if work is None else (3, 1, 2)
+    moved = {place: swap(values, 2 * place) for place in order}
     done = None
     if work is not None:
         moved, done = beside(moved, work)

time: 85.7 us -> 85 us (level)
  transfers between devices with their start and end apart: 20 -> 20, of which waited for: 16 -> 15; matrix products, arithmetic and copies ran while one was open for 0% -> 0% of each run, Pallas kernels for 12% -> 12%
where the time goes in v6:
time: 85 us; the launch traced here: 84.9 us
  waiting for transfers between devices  29.3 us (34%)
  Pallas kernels  27.6 us (32%)
  starting transfers between devices  26.6 us (31%)
  between operations  1.04 us (1%)
    ppermute x20, waiting for transfers between devices, swap(): return lax.ppermute(values, 'stream', [(i, i ^ mask) for i in range(count)])  29.3 us
    ppermute x20, starting transfers between devices, swap(): return lax.ppermute(values, 'stream', [(i, i ^ mask) for i in range(count)])  26.6 us
    pallas_call x1, Pallas kernels, per_device(): pl.pallas_call(middle_kernel, in_specs=[here] * 8, out_specs=[here] * 4,...  7.28 us
    pallas_call x1, Pallas kernels, per_device(): pl.pallas_call(functools.partial(spanwise_kernel, (owned, total_modes, ce...  3.93 us
    pallas_call x1, Pallas kernels, per_device(): pl.pallas_call(input_grad_kernel, in_specs=[here] * 5, out_specs=apart, o...  3.39 us
    pallas_call x1, Pallas kernels, weight_grad(): pl.pallas_call(weight_grad_kernel, in_specs=[here] * 2, out_specs=here, o...  3.26 us
    pallas_call x1, Pallas kernels, local_forward(): pl.pallas_call(functools.partial(pointwise_kernel, True), in_specs=[here]...  2.46 us
    pallas_call x1, Pallas kernels, local_backward(): pl.pallas_call(lambda values, weight, out: pointwise_kernel(False, values...  2.15 us
  transfers between devices with their start and end apart: 20, of which 15 were waited for; matrix products, arithmetic and copies ran while one was open for 0% of the time, Pallas kernels for 12%

profile of v6, /device:TPU:0, one launch (start us, length us, event | category | flops | bytes accessed | tf_op | source)
XLA Modules:
  0.0 84.9 jit_solution(17476821034190109506)
XLA Ops:
  0.6 0.0 copy-start
  0.6 0.0 copy-start.6
  0.7 0.0 copy-start.7
  0.7 3.9 %spanwise.1 = (f32[16,2,32,128]{3,2,1,0:T(8,128)S(1)}, f32[2,4,256,128]{3,2,1,0:T(8,128)S(1)}, bf16[2,256,256]{2,1,0:T(8,128)(2,1)S(1)}, bf16[2,256,256]{2,1,0:T(8,128)(2,1)S(1)}) custom-call(f32[16,2,64,512]{3,2,1,0:T(8,128)} %bitcast.5, bf16[512,256]{1,0:T(8,128)(2,1)} %constant.8.clone.table_hbm), custom_call_target="tpu_custom_call" | custom-call | tf_op jit(solution)/shard_map/spanwise/pallas_call | solution.py:519
  4.6 0.5 collective-permute-start
  5.1 0.4 keep_part.2.refs_0_
  5.6 1.1 %collective-permute-done.refs_1_ = f32[16,2,32,128]{3,2,1,0:T(8,128)S(1)} collective-permute-done((f32[16,2,32,128]{3,2,1,0:T(8,128)S(1)}, f32[16,2,32,128]{3,2,1,0:T(8,128)S(1)}, u32[]{:S(2)}, u32[]{:S(2)}) %collective-permute-start) | collective-permute-done | bytes 524320 | tf_op jit(solution)/shard_map/ppermute | solution.py:445
  6.7 0.1 slice_add_fusion.3
  6.7 3.0 %collective-permute-start.3 = (f32[4,2,32,128]{3,2,1,0:T(8,128)S(1)}, f32[4,2,32,128]{3,2,1,0:T(8,128)S(1)}, u32[]{:S(2)}, u32[]{:S(2)}) collective-permute-start(f32[4,2,32,128]{3,2,1,0:T(8,128)S(1)} %get-tuple-element.70), channel_id=1, source_target_pairs={{0,4},{1,5},{2,6},{3,7},{4,0},{5,1},{6,2},{7,3},{8,12},{9,13},{10,... | collective-permute-start | bytes 393224 | tf_op jit(solution)/shard_map/ppermute | solution.py:445
  9.7 1.5 %collective-permute-start.2 = (f32[4,2,32,128]{3,2,1,0:T(8,128)S(1)}, f32[4,2,32,128]{3,2,1,0:T(8,128)S(1)}, u32[]{:S(2)}, u32[]{:S(2)}) collective-permute-start(f32[4,2,32,128]{3,2,1,0:T(8,128)S(1)} %get-tuple-element.71), channel_id=1, source_target_pairs={{0,2},{1,3},{2,0},{3,1},{4,6},{5,7},{6,4},{7,5},{8,10},{9,11},{10,... | collective-permute-start | bytes 393224 | tf_op jit(solution)/shard_map/ppermute | solution.py:445
  11.2 0.0 collective-permute-start.1
  11.3 0.0 copy-done
  11.3 0.0 copy-done.6
  11.3 2.5 %local_forward.1.local_ref = f32[16,2,64,512]{3,2,1,0:T(8,128)S(1)} custom-call(f32[16,2,64,512]{3,2,1,0:T(8,128)S(1)} %bitcast.6, f32[64,64]{1,0:T(8,128)S(1)} %copy-done.6, f32[1,64]{1,0:T(1,128)S(1)} %bitcast.8), custom_call_target="tpu_custom_call" | custom-call | tf_op jit(solution)/shard_map/local_forward/pallas_call | solution.py:550
  13.8 0.0 copy-start.2
  13.8 0.0 copy-start.4
  13.8 0.0 copy-start.5
  13.8 0.0 collective-permute-done.3.refs_4_
  13.8 4.0 %collective-permute-done.2.refs_3_ = f32[4,2,32,128]{3,2,1,0:T(8,128)S(1)} collective-permute-done((f32[4,2,32,128]{3,2,1,0:T(8,128)S(1)}, f32[4,2,32,128]{3,2,1,0:T(8,128)S(1)}, u32[]{:S(2)}, u32[]{:S(2)}) %collective-permute-start.2) | collective-permute-done | bytes 131104 | tf_op jit(solution)/shard_map/ppermute | solution.py:445
  17.8 0.0 collective-permute-done.1.refs_2_
  17.8 2.7 %collective-permute-start.4 = (f32[2,2,32,128]{3,2,1,0:T(8,128)S(1)}, f32[2,2,32,128]{3,2,1,0:T(8,128)S(1)}, u32[]{:S(2)}, u32[]{:S(2)}) collective-permute-start(f32[2,2,32,128]{3,2,1,0:T(8,128)S(1)} %slice_add_fusion.7), channel_id=1, source_target_pairs={{0,8},{1,9},{2,10},{3,11},{4,12},{5,13},{6,14},{7,15},{8,0},{9,1},... | collective-permute-start | bytes 196616 | tf_op jit(solution)/shard_map/ppermute | solution.py:445
  20.5 2.6 %collective-permute-done.4.refs_5_ = f32[2,2,32,128]{3,2,1,0:T(8,128)S(1)} collective-permute-done((f32[2,2,32,128]{3,2,1,0:T(8,128)S(1)}, f32[2,2,32,128]{3,2,1,0:T(8,128)S(1)}, u32[]{:S(2)}, u32[]{:S(2)}) %collective-permute-start.4) | collective-permute-done | bytes 65568 | tf_op jit(solution)/shard_map/ppermute | solution.py:445
  23.1 0.0 copy-done.1
  23.1 1.3 %mix.1 = (f32[2,2,32,128]{3,2,1,0:T(8,128)S(1)}, f32[2,2,32,128]{3,2,1,0:T(8,128)S(1)}) custom-call(f32[16,2,32,128]{3,2,1,0:T(8,128)S(1)} %keep_part.2.refs_0_, f32[16,2,32,128]{3,2,1,0:T(8,128)S(1)} %collective-permute-done.refs_1_, f32[4,2,32,128]{3,2,1,0:T(8,128)S(1)} %collective-permute-done.1.refs_2_, ...), custom_call_target="tpu_custom_call" | custom-call | tf_op jit(solution)/shard_map/mix/pallas_call | solution.py:560
  24.4 2.7 %collective-permute-start.5 = (f32[2,2,32,128]{3,2,1,0:T(8,128)S(1)}, f32[2,2,32,128]{3,2,1,0:T(8,128)S(1)}, u32[]{:S(2)}, u32[]{:S(2)}) collective-permute-start(f32[2,2,32,128]{3,2,1,0:T(8,128)S(1)} %get-tuple-element.44), channel_id=1, source_target_pairs={{0,8},{1,9},{2,10},{3,11},{4,12},{5,13},{6,14},{7,15},{8,0},{9,1},... | collective-permute-start | bytes 196616 | tf_op jit(solution)/shard_map/ppermute | solution.py:445
  27.1 2.5 %collective-permute-done.5 = f32[2,2,32,128]{3,2,1,0:T(8,128)S(1)} collective-permute-done((f32[2,2,32,128]{3,2,1,0:T(8,128)S(1)}, f32[2,2,32,128]{3,2,1,0:T(8,128)S(1)}, u32[]{:S(2)}, u32[]{:S(2)}) %collective-permute-start.5) | collective-permute-done | bytes 65568 | tf_op jit(solution)/shard_map/ppermute | solution.py:445
  29.6 2.3 %collective-permute-start.6 = (f32[4,2,32,128]{3,2,1,0:T(8,128)S(1)}, f32[4,2,32,128]{3,2,1,0:T(8,128)S(1)}, u32[]{:S(2)}, u32[]{:S(2)}) collective-permute-start(f32[4,2,32,128]{3,2,1,0:T(8,128)S(1)} %get-tuple-element.77), channel_id=1, source_target_pairs={{0,2},{1,3},{2,0},{3,1},{4,6},{5,7},{6,4},{7,5},{8,10},{9,11},{10,... | collective-permute-start | bytes 393224 | tf_op jit(solution)/shard_map/ppermute | solution.py:445
  31.9 0.0 collective-permute-start.7
  31.9 1.5 %collective-permute-start.8 = (f32[4,2,32,128]{3,2,1,0:T(8,128)S(1)}, f32[4,2,32,128]{3,2,1,0:T(8,128)S(1)}, u32[]{:S(2)}, u32[]{:S(2)}) collective-permute-start(f32[4,2,32,128]{3,2,1,0:T(8,128)S(1)} %get-tuple-element.77), channel_id=1, source_target_pairs={{0,6},{1,7},{2,4},{3,5},{4,2},{5,3},{6,0},{7,1},{8,14},{9,15},{10,... | collective-permute-start | bytes 393224 | tf_op jit(solution)/shard_map/ppermute | solution.py:445
  33.4 2.0 %collective-permute-done.6 = f32[4,2,32,128]{3,2,1,0:T(8,128)S(1)} collective-permute-done((f32[4,2,32,128]{3,2,1,0:T(8,128)S(1)}, f32[4,2,32,128]{3,2,1,0:T(8,128)S(1)}, u32[]{:S(2)}, u32[]{:S(2)}) %collective-permute-start.6) | collective-permute-done | bytes 131104 | tf_op jit(solution)/shard_map/ppermute | solution.py:445
  35.4 1.4 %collective-permute-done.7 = f32[4,2,32,128]{3,2,1,0:T(8,128)S(1)} collective-permute-done((f32[4,2,32,128]{3,2,1,0:T(8,128)S(1)}, f32[4,2,32,128]{3,2,1,0:T(8,128)S(1)}, u32[]{:S(2)}, u32[]{:S(2)}) %collective-permute-start.7) | collective-permute-done | bytes 131104 | tf_op jit(solution)/shard_map/ppermute | solution.py:445
  36.9 0.9 %collective-permute-done.8 = f32[4,2,32,128]{3,2,1,0:T(8,128)S(1)} collective-permute-done((f32[4,2,32,128]{3,2,1,0:T(8,128)S(1)}, f32[4,2,32,128]{3,2,1,0:T(8,128)S(1)}, u32[]{:S(2)}, u32[]{:S(2)}) %collective-permute-start.8) | collective-permute-done | bytes 131104 | tf_op jit(solution)/shard_map/ppermute | solution.py:445
  37.8 0.1 collective-permute-start.9
  37.9 0.7 front_part.2.inv_ref
  38.5 1.2 %collective-permute-done.9.behind_ref = f32[16,2,32,128]{3,2,1,0:T(8,128)S(1)} collective-permute-done((f32[16,2,32,128]{3,2,1,0:T(8,128)S(1)}, f32[16,2,32,128]{3,2,1,0:T(8,128)S(1)}, u32[]{:S(2)}, u32[]{:S(2)}) %collective-permute-start.9) | collective-permute-done | bytes 524320 | tf_op jit(solution)/shard_map/ppermute | solution.py:445
  39.8 7.3 %middle.1 = (f32[16,2,64,512]{3,2,1,0:T(8,128)}, f32[16,2,64,512]{3,2,1,0:T(8,128)S(1)}, f32[16,2,32,128]{3,2,1,0:T(8,128)S(1)}, f32[2,4,256,128]{3,2,1,0:T(8,128)S(1)}) custom-call(f32[16,2,64,512]{3,2,1,0:T(8,128)S(1)} %local_forward.1.local_ref, f32[16,2,64,512]{3,2,1,0:T(8,128)S(1)} %bitcast.7, f32[16,2,32,128]{3,2,1,0:T(8,128)S(1)} %collective-permute-done.9.behind_ref, ...), custom_call_target="tpu_custom_call" | custom-call | tf_op jit(solution)/shard_map/middle/pallas_call | solution.py:569
  47.0 0.1 collective-permute-start.10
  47.2 0.4 keep_part.3.refs_0_
  47.6 1.3 %collective-permute-done.10.refs_1_ = f32[16,2,32,128]{3,2,1,0:T(8,128)S(1)} collective-permute-done((f32[16,2,32,128]{3,2,1,0:T(8,128)S(1)}, f32[16,2,32,128]{3,2,1,0:T(8,128)S(1)}, u32[]{:S(2)}, u32[]{:S(2)}) %collective-permute-start.10) | collective-permute-done | bytes 524320 | tf_op jit(solution)/shard_map/ppermute | solution.py:445
  49.0 0.1 slice_add_fusion
  49.0 2.1 %collective-permute-start.13 = (f32[4,2,32,128]{3,2,1,0:T(8,128)S(1)}, f32[4,2,32,128]{3,2,1,0:T(8,128)S(1)}, u32[]{:S(2)}, u32[]{:S(2)}) collective-permute-start(f32[4,2,32,128]{3,2,1,0:T(8,128)S(1)} %get-tuple-element.67), channel_id=1, source_target_pairs={{0,4},{1,5},{2,6},{3,7},{4,0},{5,1},{6,2},{7,3},{8,12},{9,13},{10,... | collective-permute-start | bytes 393224 | tf_op jit(solution)/shard_map/ppermute | solution.py:445
  51.1 0.1 collective-permute-start.12
  51.2 1.5 %collective-permute-start.11 = (f32[4,2,32,128]{3,2,1,0:T(8,128)S(1)}, f32[4,2,32,128]{3,2,1,0:T(8,128)S(1)}, u32[]{:S(2)}, u32[]{:S(2)}) collective-permute-start(f32[4,2,32,128]{3,2,1,0:T(8,128)S(1)} %get-tuple-element.69), channel_id=1, source_target_pairs={{0,6},{1,7},{2,4},{3,5},{4,2},{5,3},{6,0},{7,1},{8,14},{9,15},{10,... | collective-permute-start | bytes 393224 | tf_op jit(solution)/shard_map/ppermute | solution.py:445
  52.6 2.1 %local_backward.1.local_ref = f32[16,2,64,512]{3,2,1,0:T(8,128)S(1)} custom-call(f32[16,2,64,512]{3,2,1,0:T(8,128)S(1)} %get-tuple-element.53.values, f32[64,64]{1,0:T(8,128)S(1)} %copy-done.6), custom_call_target="tpu_custom_call" | custom-call | tf_op jit(solution)/shard_map/local_backward/pallas_call | solution.py:580
  54.8 0.2 collective-permute-done.13.refs_4_
  55.0 4.2 %collective-permute-done.12.refs_3_ = f32[4,2,32,128]{3,2,1,0:T(8,128)S(1)} collective-permute-done((f32[4,2,32,128]{3,2,1,0:T(8,128)S(1)}, f32[4,2,32,128]{3,2,1,0:T(8,128)S(1)}, u32[]{:S(2)}, u32[]{:S(2)}) %collective-permute-start.12) | collective-permute-done | bytes 131104 | tf_op jit(solution)/shard_map/ppermute | solution.py:445
  59.2 0.0 collective-permute-done.11.refs_2_
  59.2 0.0 copy-start.3
  59.2 2.7 %collective-permute-start.14 = (f32[2,2,32,128]{3,2,1,0:T(8,128)S(1)}, f32[2,2,32,128]{3,2,1,0:T(8,128)S(1)}, u32[]{:S(2)}, u32[]{:S(2)}) collective-permute-start(f32[2,2,32,128]{3,2,1,0:T(8,128)S(1)} %slice_add_fusion.6), channel_id=1, source_target_pairs={{0,8},{1,9},{2,10},{3,11},{4,12},{5,13},{6,14},{7,15},{8,0},{9,1},... | collective-permute-start | bytes 196616 | tf_op jit(solution)/shard_map/ppermute | solution.py:445
  61.9 3.0 %collective-permute-done.14.refs_5_ = f32[2,2,32,128]{3,2,1,0:T(8,128)S(1)} collective-permute-done((f32[2,2,32,128]{3,2,1,0:T(8,128)S(1)}, f32[2,2,32,128]{3,2,1,0:T(8,128)S(1)}, u32[]{:S(2)}, u32[]{:S(2)}) %collective-permute-start.14) | collective-permute-done | bytes 65568 | tf_op jit(solution)/shard_map/ppermute | solution.py:445
  64.9 1.6 %adjoint.1 = (f32[2,2,32,128]{3,2,1,0:T(8,128)S(1)}, f32[2,2,32,128]{3,2,1,0:T(8,128)S(1)}) custom-call(f32[16,2,32,128]{3,2,1,0:T(8,128)S(1)} %keep_part.3.refs_0_, f32[16,2,32,128]{3,2,1,0:T(8,128)S(1)} %collective-permute-done.10.refs_1_, f32[4,2,32,128]{3,2,1,0:T(8,128)S(1)} %collective-permute-done.11.refs_2_, ...), custom_call_target="tpu_custom_call" | custom-call | tf_op jit(solution)/shard_map/adjoint/pallas_call | solution.py:590
  66.6 2.2 %collective-permute-start.15 = (f32[2,2,32,128]{3,2,1,0:T(8,128)S(1)}, f32[2,2,32,128]{3,2,1,0:T(8,128)S(1)}, u32[]{:S(2)}, u32[]{:S(2)}) collective-permute-start(f32[2,2,32,128]{3,2,1,0:T(8,128)S(1)} %get-tuple-element.58), channel_id=1, source_target_pairs={{0,8},{1,9},{2,10},{3,11},{4,12},{5,13},{6,14},{7,15},{8,0},{9,1},... | collective-permute-start | bytes 196616 | tf_op jit(solution)/shard_map/ppermute | solution.py:445
  68.8 3.2 %collective-permute-done.15 = f32[2,2,32,128]{3,2,1,0:T(8,128)S(1)} collective-permute-done((f32[2,2,32,128]{3,2,1,0:T(8,128)S(1)}, f32[2,2,32,128]{3,2,1,0:T(8,128)S(1)}, u32[]{:S(2)}, u32[]{:S(2)}) %collective-permute-start.15) | collective-permute-done | bytes 65568 | tf_op jit(solution)/shard_map/ppermute | solution.py:445
  72.0 1.2 %collective-permute-start.18 = (f32[4,2,32,128]{3,2,1,0:T(8,128)S(1)}, f32[4,2,32,128]{3,2,1,0:T(8,128)S(1)}, u32[]{:S(2)}, u32[]{:S(2)}) collective-permute-start(f32[4,2,32,128]{3,2,1,0:T(8,128)S(1)} %get-tuple-element.73), channel_id=1, source_target_pairs={{0,6},{1,7},{2,4},{3,5},{4,2},{5,3},{6,0},{7,1},{8,14},{9,15},{10,... | collective-permute-start | bytes 393224 | tf_op jit(solution)/shard_map/ppermute | solution.py:445
  73.1 0.1 collective-permute-start.17
  73.2 2.3 %collective-permute-start.16 = (f32[4,2,32,128]{3,2,1,0:T(8,128)S(1)}, f32[4,2,32,128]{3,2,1,0:T(8,128)S(1)}, u32[]{:S(2)}, u32[]{:S(2)}) collective-permute-start(f32[4,2,32,128]{3,2,1,0:T(8,128)S(1)} %get-tuple-element.73), channel_id=1, source_target_pairs={{0,2},{1,3},{2,0},{3,1},{4,6},{5,7},{6,4},{7,5},{8,10},{9,11},{10,... | collective-permute-start | bytes 393224 | tf_op jit(solution)/shard_map/ppermute | solution.py:445
  75.5 3.3 %weight_grad.1 = f32[2,32,64,128]{3,2,1,0:T(8,128)} custom-call(f32[2,2,32,128]{3,2,1,0:T(8,128)S(1)} %get-tuple-element.59.modes_ref, f32[2,2,32,128]{3,2,1,0:T(8,128)S(1)} %get-tuple-element.60.dmixed_ref), custom_call_target="tpu_custom_call" | custom-call | tf_op jit(solution)/shard_map/weight_grad/pallas_call | solution.py:600
  78.8 0.0 collective-permute-done.18
  78.8 0.0 collective-permute-done.17
  78.8 0.5 collective-permute-done.16
  79.3 0.1 collective-permute-start.19
  79.4 0.7 front_part.3.inv_ref
  80.1 1.2 %collective-permute-done.19.behind_ref = f32[16,2,32,128]{3,2,1,0:T(8,128)S(1)} collective-permute-done((f32[16,2,32,128]{3,2,1,0:T(8,128)S(1)}, f32[16,2,32,128]{3,2,1,0:T(8,128)S(1)}, u32[]{:S(2)}, u32[]{:S(2)}) %collective-permute-start.19) | collective-permute-done | bytes 524320 | tf_op jit(solution)/shard_map/ppermute | solution.py:445
  81.3 3.4 %input_grad.1 = f32[16,2,64,512]{3,2,1,0:T(8,128)} custom-call(f32[16,2,64,512]{3,2,1,0:T(8,128)S(1)} %local_backward.1.local_ref, f32[16,2,32,128]{3,2,1,0:T(8,128)S(1)} %collective-permute-done.19.behind_ref, f32[2,4,128,128]{3,2,1,0:T(8,128)S(1)} %front_part.3.inv_ref, bf16[256,512]{1,0:T(8,128)(2,1)S(1)} %copy-done.3, ...), custom_call_target="tpu_custom_call" | custom-call | tf_op jit(solution)/shard_map/input_grad/pallas_call | solution.py:610
  (18 shorter events, 0.2 us)
Async XLA Ops:
  0.6 10.6 %copy-start = (f32[16,2,512,64]{2,3,1,0:T(8,128)S(1)}, f32[16,2,512,64]{2,3,1,0:T(8,128)}, u32[]{:S(2)}) copy-start(f32[16,2,512,64]{2,3,1,0:T(8,128)} %param.9) | copy-start | bytes 12582916
  0.6 10.6 %copy-start.6 = (f32[64,64]{1,0:T(8,128)S(1)}, f32[64,64]{1,0:T(8,128)}, u32[]{:S(2)}) copy-start(f32[64,64]{1,0:T(8,128)} %weight.1) | copy-start | bytes 49156
  0.7 10.6 %copy-start.7 = (f32[64]{0:T(128)S(1)}, f32[64]{0:T(128)}, u32[]{:S(2)}) copy-start(f32[64]{0:T(128)} %param.12) | copy-start | bytes 772
  4.6 2.1 %collective-permute-start = (f32[16,2,32,128]{3,2,1,0:T(8,128)S(1)}, f32[16,2,32,128]{3,2,1,0:T(8,128)S(1)}, u32[]{:S(2)}, u32[]{:S(2)}) collective-permute-start(f32[16,2,32,128]{3,2,1,0:T(8,128)S(1)} %get-tuple-element.35), channel_id=1, source_target_pairs={{0,1},{1,0},{2,3},{3,2},{4,5},{5,4},{6,7},{7,6},{8,9},{9,8},{10,11... | collective-permute-start | bytes 1572872 | tf_op jit(solution)/shard_map/ppermute | solution.py:445
  6.7 7.1 %collective-permute-start.3 = (f32[4,2,32,128]{3,2,1,0:T(8,128)S(1)}, f32[4,2,32,128]{3,2,1,0:T(8,128)S(1)}, u32[]{:S(2)}, u32[]{:S(2)}) collective-permute-start(f32[4,2,32,128]{3,2,1,0:T(8,128)S(1)} %get-tuple-element.70), channel_id=1, source_target_pairs={{0,4},{1,5},{2,6},{3,7},{4,0},{5,1},{6,2},{7,3},{8,12},{9,13},{10,... | collective-permute-start | bytes 393224 | tf_op jit(solution)/shard_map/ppermute | solution.py:445
  9.7 8.1 %collective-permute-start.2 = (f32[4,2,32,128]{3,2,1,0:T(8,128)S(1)}, f32[4,2,32,128]{3,2,1,0:T(8,128)S(1)}, u32[]{:S(2)}, u32[]{:S(2)}) collective-permute-start(f32[4,2,32,128]{3,2,1,0:T(8,128)S(1)} %get-tuple-element.71), channel_id=1, source_target_pairs={{0,2},{1,3},{2,0},{3,1},{4,6},{5,7},{6,4},{7,5},{8,10},{9,11},{10,... | collective-permute-start | bytes 393224 | tf_op jit(solution)/shard_map/ppermute | solution.py:445
  11.2 6.6 %collective-permute-start.1 = (f32[4,2,32,128]{3,2,1,0:T(8,128)S(1)}, f32[4,2,32,128]{3,2,1,0:T(8,128)S(1)}, u32[]{:S(2)}, u32[]{:S(2)}) collective-permute-start(f32[4,2,32,128]{3,2,1,0:T(8,128)S(1)} %get-tuple-element.72), channel_id=1, source_target_pairs={{0,6},{1,7},{2,4},{3,5},{4,2},{5,3},{6,0},{7,1},{8,14},{9,15},{10,... | collective-permute-start | bytes 393224 | tf_op jit(solution)/shard_map/ppermute | solution.py:445
  11.3 11.8 %copy-start.1 = (f32[2,32,64,128]{3,2,1,0:T(8,128)S(1)}, f32[2,32,64,128]{3,2,1,0:T(8,128)}, u32[]{:S(2)}) copy-start(f32[2,32,64,128]{3,2,1,0:T(8,128)} %refs_6_.3) | copy-start | bytes 6291460
  13.8 26.0 %copy-start.2 = (f32[16,2,512,64]{2,3,1,0:T(8,128)S(1)}, f32[16,2,512,64]{2,3,1,0:T(8,128)}, u32[]{:S(2)}) copy-start(f32[16,2,512,64]{2,3,1,0:T(8,128)} %param.13) | copy-start | bytes 12582916
  13.8 26.0 %copy-start.4 = (bf16[256,512]{1,0:T(8,128)(2,1)S(1)}, bf16[256,512]{1,0:T(8,128)(2,1)}, u32[]{:S(2)}) copy-start(bf16[256,512]{1,0:T(8,128)(2,1)} %constant.11.clone.synth_ref) | copy-start | bytes 786436
  13.8 26.0 %copy-start.5 = (bf16[512,256]{1,0:T(8,128)(2,1)S(1)}, bf16[512,256]{1,0:T(8,128)(2,1)}, u32[]{:S(2)}) copy-start(bf16[512,256]{1,0:T(8,128)(2,1)} %constant.9.clone.table_ref) | copy-start | bytes 786436
  17.8 5.2 %collective-permute-start.4 = (f32[2,2,32,128]{3,2,1,0:T(8,128)S(1)}, f32[2,2,32,128]{3,2,1,0:T(8,128)S(1)}, u32[]{:S(2)}, u32[]{:S(2)}) collective-permute-start(f32[2,2,32,128]{3,2,1,0:T(8,128)S(1)} %slice_add_fusion.7), channel_id=1, source_target_pairs={{0,8},{1,9},{2,10},{3,11},{4,12},{5,13},{6,14},{7,15},{8,0},{9,1},... | collective-permute-start | bytes 196616 | tf_op jit(solution)/shard_map/ppermute | solution.py:445
  24.4 5.2 %collective-permute-start.5 = (f32[2,2,32,128]{3,2,1,0:T(8,128)S(1)}, f32[2,2,32,128]{3,2,1,0:T(8,128)S(1)}, u32[]{:S(2)}, u32[]{:S(2)}) collective-permute-start(f32[2,2,32,128]{3,2,1,0:T(8,128)S(1)} %get-tuple-element.44), channel_id=1, source_target_pairs={{0,8},{1,9},{2,10},{3,11},{4,12},{5,13},{6,14},{7,15},{8,0},{9,1},... | collective-permute-start | bytes 196616 | tf_op jit(solution)/shard_map/ppermute | solution.py:445
  29.6 5.8 %collective-permute-start.6 = (f32[4,2,32,128]{3,2,1,0:T(8,128)S(1)}, f32[4,2,32,128]{3,2,1,0:T(8,128)S(1)}, u32[]{:S(2)}, u32[]{:S(2)}) collective-permute-start(f32[4,2,32,128]{3,2,1,0:T(8,128)S(1)} %get-tuple-element.77), channel_id=1, source_target_pairs={{0,2},{1,3},{2,0},{3,1},{4,6},{5,7},{6,4},{7,5},{8,10},{9,11},{10,... | collective-permute-start | bytes 393224 | tf_op jit(solution)/shard_map/ppermute | solution.py:445
  31.9 5.0 %collective-permute-start.7 = (f32[4,2,32,128]{3,2,1,0:T(8,128)S(1)}, f32[4,2,32,128]{3,2,1,0:T(8,128)S(1)}, u32[]{:S(2)}, u32[]{:S(2)}) collective-permute-start(f32[4,2,32,128]{3,2,1,0:T(8,128)S(1)} %get-tuple-element.77), channel_id=1, source_target_pairs={{0,4},{1,5},{2,6},{3,7},{4,0},{5,1},{6,2},{7,3},{8,12},{9,13},{10,... | collective-permute-start | bytes 393224 | tf_op jit(solution)/shard_map/ppermute | solution.py:445
  31.9 5.9 %collective-permute-start.8 = (f32[4,2,32,128]{3,2,1,0:T(8,128)S(1)}, f32[4,2,32,128]{3,2,1,0:T(8,128)S(1)}, u32[]{:S(2)}, u32[]{:S(2)}) collective-permute-start(f32[4,2,32,128]{3,2,1,0:T(8,128)S(1)} %get-tuple-element.77), channel_id=1, source_target_pairs={{0,6},{1,7},{2,4},{3,5},{4,2},{5,3},{6,0},{7,1},{8,14},{9,15},{10,... | collective-permute-start | bytes 393224 | tf_op jit(solution)/shard_map/ppermute | solution.py:445
  37.8 2.0 %collective-permute-start.9 = (f32[16,2,32,128]{3,2,1,0:T(8,128)S(1)}, f32[16,2,32,128]{3,2,1,0:T(8,128)S(1)}, u32[]{:S(2)}, u32[]{:S(2)}) collective-permute-start(f32[16,2,32,128]{3,2,1,0:T(8,128)S(1)} %constant_dynamic-update-slice_fusion.2.front_ref), channel_id=1, source_target_pairs={{0,1},{1,0},{2,3},{3,2},{4,5},{5,4},{6,7},{7,6},{8,9},{9,8},{10,11... | collective-permute-start | bytes 1572872 | tf_op jit(solution)/shard_map/ppermute | solution.py:445
  47.0 1.9 %collective-permute-start.10 = (f32[16,2,32,128]{3,2,1,0:T(8,128)S(1)}, f32[16,2,32,128]{3,2,1,0:T(8,128)S(1)}, u32[]{:S(2)}, u32[]{:S(2)}) collective-permute-start(f32[16,2,32,128]{3,2,1,0:T(8,128)S(1)} %get-tuple-element.49), channel_id=1, source_target_pairs={{0,1},{1,0},{2,3},{3,2},{4,5},{5,4},{6,7},{7,6},{8,9},{9,8},{10,11... | collective-permute-start | bytes 1572872 | tf_op jit(solution)/shard_map/ppermute | solution.py:445
  49.0 6.0 %collective-permute-start.13 = (f32[4,2,32,128]{3,2,1,0:T(8,128)S(1)}, f32[4,2,32,128]{3,2,1,0:T(8,128)S(1)}, u32[]{:S(2)}, u32[]{:S(2)}) collective-permute-start(f32[4,2,32,128]{3,2,1,0:T(8,128)S(1)} %get-tuple-element.67), channel_id=1, source_target_pairs={{0,4},{1,5},{2,6},{3,7},{4,0},{5,1},{6,2},{7,3},{8,12},{9,13},{10,... | collective-permute-start | bytes 393224 | tf_op jit(solution)/shard_map/ppermute | solution.py:445
  51.1 8.1 %collective-permute-start.12 = (f32[4,2,32,128]{3,2,1,0:T(8,128)S(1)}, f32[4,2,32,128]{3,2,1,0:T(8,128)S(1)}, u32[]{:S(2)}, u32[]{:S(2)}) collective-permute-start(f32[4,2,32,128]{3,2,1,0:T(8,128)S(1)} %get-tuple-element.68), channel_id=1, source_target_pairs={{0,2},{1,3},{2,0},{3,1},{4,6},{5,7},{6,4},{7,5},{8,10},{9,11},{10,... | collective-permute-start | bytes 393224 | tf_op jit(solution)/shard_map/ppermute | solution.py:445
  51.2 8.0 %collective-permute-start.11 = (f32[4,2,32,128]{3,2,1,0:T(8,128)S(1)}, f32[4,2,32,128]{3,2,1,0:T(8,128)S(1)}, u32[]{:S(2)}, u32[]{:S(2)}) collective-permute-start(f32[4,2,32,128]{3,2,1,0:T(8,128)S(1)} %get-tuple-element.69), channel_id=1, source_target_pairs={{0,6},{1,7},{2,4},{3,5},{4,2},{5,3},{6,0},{7,1},{8,14},{9,15},{10,... | collective-permute-start | bytes 393224 | tf_op jit(solution)/shard_map/ppermute | solution.py:445
  59.2 22.1 %copy-start.3 = (bf16[256,512]{1,0:T(8,128)(2,1)S(1)}, bf16[256,512]{1,0:T(8,128)(2,1)}, u32[]{:S(2)}) copy-start(bf16[256,512]{1,0:T(8,128)(2,1)} %constant.10.clone.synth_ref) | copy-start | bytes 786436
  59.2 5.7 %collective-permute-start.14 = (f32[2,2,32,128]{3,2,1,0:T(8,128)S(1)}, f32[2,2,32,128]{3,2,1,0:T(8,128)S(1)}, u32[]{:S(2)}, u32[]{:S(2)}) collective-permute-start(f32[2,2,32,128]{3,2,1,0:T(8,128)S(1)} %slice_add_fusion.6), channel_id=1, source_target_pairs={{0,8},{1,9},{2,10},{3,11},{4,12},{5,13},{6,14},{7,15},{8,0},{9,1},... | collective-permute-start | bytes 196616 | tf_op jit(solution)/shard_map/ppermute | solution.py:445
  66.6 5.4 %collective-permute-start.15 = (f32[2,2,32,128]{3,2,1,0:T(8,128)S(1)}, f32[2,2,32,128]{3,2,1,0:T(8,128)S(1)}, u32[]{:S(2)}, u32[]{:S(2)}) collective-permute-start(f32[2,2,32,128]{3,2,1,0:T(8,128)S(1)} %get-tuple-element.58), channel_id=1, source_target_pairs={{0,8},{1,9},{2,10},{3,11},{4,12},{5,13},{6,14},{7,15},{8,0},{9,1},... | collective-permute-start | bytes 196616 | tf_op jit(solution)/shard_map/ppermute | solution.py:445
  72.0 6.8 %collective-permute-start.18 = (f32[4,2,32,128]{3,2,1,0:T(8,128)S(1)}, f32[4,2,32,128]{3,2,1,0:T(8,128)S(1)}, u32[]{:S(2)}, u32[]{:S(2)}) collective-permute-start(f32[4,2,32,128]{3,2,1,0:T(8,128)S(1)} %get-tuple-element.73), channel_id=1, source_target_pairs={{0,6},{1,7},{2,4},{3,5},{4,2},{5,3},{6,0},{7,1},{8,14},{9,15},{10,... | collective-permute-start | bytes 393224 | tf_op jit(solution)/shard_map/ppermute | solution.py:445
  73.1 5.7 %collective-permute-start.17 = (f32[4,2,32,128]{3,2,1,0:T(8,128)S(1)}, f32[4,2,32,128]{3,2,1,0:T(8,128)S(1)}, u32[]{:S(2)}, u32[]{:S(2)}) collective-permute-start(f32[4,2,32,128]{3,2,1,0:T(8,128)S(1)} %get-tuple-element.73), channel_id=1, source_target_pairs={{0,4},{1,5},{2,6},{3,7},{4,0},{5,1},{6,2},{7,3},{8,12},{9,13},{10,... | collective-permute-start | bytes 393224 | tf_op jit(solution)/shard_map/ppermute | solution.py:445
  73.2 6.1 %collective-permute-start.16 = (f32[4,2,32,128]{3,2,1,0:T(8,128)S(1)}, f32[4,2,32,128]{3,2,1,0:T(8,128)S(1)}, u32[]{:S(2)}, u32[]{:S(2)}) collective-permute-start(f32[4,2,32,128]{3,2,1,0:T(8,128)S(1)} %get-tuple-element.73), channel_id=1, source_target_pairs={{0,2},{1,3},{2,0},{3,1},{4,6},{5,7},{6,4},{7,5},{8,10},{9,11},{10,... | collective-permute-start | bytes 393224 | tf_op jit(solution)/shard_map/ppermute | solution.py:445
  79.3 2.0 %collective-permute-start.19 = (f32[16,2,32,128]{3,2,1,0:T(8,128)S(1)}, f32[16,2,32,128]{3,2,1,0:T(8,128)S(1)}, u32[]{:S(2)}, u32[]{:S(2)}) collective-permute-start(f32[16,2,32,128]{3,2,1,0:T(8,128)S(1)} %constant_dynamic-update-slice_fusion.9.front_ref), channel_id=1, source_target_pairs={{0,1},{1,0},{2,3},{3,2},{4,5},{5,4},{6,7},{7,6},{8,9},{9,8},{10,11... | collective-permute-start | bytes 1572872 | tf_op jit(solution)/shard_map/ppermute | solution.py:445

commit v7 on v6

--- a/solution.py
+++ b/solution.py
@@ -227,8 +227,8 @@
     return jnp.where(lane, rolled, -rolled)
 
 
-def chunks(cells, planes):
-    return [(p, at) for p in range(planes) for at in range(0, cells, STEP)]
+def chunks(cells, planes, step=STEP):
+    return [(p, at) for p in range(planes) for at in range(0, cells, step)]
 
 
 def spanwise_kernel(
@@ -346,14 +346,18 @@
     for p in range(planes):
         finish_modes(behind_ref, back_table_ref, inv_ref, lhs_ref, p)
     for p, at in chunks(cells, planes):
-        rows = pl.ds(at, STEP)
         spectral = synthesise(lhs_ref.at[p], at, STEP, synth_ref)
-        pre = spectral.reshape(STEP, channels, span) + local_ref[rows, p]
-        cumulative, density = normal_parts(pre)
-        act_ref[rows, p] = pre * cumulative
-        dpre = up_ref[rows, p] * (cumulative + pre * density)
-        dpre_ref[rows, p] = dpre
-        high, low = split(dpre.reshape(STEP * channels, span))
+        spectral = spectral.reshape(STEP, channels, span)
+        halves = []
+        for cell in range(STEP):
+            pre = spectral[cell] + local_ref[at + cell, p]
+            cumulative, density = normal_parts(pre)
+            act_ref[at + cell, p] = pre * cumulative
+            dpre = up_ref[at + cell, p] * (cumulative + pre * density)
+            dpre_ref[at + cell, p] = dpre
+            halves.append(split(dpre))
+        high = jnp.concatenate([half[0] for half in halves], axis=0)
+        low = jnp.concatenate([half[1] for half in halves], axis=0)
         analyse(high, low, table_ref, at, coef_ref.at[p])
     to_modes(coef_ref, down_ref, send_ref, 1)
 
@@ -428,13 +432,14 @@
 ):
     cells, planes, channels, span = local_ref.shape
     copies = []
-    for i, (p, at) in enumerate(chunks(cells, planes)):
+    for i, (p, at) in enumerate(chunks(cells, planes, STEP // 2)):
         if at == 0:
             finish_modes(behind_ref, back_table_ref, inv_ref, lhs_ref, p)
-        rows = pl.ds(at, STEP)
-        spectral = synthesise(lhs_ref.at[p], at, STEP, synth_ref)
-        out_scr[i] = spectral.reshape(STEP, channels, span) + local_ref[rows, p]
-        copies.append(pltpu.make_async_copy(out_scr.at[i], out_ref.at[rows, p], sems.at[i]))
+        rows = pl.ds(at, STEP // 2)
+        spectral = synthesise(lhs_ref.at[p], at, STEP // 2, synth_ref)
+        piece = out_scr.at[i // 2, pl.ds(i % 2 * (STEP // 2), STEP // 2)]
+        piece[...] = spectral.reshape(STEP // 2, channels, span) + local_ref[rows, p]
+        copies.append(pltpu.make_async_copy(piece, out_ref.at[rows, p], sems.at[i]))
         copies[-1].start()
     for copy in copies:
         copy.wait()

time: 85 us -> 84.9 us (level)
  no operation moved by 1% of the time
where the time goes in v7:
time: 84.9 us; the launch traced here: 84.8 us
  waiting for transfers between devices  29.3 us (35%)
  Pallas kernels  27.4 us (32%)
  starting transfers between devices  26.6 us (31%)
  between operations  1.04 us (1%)
    ppermute x20, waiting for transfers between devices, swap(): return lax.ppermute(values, 'stream', [(i, i ^ mask) for i in range(count)])  29.3 us
    ppermute x20, starting transfers between devices, swap(): return lax.ppermute(values, 'stream', [(i, i ^ mask) for i in range(count)])  26.6 us
    pallas_call x1, Pallas kernels, per_device(): pl.pallas_call(middle_kernel, in_specs=[here] * 8, out_specs=[here] * 4,...  7.28 us
    pallas_call x1, Pallas kernels, per_device(): pl.pallas_call(functools.partial(spanwise_kernel, (owned, total_modes, ce...  3.93 us
    pallas_call x1, Pallas kernels, per_device(): pl.pallas_call(input_grad_kernel, in_specs=[here] * 5, out_specs=apart, o...  3.26 us
    pallas_call x1, Pallas kernels, weight_grad(): pl.pallas_call(weight_grad_kernel, in_specs=[here] * 2, out_specs=here, o...  3.26 us
    pallas_call x1, Pallas kernels, local_forward(): pl.pallas_call(functools.partial(pointwise_kernel, True), in_specs=[here]...  2.46 us
    pallas_call x1, Pallas kernels, local_backward(): pl.pallas_call(lambda values, weight, out: pointwise_kernel(False, values...  2.15 us
  transfers between devices with their start and end apart: 20, of which 15 were waited for; matrix products, arithmetic and copies ran while one was open for 0% of the time, Pallas kernels for 12%

profile of v7, /device:TPU:0, one launch (start us, length us, event | category | flops | bytes accessed | tf_op | source)
XLA Modules:
  0.0 84.8 jit_solution(10068054509130675009)
XLA Ops:
  0.6 0.0 copy-start
  0.6 0.0 copy-start.6
  0.7 0.0 copy-start.7
  0.7 3.9 %spanwise.1 = (f32[16,2,32,128]{3,2,1,0:T(8,128)S(1)}, f32[2,4,256,128]{3,2,1,0:T(8,128)S(1)}, bf16[2,256,256]{2,1,0:T(8,128)(2,1)S(1)}, bf16[2,256,256]{2,1,0:T(8,128)(2,1)S(1)}) custom-call(f32[16,2,64,512]{3,2,1,0:T(8,128)} %bitcast.5, bf16[512,256]{1,0:T(8,128)(2,1)} %constant.8.clone.table_hbm), custom_call_target="tpu_custom_call" | custom-call | tf_op jit(solution)/shard_map/spanwise/pallas_call | solution.py:524
  4.6 0.5 collective-permute-start
  5.1 0.4 keep_part.2.refs_0_
  5.6 1.1 %collective-permute-done.refs_1_ = f32[16,2,32,128]{3,2,1,0:T(8,128)S(1)} collective-permute-done((f32[16,2,32,128]{3,2,1,0:T(8,128)S(1)}, f32[16,2,32,128]{3,2,1,0:T(8,128)S(1)}, u32[]{:S(2)}, u32[]{:S(2)}) %collective-permute-start) | collective-permute-done | bytes 524320 | tf_op jit(solution)/shard_map/ppermute | solution.py:450
  6.7 0.1 slice_add_fusion.3
  6.7 3.0 %collective-permute-start.3 = (f32[4,2,32,128]{3,2,1,0:T(8,128)S(1)}, f32[4,2,32,128]{3,2,1,0:T(8,128)S(1)}, u32[]{:S(2)}, u32[]{:S(2)}) collective-permute-start(f32[4,2,32,128]{3,2,1,0:T(8,128)S(1)} %get-tuple-element.70), channel_id=1, source_target_pairs={{0,4},{1,5},{2,6},{3,7},{4,0},{5,1},{6,2},{7,3},{8,12},{9,13},{10,... | collective-permute-start | bytes 393224 | tf_op jit(solution)/shard_map/ppermute | solution.py:450
  9.7 1.5 %collective-permute-start.2 = (f32[4,2,32,128]{3,2,1,0:T(8,128)S(1)}, f32[4,2,32,128]{3,2,1,0:T(8,128)S(1)}, u32[]{:S(2)}, u32[]{:S(2)}) collective-permute-start(f32[4,2,32,128]{3,2,1,0:T(8,128)S(1)} %get-tuple-element.71), channel_id=1, source_target_pairs={{0,2},{1,3},{2,0},{3,1},{4,6},{5,7},{6,4},{7,5},{8,10},{9,11},{10,... | collective-permute-start | bytes 393224 | tf_op jit(solution)/shard_map/ppermute | solution.py:450
  11.2 0.0 collective-permute-start.1
  11.3 0.0 copy-done
  11.3 0.0 copy-done.6
  11.3 2.5 %local_forward.1.local_ref = f32[16,2,64,512]{3,2,1,0:T(8,128)S(1)} custom-call(f32[16,2,64,512]{3,2,1,0:T(8,128)S(1)} %bitcast.6, f32[64,64]{1,0:T(8,128)S(1)} %copy-done.6, f32[1,64]{1,0:T(1,128)S(1)} %bitcast.8), custom_call_target="tpu_custom_call" | custom-call | tf_op jit(solution)/shard_map/local_forward/pallas_call | solution.py:555
  13.8 0.0 copy-start.2
  13.8 0.0 copy-start.4
  13.8 0.0 copy-start.5
  13.8 0.0 collective-permute-done.3.refs_4_
  13.8 4.0 %collective-permute-done.2.refs_3_ = f32[4,2,32,128]{3,2,1,0:T(8,128)S(1)} collective-permute-done((f32[4,2,32,128]{3,2,1,0:T(8,128)S(1)}, f32[4,2,32,128]{3,2,1,0:T(8,128)S(1)}, u32[]{:S(2)}, u32[]{:S(2)}) %collective-permute-start.2) | collective-permute-done | bytes 131104 | tf_op jit(solution)/shard_map/ppermute | solution.py:450
  17.8 0.0 collective-permute-done.1.refs_2_
  17.8 2.7 %collective-permute-start.4 = (f32[2,2,32,128]{3,2,1,0:T(8,128)S(1)}, f32[2,2,32,128]{3,2,1,0:T(8,128)S(1)}, u32[]{:S(2)}, u32[]{:S(2)}) collective-permute-start(f32[2,2,32,128]{3,2,1,0:T(8,128)S(1)} %slice_add_fusion.7), channel_id=1, source_target_pairs={{0,8},{1,9},{2,10},{3,11},{4,12},{5,13},{6,14},{7,15},{8,0},{9,1},... | collective-permute-start | bytes 196616 | tf_op jit(solution)/shard_map/ppermute | solution.py:450
  20.5 2.6 %collective-permute-done.4.refs_5_ = f32[2,2,32,128]{3,2,1,0:T(8,128)S(1)} collective-permute-done((f32[2,2,32,128]{3,2,1,0:T(8,128)S(1)}, f32[2,2,32,128]{3,2,1,0:T(8,128)S(1)}, u32[]{:S(2)}, u32[]{:S(2)}) %collective-permute-start.4) | collective-permute-done | bytes 65568 | tf_op jit(solution)/shard_map/ppermute | solution.py:450
  23.1 0.0 copy-done.1
  23.1 1.3 %mix.1 = (f32[2,2,32,128]{3,2,1,0:T(8,128)S(1)}, f32[2,2,32,128]{3,2,1,0:T(8,128)S(1)}) custom-call(f32[16,2,32,128]{3,2,1,0:T(8,128)S(1)} %keep_part.2.refs_0_, f32[16,2,32,128]{3,2,1,0:T(8,128)S(1)} %collective-permute-done.refs_1_, f32[4,2,32,128]{3,2,1,0:T(8,128)S(1)} %collective-permute-done.1.refs_2_, ...), custom_call_target="tpu_custom_call" | custom-call | tf_op jit(solution)/shard_map/mix/pallas_call | solution.py:565
  24.4 2.7 %collective-permute-start.5 = (f32[2,2,32,128]{3,2,1,0:T(8,128)S(1)}, f32[2,2,32,128]{3,2,1,0:T(8,128)S(1)}, u32[]{:S(2)}, u32[]{:S(2)}) collective-permute-start(f32[2,2,32,128]{3,2,1,0:T(8,128)S(1)} %get-tuple-element.44), channel_id=1, source_target_pairs={{0,8},{1,9},{2,10},{3,11},{4,12},{5,13},{6,14},{7,15},{8,0},{9,1},... | collective-permute-start | bytes 196616 | tf_op jit(solution)/shard_map/ppermute | solution.py:450
  27.1 2.5 %collective-permute-done.5 = f32[2,2,32,128]{3,2,1,0:T(8,128)S(1)} collective-permute-done((f32[2,2,32,128]{3,2,1,0:T(8,128)S(1)}, f32[2,2,32,128]{3,2,1,0:T(8,128)S(1)}, u32[]{:S(2)}, u32[]{:S(2)}) %collective-permute-start.5) | collective-permute-done | bytes 65568 | tf_op jit(solution)/shard_map/ppermute | solution.py:450
  29.6 2.3 %collective-permute-start.6 = (f32[4,2,32,128]{3,2,1,0:T(8,128)S(1)}, f32[4,2,32,128]{3,2,1,0:T(8,128)S(1)}, u32[]{:S(2)}, u32[]{:S(2)}) collective-permute-start(f32[4,2,32,128]{3,2,1,0:T(8,128)S(1)} %get-tuple-element.77), channel_id=1, source_target_pairs={{0,2},{1,3},{2,0},{3,1},{4,6},{5,7},{6,4},{7,5},{8,10},{9,11},{10,... | collective-permute-start | bytes 393224 | tf_op jit(solution)/shard_map/ppermute | solution.py:450
  31.9 0.0 collective-permute-start.7
  31.9 1.5 %collective-permute-start.8 = (f32[4,2,32,128]{3,2,1,0:T(8,128)S(1)}, f32[4,2,32,128]{3,2,1,0:T(8,128)S(1)}, u32[]{:S(2)}, u32[]{:S(2)}) collective-permute-start(f32[4,2,32,128]{3,2,1,0:T(8,128)S(1)} %get-tuple-element.77), channel_id=1, source_target_pairs={{0,6},{1,7},{2,4},{3,5},{4,2},{5,3},{6,0},{7,1},{8,14},{9,15},{10,... | collective-permute-start | bytes 393224 | tf_op jit(solution)/shard_map/ppermute | solution.py:450
  33.4 2.0 %collective-permute-done.6 = f32[4,2,32,128]{3,2,1,0:T(8,128)S(1)} collective-permute-done((f32[4,2,32,128]{3,2,1,0:T(8,128)S(1)}, f32[4,2,32,128]{3,2,1,0:T(8,128)S(1)}, u32[]{:S(2)}, u32[]{:S(2)}) %collective-permute-start.6) | collective-permute-done | bytes 131104 | tf_op jit(solution)/shard_map/ppermute | solution.py:450
  35.4 1.4 %collective-permute-done.7 = f32[4,2,32,128]{3,2,1,0:T(8,128)S(1)} collective-permute-done((f32[4,2,32,128]{3,2,1,0:T(8,128)S(1)}, f32[4,2,32,128]{3,2,1,0:T(8,128)S(1)}, u32[]{:S(2)}, u32[]{:S(2)}) %collective-permute-start.7) | collective-permute-done | bytes 131104 | tf_op jit(solution)/shard_map/ppermute | solution.py:450
  36.9 0.9 %collective-permute-done.8 = f32[4,2,32,128]{3,2,1,0:T(8,128)S(1)} collective-permute-done((f32[4,2,32,128]{3,2,1,0:T(8,128)S(1)}, f32[4,2,32,128]{3,2,1,0:T(8,128)S(1)}, u32[]{:S(2)}, u32[]{:S(2)}) %collective-permute-start.8) | collective-permute-done | bytes 131104 | tf_op jit(solution)/shard_map/ppermute | solution.py:450
  37.8 0.1 collective-permute-start.9
  37.9 0.7 front_part.2.inv_ref
  38.5 1.2 %collective-permute-done.9.behind_ref = f32[16,2,32,128]{3,2,1,0:T(8,128)S(1)} collective-permute-done((f32[16,2,32,128]{3,2,1,0:T(8,128)S(1)}, f32[16,2,32,128]{3,2,1,0:T(8,128)S(1)}, u32[]{:S(2)}, u32[]{:S(2)}) %collective-permute-start.9) | collective-permute-done | bytes 524320 | tf_op jit(solution)/shard_map/ppermute | solution.py:450
  39.8 7.3 %middle.1 = (f32[16,2,64,512]{3,2,1,0:T(8,128)}, f32[16,2,64,512]{3,2,1,0:T(8,128)S(1)}, f32[16,2,32,128]{3,2,1,0:T(8,128)S(1)}, f32[2,4,256,128]{3,2,1,0:T(8,128)S(1)}) custom-call(f32[16,2,64,512]{3,2,1,0:T(8,128)S(1)} %local_forward.1.local_ref, f32[16,2,64,512]{3,2,1,0:T(8,128)S(1)} %bitcast.7, f32[16,2,32,128]{3,2,1,0:T(8,128)S(1)} %collective-permute-done.9.behind_ref, ...), custom_call_target="tpu_custom_call" | custom-call | tf_op jit(solution)/shard_map/middle/pallas_call | solution.py:574
  47.0 0.1 collective-permute-start.10
  47.2 0.4 keep_part.3.refs_0_
  47.6 1.3 %collective-permute-done.10.refs_1_ = f32[16,2,32,128]{3,2,1,0:T(8,128)S(1)} collective-permute-done((f32[16,2,32,128]{3,2,1,0:T(8,128)S(1)}, f32[16,2,32,128]{3,2,1,0:T(8,128)S(1)}, u32[]{:S(2)}, u32[]{:S(2)}) %collective-permute-start.10) | collective-permute-done | bytes 524320 | tf_op jit(solution)/shard_map/ppermute | solution.py:450
  49.0 0.1 slice_add_fusion
  49.0 2.1 %collective-permute-start.13 = (f32[4,2,32,128]{3,2,1,0:T(8,128)S(1)}, f32[4,2,32,128]{3,2,1,0:T(8,128)S(1)}, u32[]{:S(2)}, u32[]{:S(2)}) collective-permute-start(f32[4,2,32,128]{3,2,1,0:T(8,128)S(1)} %get-tuple-element.67), channel_id=1, source_target_pairs={{0,4},{1,5},{2,6},{3,7},{4,0},{5,1},{6,2},{7,3},{8,12},{9,13},{10,... | collective-permute-start | bytes 393224 | tf_op jit(solution)/shard_map/ppermute | solution.py:450
  51.1 0.1 collective-permute-start.12
  51.2 1.5 %collective-permute-start.11 = (f32[4,2,32,128]{3,2,1,0:T(8,128)S(1)}, f32[4,2,32,128]{3,2,1,0:T(8,128)S(1)}, u32[]{:S(2)}, u32[]{:S(2)}) collective-permute-start(f32[4,2,32,128]{3,2,1,0:T(8,128)S(1)} %get-tuple-element.69), channel_id=1, source_target_pairs={{0,6},{1,7},{2,4},{3,5},{4,2},{5,3},{6,0},{7,1},{8,14},{9,15},{10,... | collective-permute-start | bytes 393224 | tf_op jit(solution)/shard_map/ppermute | solution.py:450
  52.6 2.1 %local_backward.1.local_ref = f32[16,2,64,512]{3,2,1,0:T(8,128)S(1)} custom-call(f32[16,2,64,512]{3,2,1,0:T(8,128)S(1)} %get-tuple-element.53.values, f32[64,64]{1,0:T(8,128)S(1)} %copy-done.6), custom_call_target="tpu_custom_call" | custom-call | tf_op jit(solution)/shard_map/local_backward/pallas_call | solution.py:585
  54.8 0.2 collective-permute-done.13.refs_4_
  55.0 4.2 %collective-permute-done.12.refs_3_ = f32[4,2,32,128]{3,2,1,0:T(8,128)S(1)} collective-permute-done((f32[4,2,32,128]{3,2,1,0:T(8,128)S(1)}, f32[4,2,32,128]{3,2,1,0:T(8,128)S(1)}, u32[]{:S(2)}, u32[]{:S(2)}) %collective-permute-start.12) | collective-permute-done | bytes 131104 | tf_op jit(solution)/shard_map/ppermute | solution.py:450
  59.2 0.0 collective-permute-done.11.refs_2_
  59.2 0.0 copy-start.3
  59.2 2.7 %collective-permute-start.14 = (f32[2,2,32,128]{3,2,1,0:T(8,128)S(1)}, f32[2,2,32,128]{3,2,1,0:T(8,128)S(1)}, u32[]{:S(2)}, u32[]{:S(2)}) collective-permute-start(f32[2,2,32,128]{3,2,1,0:T(8,128)S(1)} %slice_add_fusion.6), channel_id=1, source_target_pairs={{0,8},{1,9},{2,10},{3,11},{4,12},{5,13},{6,14},{7,15},{8,0},{9,1},... | collective-permute-start | bytes 196616 | tf_op jit(solution)/shard_map/ppermute | solution.py:450
  61.9 3.0 %collective-permute-done.14.refs_5_ = f32[2,2,32,128]{3,2,1,0:T(8,128)S(1)} collective-permute-done((f32[2,2,32,128]{3,2,1,0:T(8,128)S(1)}, f32[2,2,32,128]{3,2,1,0:T(8,128)S(1)}, u32[]{:S(2)}, u32[]{:S(2)}) %collective-permute-start.14) | collective-permute-done | bytes 65568 | tf_op jit(solution)/shard_map/ppermute | solution.py:450
  64.9 1.6 %adjoint.1 = (f32[2,2,32,128]{3,2,1,0:T(8,128)S(1)}, f32[2,2,32,128]{3,2,1,0:T(8,128)S(1)}) custom-call(f32[16,2,32,128]{3,2,1,0:T(8,128)S(1)} %keep_part.3.refs_0_, f32[16,2,32,128]{3,2,1,0:T(8,128)S(1)} %collective-permute-done.10.refs_1_, f32[4,2,32,128]{3,2,1,0:T(8,128)S(1)} %collective-permute-done.11.refs_2_, ...), custom_call_target="tpu_custom_call" | custom-call | tf_op jit(solution)/shard_map/adjoint/pallas_call | solution.py:595
  66.6 2.2 %collective-permute-start.15 = (f32[2,2,32,128]{3,2,1,0:T(8,128)S(1)}, f32[2,2,32,128]{3,2,1,0:T(8,128)S(1)}, u32[]{:S(2)}, u32[]{:S(2)}) collective-permute-start(f32[2,2,32,128]{3,2,1,0:T(8,128)S(1)} %get-tuple-element.58), channel_id=1, source_target_pairs={{0,8},{1,9},{2,10},{3,11},{4,12},{5,13},{6,14},{7,15},{8,0},{9,1},... | collective-permute-start | bytes 196616 | tf_op jit(solution)/shard_map/ppermute | solution.py:450
  68.8 3.2 %collective-permute-done.15 = f32[2,2,32,128]{3,2,1,0:T(8,128)S(1)} collective-permute-done((f32[2,2,32,128]{3,2,1,0:T(8,128)S(1)}, f32[2,2,32,128]{3,2,1,0:T(8,128)S(1)}, u32[]{:S(2)}, u32[]{:S(2)}) %collective-permute-start.15) | collective-permute-done | bytes 65568 | tf_op jit(solution)/shard_map/ppermute | solution.py:450
  72.0 1.2 %collective-permute-start.18 = (f32[4,2,32,128]{3,2,1,0:T(8,128)S(1)}, f32[4,2,32,128]{3,2,1,0:T(8,128)S(1)}, u32[]{:S(2)}, u32[]{:S(2)}) collective-permute-start(f32[4,2,32,128]{3,2,1,0:T(8,128)S(1)} %get-tuple-element.73), channel_id=1, source_target_pairs={{0,6},{1,7},{2,4},{3,5},{4,2},{5,3},{6,0},{7,1},{8,14},{9,15},{10,... | collective-permute-start | bytes 393224 | tf_op jit(solution)/shard_map/ppermute | solution.py:450
  73.1 0.1 collective-permute-start.17
  73.2 2.3 %collective-permute-start.16 = (f32[4,2,32,128]{3,2,1,0:T(8,128)S(1)}, f32[4,2,32,128]{3,2,1,0:T(8,128)S(1)}, u32[]{:S(2)}, u32[]{:S(2)}) collective-permute-start(f32[4,2,32,128]{3,2,1,0:T(8,128)S(1)} %get-tuple-element.73), channel_id=1, source_target_pairs={{0,2},{1,3},{2,0},{3,1},{4,6},{5,7},{6,4},{7,5},{8,10},{9,11},{10,... | collective-permute-start | bytes 393224 | tf_op jit(solution)/shard_map/ppermute | solution.py:450
  75.5 3.3 %weight_grad.1 = f32[2,32,64,128]{3,2,1,0:T(8,128)} custom-call(f32[2,2,32,128]{3,2,1,0:T(8,128)S(1)} %get-tuple-element.59.modes_ref, f32[2,2,32,128]{3,2,1,0:T(8,128)S(1)} %get-tuple-element.60.dmixed_ref), custom_call_target="tpu_custom_call" | custom-call | tf_op jit(solution)/shard_map/weight_grad/pallas_call | solution.py:605
  78.8 0.0 collective-permute-done.18
  78.8 0.0 collective-permute-done.17
  78.8 0.5 collective-permute-done.16
  79.3 0.1 collective-permute-start.19
  79.4 0.7 front_part.3.inv_ref
  80.1 1.2 %collective-permute-done.19.behind_ref = f32[16,2,32,128]{3,2,1,0:T(8,128)S(1)} collective-permute-done((f32[16,2,32,128]{3,2,1,0:T(8,128)S(1)}, f32[16,2,32,128]{3,2,1,0:T(8,128)S(1)}, u32[]{:S(2)}, u32[]{:S(2)}) %collective-permute-start.19) | collective-permute-done | bytes 524320 | tf_op jit(solution)/shard_map/ppermute | solution.py:450
  81.3 3.3 %input_grad.1 = f32[16,2,64,512]{3,2,1,0:T(8,128)} custom-call(f32[16,2,64,512]{3,2,1,0:T(8,128)S(1)} %local_backward.1.local_ref, f32[16,2,32,128]{3,2,1,0:T(8,128)S(1)} %collective-permute-done.19.behind_ref, f32[2,4,128,128]{3,2,1,0:T(8,128)S(1)} %front_part.3.inv_ref, bf16[256,512]{1,0:T(8,128)(2,1)S(1)} %copy-done.3, ...), custom_call_target="tpu_custom_call" | custom-call | tf_op jit(solution)/shard_map/input_grad/pallas_call | solution.py:615
  (18 shorter events, 0.2 us)
Async XLA Ops:
  0.6 10.6 %copy-start = (f32[16,2,512,64]{2,3,1,0:T(8,128)S(1)}, f32[16,2,512,64]{2,3,1,0:T(8,128)}, u32[]{:S(2)}) copy-start(f32[16,2,512,64]{2,3,1,0:T(8,128)} %param.9) | copy-start | bytes 12582916
  0.6 10.6 %copy-start.6 = (f32[64,64]{1,0:T(8,128)S(1)}, f32[64,64]{1,0:T(8,128)}, u32[]{:S(2)}) copy-start(f32[64,64]{1,0:T(8,128)} %weight.1) | copy-start | bytes 49156
  0.7 10.6 %copy-start.7 = (f32[64]{0:T(128)S(1)}, f32[64]{0:T(128)}, u32[]{:S(2)}) copy-start(f32[64]{0:T(128)} %param.12) | copy-start | bytes 772
  4.6 2.1 %collective-permute-start = (f32[16,2,32,128]{3,2,1,0:T(8,128)S(1)}, f32[16,2,32,128]{3,2,1,0:T(8,128)S(1)}, u32[]{:S(2)}, u32[]{:S(2)}) collective-permute-start(f32[16,2,32,128]{3,2,1,0:T(8,128)S(1)} %get-tuple-element.35), channel_id=1, source_target_pairs={{0,1},{1,0},{2,3},{3,2},{4,5},{5,4},{6,7},{7,6},{8,9},{9,8},{10,11... | collective-permute-start | bytes 1572872 | tf_op jit(solution)/shard_map/ppermute | solution.py:450
  6.7 7.1 %collective-permute-start.3 = (f32[4,2,32,128]{3,2,1,0:T(8,128)S(1)}, f32[4,2,32,128]{3,2,1,0:T(8,128)S(1)}, u32[]{:S(2)}, u32[]{:S(2)}) collective-permute-start(f32[4,2,32,128]{3,2,1,0:T(8,128)S(1)} %get-tuple-element.70), channel_id=1, source_target_pairs={{0,4},{1,5},{2,6},{3,7},{4,0},{5,1},{6,2},{7,3},{8,12},{9,13},{10,... | collective-permute-start | bytes 393224 | tf_op jit(solution)/shard_map/ppermute | solution.py:450
  9.7 8.1 %collective-permute-start.2 = (f32[4,2,32,128]{3,2,1,0:T(8,128)S(1)}, f32[4,2,32,128]{3,2,1,0:T(8,128)S(1)}, u32[]{:S(2)}, u32[]{:S(2)}) collective-permute-start(f32[4,2,32,128]{3,2,1,0:T(8,128)S(1)} %get-tuple-element.71), channel_id=1, source_target_pairs={{0,2},{1,3},{2,0},{3,1},{4,6},{5,7},{6,4},{7,5},{8,10},{9,11},{10,... | collective-permute-start | bytes 393224 | tf_op jit(solution)/shard_map/ppermute | solution.py:450
  11.2 6.6 %collective-permute-start.1 = (f32[4,2,32,128]{3,2,1,0:T(8,128)S(1)}, f32[4,2,32,128]{3,2,1,0:T(8,128)S(1)}, u32[]{:S(2)}, u32[]{:S(2)}) collective-permute-start(f32[4,2,32,128]{3,2,1,0:T(8,128)S(1)} %get-tuple-element.72), channel_id=1, source_target_pairs={{0,6},{1,7},{2,4},{3,5},{4,2},{5,3},{6,0},{7,1},{8,14},{9,15},{10,... | collective-permute-start | bytes 393224 | tf_op jit(solution)/shard_map/ppermute | solution.py:450
  11.3 11.8 %copy-start.1 = (f32[2,32,64,128]{3,2,1,0:T(8,128)S(1)}, f32[2,32,64,128]{3,2,1,0:T(8,128)}, u32[]{:S(2)}) copy-start(f32[2,32,64,128]{3,2,1,0:T(8,128)} %refs_6_.3) | copy-start | bytes 6291460
  13.8 26.0 %copy-start.2 = (f32[16,2,512,64]{2,3,1,0:T(8,128)S(1)}, f32[16,2,512,64]{2,3,1,0:T(8,128)}, u32[]{:S(2)}) copy-start(f32[16,2,512,64]{2,3,1,0:T(8,128)} %param.13) | copy-start | bytes 12582916
  13.8 26.0 %copy-start.4 = (bf16[256,512]{1,0:T(8,128)(2,1)S(1)}, bf16[256,512]{1,0:T(8,128)(2,1)}, u32[]{:S(2)}) copy-start(bf16[256,512]{1,0:T(8,128)(2,1)} %constant.11.clone.synth_ref) | copy-start | bytes 786436
  13.8 26.0 %copy-start.5 = (bf16[512,256]{1,0:T(8,128)(2,1)S(1)}, bf16[512,256]{1,0:T(8,128)(2,1)}, u32[]{:S(2)}) copy-start(bf16[512,256]{1,0:T(8,128)(2,1)} %constant.9.clone.table_ref) | copy-start | bytes 786436
  17.8 5.2 %collective-permute-start.4 = (f32[2,2,32,128]{3,2,1,0:T(8,128)S(1)}, f32[2,2,32,128]{3,2,1,0:T(8,128)S(1)}, u32[]{:S(2)}, u32[]{:S(2)}) collective-permute-start(f32[2,2,32,128]{3,2,1,0:T(8,128)S(1)} %slice_add_fusion.7), channel_id=1, source_target_pairs={{0,8},{1,9},{2,10},{3,11},{4,12},{5,13},{6,14},{7,15},{8,0},{9,1},... | collective-permute-start | bytes 196616 | tf_op jit(solution)/shard_map/ppermute | solution.py:450
  24.4 5.2 %collective-permute-start.5 = (f32[2,2,32,128]{3,2,1,0:T(8,128)S(1)}, f32[2,2,32,128]{3,2,1,0:T(8,128)S(1)}, u32[]{:S(2)}, u32[]{:S(2)}) collective-permute-start(f32[2,2,32,128]{3,2,1,0:T(8,128)S(1)} %get-tuple-element.44), channel_id=1, source_target_pairs={{0,8},{1,9},{2,10},{3,11},{4,12},{5,13},{6,14},{7,15},{8,0},{9,1},... | collective-permute-start | bytes 196616 | tf_op jit(solution)/shard_map/ppermute | solution.py:450
  29.6 5.8 %collective-permute-start.6 = (f32[4,2,32,128]{3,2,1,0:T(8,128)S(1)}, f32[4,2,32,128]{3,2,1,0:T(8,128)S(1)}, u32[]{:S(2)}, u32[]{:S(2)}) collective-permute-start(f32[4,2,32,128]{3,2,1,0:T(8,128)S(1)} %get-tuple-element.77), channel_id=1, source_target_pairs={{0,2},{1,3},{2,0},{3,1},{4,6},{5,7},{6,4},{7,5},{8,10},{9,11},{10,... | collective-permute-start | bytes 393224 | tf_op jit(solution)/shard_map/ppermute | solution.py:450
  31.9 5.0 %collective-permute-start.7 = (f32[4,2,32,128]{3,2,1,0:T(8,128)S(1)}, f32[4,2,32,128]{3,2,1,0:T(8,128)S(1)}, u32[]{:S(2)}, u32[]{:S(2)}) collective-permute-start(f32[4,2,32,128]{3,2,1,0:T(8,128)S(1)} %get-tuple-element.77), channel_id=1, source_target_pairs={{0,4},{1,5},{2,6},{3,7},{4,0},{5,1},{6,2},{7,3},{8,12},{9,13},{10,... | collective-permute-start | bytes 393224 | tf_op jit(solution)/shard_map/ppermute | solution.py:450
  31.9 5.9 %collective-permute-start.8 = (f32[4,2,32,128]{3,2,1,0:T(8,128)S(1)}, f32[4,2,32,128]{3,2,1,0:T(8,128)S(1)}, u32[]{:S(2)}, u32[]{:S(2)}) collective-permute-start(f32[4,2,32,128]{3,2,1,0:T(8,128)S(1)} %get-tuple-element.77), channel_id=1, source_target_pairs={{0,6},{1,7},{2,4},{3,5},{4,2},{5,3},{6,0},{7,1},{8,14},{9,15},{10,... | collective-permute-start | bytes 393224 | tf_op jit(solution)/shard_map/ppermute | solution.py:450
  37.8 2.0 %collective-permute-start.9 = (f32[16,2,32,128]{3,2,1,0:T(8,128)S(1)}, f32[16,2,32,128]{3,2,1,0:T(8,128)S(1)}, u32[]{:S(2)}, u32[]{:S(2)}) collective-permute-start(f32[16,2,32,128]{3,2,1,0:T(8,128)S(1)} %constant_dynamic-update-slice_fusion.2.front_ref), channel_id=1, source_target_pairs={{0,1},{1,0},{2,3},{3,2},{4,5},{5,4},{6,7},{7,6},{8,9},{9,8},{10,11... | collective-permute-start | bytes 1572872 | tf_op jit(solution)/shard_map/ppermute | solution.py:450
  47.0 1.9 %collective-permute-start.10 = (f32[16,2,32,128]{3,2,1,0:T(8,128)S(1)}, f32[16,2,32,128]{3,2,1,0:T(8,128)S(1)}, u32[]{:S(2)}, u32[]{:S(2)}) collective-permute-start(f32[16,2,32,128]{3,2,1,0:T(8,128)S(1)} %get-tuple-element.49), channel_id=1, source_target_pairs={{0,1},{1,0},{2,3},{3,2},{4,5},{5,4},{6,7},{7,6},{8,9},{9,8},{10,11... | collective-permute-start | bytes 1572872 | tf_op jit(solution)/shard_map/ppermute | solution.py:450
  49.0 6.0 %collective-permute-start.13 = (f32[4,2,32,128]{3,2,1,0:T(8,128)S(1)}, f32[4,2,32,128]{3,2,1,0:T(8,128)S(1)}, u32[]{:S(2)}, u32[]{:S(2)}) collective-permute-start(f32[4,2,32,128]{3,2,1,0:T(8,128)S(1)} %get-tuple-element.67), channel_id=1, source_target_pairs={{0,4},{1,5},{2,6},{3,7},{4,0},{5,1},{6,2},{7,3},{8,12},{9,13},{10,... | collective-permute-start | bytes 393224 | tf_op jit(solution)/shard_map/ppermute | solution.py:450
  51.1 8.1 %collective-permute-start.12 = (f32[4,2,32,128]{3,2,1,0:T(8,128)S(1)}, f32[4,2,32,128]{3,2,1,0:T(8,128)S(1)}, u32[]{:S(2)}, u32[]{:S(2)}) collective-permute-start(f32[4,2,32,128]{3,2,1,0:T(8,128)S(1)} %get-tuple-element.68), channel_id=1, source_target_pairs={{0,2},{1,3},{2,0},{3,1},{4,6},{5,7},{6,4},{7,5},{8,10},{9,11},{10,... | collective-permute-start | bytes 393224 | tf_op jit(solution)/shard_map/ppermute | solution.py:450
  51.2 8.0 %collective-permute-start.11 = (f32[4,2,32,128]{3,2,1,0:T(8,128)S(1)}, f32[4,2,32,128]{3,2,1,0:T(8,128)S(1)}, u32[]{:S(2)}, u32[]{:S(2)}) collective-permute-start(f32[4,2,32,128]{3,2,1,0:T(8,128)S(1)} %get-tuple-element.69), channel_id=1, source_target_pairs={{0,6},{1,7},{2,4},{3,5},{4,2},{5,3},{6,0},{7,1},{8,14},{9,15},{10,... | collective-permute-start | bytes 393224 | tf_op jit(solution)/shard_map/ppermute | solution.py:450
  59.2 22.1 %copy-start.3 = (bf16[256,512]{1,0:T(8,128)(2,1)S(1)}, bf16[256,512]{1,0:T(8,128)(2,1)}, u32[]{:S(2)}) copy-start(bf16[256,512]{1,0:T(8,128)(2,1)} %constant.10.clone.synth_ref) | copy-start | bytes 786436
  59.2 5.7 %collective-permute-start.14 = (f32[2,2,32,128]{3,2,1,0:T(8,128)S(1)}, f32[2,2,32,128]{3,2,1,0:T(8,128)S(1)}, u32[]{:S(2)}, u32[]{:S(2)}) collective-permute-start(f32[2,2,32,128]{3,2,1,0:T(8,128)S(1)} %slice_add_fusion.6), channel_id=1, source_target_pairs={{0,8},{1,9},{2,10},{3,11},{4,12},{5,13},{6,14},{7,15},{8,0},{9,1},... | collective-permute-start | bytes 196616 | tf_op jit(solution)/shard_map/ppermute | solution.py:450
  66.6 5.4 %collective-permute-start.15 = (f32[2,2,32,128]{3,2,1,0:T(8,128)S(1)}, f32[2,2,32,128]{3,2,1,0:T(8,128)S(1)}, u32[]{:S(2)}, u32[]{:S(2)}) collective-permute-start(f32[2,2,32,128]{3,2,1,0:T(8,128)S(1)} %get-tuple-element.58), channel_id=1, source_target_pairs={{0,8},{1,9},{2,10},{3,11},{4,12},{5,13},{6,14},{7,15},{8,0},{9,1},... | collective-permute-start | bytes 196616 | tf_op jit(solution)/shard_map/ppermute | solution.py:450
  72.0 6.8 %collective-permute-start.18 = (f32[4,2,32,128]{3,2,1,0:T(8,128)S(1)}, f32[4,2,32,128]{3,2,1,0:T(8,128)S(1)}, u32[]{:S(2)}, u32[]{:S(2)}) collective-permute-start(f32[4,2,32,128]{3,2,1,0:T(8,128)S(1)} %get-tuple-element.73), channel_id=1, source_target_pairs={{0,6},{1,7},{2,4},{3,5},{4,2},{5,3},{6,0},{7,1},{8,14},{9,15},{10,... | collective-permute-start | bytes 393224 | tf_op jit(solution)/shard_map/ppermute | solution.py:450
  73.1 5.7 %collective-permute-start.17 = (f32[4,2,32,128]{3,2,1,0:T(8,128)S(1)}, f32[4,2,32,128]{3,2,1,0:T(8,128)S(1)}, u32[]{:S(2)}, u32[]{:S(2)}) collective-permute-start(f32[4,2,32,128]{3,2,1,0:T(8,128)S(1)} %get-tuple-element.73), channel_id=1, source_target_pairs={{0,4},{1,5},{2,6},{3,7},{4,0},{5,1},{6,2},{7,3},{8,12},{9,13},{10,... | collective-permute-start | bytes 393224 | tf_op jit(solution)/shard_map/ppermute | solution.py:450
  73.2 6.1 %collective-permute-start.16 = (f32[4,2,32,128]{3,2,1,0:T(8,128)S(1)}, f32[4,2,32,128]{3,2,1,0:T(8,128)S(1)}, u32[]{:S(2)}, u32[]{:S(2)}) collective-permute-start(f32[4,2,32,128]{3,2,1,0:T(8,128)S(1)} %get-tuple-element.73), channel_id=1, source_target_pairs={{0,2},{1,3},{2,0},{3,1},{4,6},{5,7},{6,4},{7,5},{8,10},{9,11},{10,... | collective-permute-start | bytes 393224 | tf_op jit(solution)/shard_map/ppermute | solution.py:450
  79.3 2.0 %collective-permute-start.19 = (f32[16,2,32,128]{3,2,1,0:T(8,128)S(1)}, f32[16,2,32,128]{3,2,1,0:T(8,128)S(1)}, u32[]{:S(2)}, u32[]{:S(2)}) collective-permute-start(f32[16,2,32,128]{3,2,1,0:T(8,128)S(1)} %constant_dynamic-update-slice_fusion.9.front_ref), channel_id=1, source_target_pairs={{0,1},{1,0},{2,3},{3,2},{4,5},{5,4},{6,7},{7,6},{8,9},{9,8},{10,11... | collective-permute-start | bytes 1572872 | tf_op jit(solution)/shard_map/ppermute | solution.py:450
